TPU v7x, 256 devices: a whole 4x4x8 slice. The times are simulated.
256 devices in a mesh: chain: 8 (over x, core), col: 32 (over y, z).
Axes of the slice: x: 4, y: 4, z: 8, core: 2. Of those that a mesh axis runs over, the one named last changes fastest.
Arguments:
- rhs: float32 [8, 32, 64, 128], P('chain', 'col'), may hold values from -6 to 6
- inverse: float32 [8, 32, 128, 128], P('chain', 'col'), as said below
- factor: float32 [8, 32, 8, 128, 128], P('chain', 'col'), may hold values from -0.1875 to 0.1875
- pattern: int32 [8, 32, 8], P('chain', 'col'), may hold values from 0 to 31, as said below
Outputs:
- forward: float32 [8, 32, 64, 128], P('chain', 'col')
- solution: float32 [8, 32, 64, 128], P('chain', 'col')
Inputs may be any that keep to these rules, and one draw needn't show every extreme that they name: `pattern`: the 8 block rows of one supernode are distinct. `inverse`: each block is lower triangular, its diagonal between 0.5 and 1.5.
All inputs are finite; a program needn't handle non-finite values.
Results may differ from a plain program's by a relative error of at most 0.00012.
Values sent between devices are 32-bit elements; how exact they have to be, the bound alone decides.
No kernel may reach another device: no remote copies, remote signals or barrier semaphores. Data moves between devices by JAX's collectives and lax.ppermute only.
A program may use at most 64 MiB of HBM per device.

v0:
```python
import jax
import jax.numpy as jnp
from jax import lax
from jax.sharding import PartitionSpec as P


def shifted(value, axis, steps):
    count = lax.axis_size(axis)
    first, last = (max(0, -steps), min(count, count - steps))
    return lax.ppermute(value, axis, [(source, source + steps) for source in range(first, last)])


def body(rhs, inverse, factor, pattern):
    levels = lax.axis_size("chain")
    supers = lax.axis_size("col")
    highest = lax.Precision.HIGHEST
    loads_block = rhs[0, 0]
    diag_inverse = inverse[0, 0]
    blocks = factor[0, 0]
    targets = pattern[0, 0]
    loads, width = loads_block.shape
    place = lax.axis_index("chain")
    onehot = (targets[:, None] == jnp.arange(supers, dtype=jnp.int32)[None, :]).astype(jnp.float32)
    pieces = 1
    rows = loads // pieces
    steps = levels + pieces - 1

    def window(step, lag):
        index = step - lag
        live = (index >= 0) & (index < pieces)
        start = jnp.clip(index, 0, pieces - 1) * rows
        return (live, start)

    def forward_step(step, carry):
        solved, incoming = carry
        live, start = window(step, place)
        residue = loads_block - incoming
        fresh = jnp.dot(residue, diag_inverse.T, precision=highest)
        solved = jnp.where(live, fresh, solved)
        terms = jnp.einsum("rb,kab->kra", fresh, blocks, precision=highest)
        summed_rows = lax.psum_scatter(
            jnp.einsum("kc,kra->cra", onehot, terms, precision=highest),
            "col",
            scatter_dimension=0,
            tiled=True,
        )[0]
        arrived = shifted(summed_rows, "chain", 1)
        got, into = window(step + 1, place)
        got = got & (place > 0)
        incoming = jnp.where(got, arrived, incoming)
        return (solved, incoming)

    empty = jnp.zeros((loads, width), jnp.float32)
    solved, unused = lax.fori_loop(0, steps, forward_step, (empty, empty))

    def backward_step(step, carry):
        answer, outgoing = carry
        lag = levels - 1 - place
        live, start = window(step, lag)
        residue = solved - outgoing
        fresh = jnp.dot(residue, diag_inverse, precision=highest)
        answer = jnp.where(live, fresh, answer)
        arrived = shifted(fresh, "chain", -1)
        picked = jnp.einsum(
            "kc,cra->kra",
            onehot,
            lax.all_gather(arrived[None], "col", axis=0, tiled=True),
            precision=highest,
        )
        term = jnp.einsum("kra,kab->rb", picked, blocks, precision=highest)
        got, into = window(step, lag - 1)
        got = got & (place < levels - 1)
        outgoing = jnp.where(got, term, outgoing)
        return (answer, outgoing)

    answer, unused_rows = lax.fori_loop(0, steps, backward_step, (empty, empty))
    return (solved[None, None], answer[None, None])


def solution(mesh):
    in_specs = (
        P("chain", "col", None, None),
        P("chain", "col", None, None),
        P("chain", "col", None, None, None),
        P("chain", "col", None),
    )
    out_specs = (P("chain", "col", None, None), P("chain", "col", None, None))
    return jax.shard_map(body, mesh=mesh, in_specs=in_specs, out_specs=out_specs, check_vma=False)
```

profile of v0, /device:TPU:24, one launch (start us, length us, event | category | flops | bytes accessed | tf_op | source)
XLA Modules:
  0.0 2474.7 jit_solution(1854762112092310647)
XLA Ops:
  7.8 1791.0 %while.35 = (s32[]{:T(128)}, f32[64,128]{1,0:T(8,128)S(1)}, f32[64,128]{1,0:T(8,128)S(1)}, s32[]{:T(128)}, f32[64,128]{1,0:T(8,128)}, /*index=5*/f32[128,128]{1,...) while((s32[]{:T(128)}, f32[64,128]{1,0:T(8,128)S(1)}, ...), condition=%wide.region_2.3_spmd.clone, body=%wide.region_0.2_spmd.clone.sunk | while | flops 138461696 | bytes 7930159 | solution.py:54
  13.4 216.3 %reduce-scatter.2.cloned.1.call-done = f32[1,64,128]{2,1,0:T(8,128)} async-done(((f32[32,64,128]{2,1,0:T(8,128)}), f32[1,64,128]{2,1,0:T(8,128)}) %reduce-scatter.2.cloned.1.call-update) | async-done | bytes 32784 | tf_op jit(solution)/shard_map/while/body/eval_jaxpr/reduce_scatter | solution.py:41
  237.7 215.9 %reduce-scatter.2.cloned.1.call-done = f32[1,64,128]{2,1,0:T(8,128)} async-done(((f32[32,64,128]{2,1,0:T(8,128)}), f32[1,64,128]{2,1,0:T(8,128)}) %reduce-scatter.2.cloned.1.call-update) | async-done | bytes 32784 | tf_op jit(solution)/shard_map/while/body/eval_jaxpr/reduce_scatter | solution.py:41
  461.5 215.9 %reduce-scatter.2.cloned.1.call-done = f32[1,64,128]{2,1,0:T(8,128)} async-done(((f32[32,64,128]{2,1,0:T(8,128)}), f32[1,64,128]{2,1,0:T(8,128)}) %reduce-scatter.2.cloned.1.call-update) | async-done | bytes 32784 | tf_op jit(solution)/shard_map/while/body/eval_jaxpr/reduce_scatter | solution.py:41
  685.3 215.8 %reduce-scatter.2.cloned.1.call-done = f32[1,64,128]{2,1,0:T(8,128)} async-done(((f32[32,64,128]{2,1,0:T(8,128)}), f32[1,64,128]{2,1,0:T(8,128)}) %reduce-scatter.2.cloned.1.call-update) | async-done | bytes 32784 | tf_op jit(solution)/shard_map/while/body/eval_jaxpr/reduce_scatter | solution.py:41
  909.1 215.9 %reduce-scatter.2.cloned.1.call-done = f32[1,64,128]{2,1,0:T(8,128)} async-done(((f32[32,64,128]{2,1,0:T(8,128)}), f32[1,64,128]{2,1,0:T(8,128)}) %reduce-scatter.2.cloned.1.call-update) | async-done | bytes 32784 | tf_op jit(solution)/shard_map/while/body/eval_jaxpr/reduce_scatter | solution.py:41
  1132.9 216.0 %reduce-scatter.2.cloned.1.call-done = f32[1,64,128]{2,1,0:T(8,128)} async-done(((f32[32,64,128]{2,1,0:T(8,128)}), f32[1,64,128]{2,1,0:T(8,128)}) %reduce-scatter.2.cloned.1.call-update) | async-done | bytes 32784 | tf_op jit(solution)/shard_map/while/body/eval_jaxpr/reduce_scatter | solution.py:41
  1356.8 215.9 %reduce-scatter.2.cloned.1.call-done = f32[1,64,128]{2,1,0:T(8,128)} async-done(((f32[32,64,128]{2,1,0:T(8,128)}), f32[1,64,128]{2,1,0:T(8,128)}) %reduce-scatter.2.cloned.1.call-update) | async-done | bytes 32784 | tf_op jit(solution)/shard_map/while/body/eval_jaxpr/reduce_scatter | solution.py:41
  1580.7 215.9 %reduce-scatter.2.cloned.1.call-done = f32[1,64,128]{2,1,0:T(8,128)} async-done(((f32[32,64,128]{2,1,0:T(8,128)}), f32[1,64,128]{2,1,0:T(8,128)}) %reduce-scatter.2.cloned.1.call-update) | async-done | bytes 32784 | tf_op jit(solution)/shard_map/while/body/eval_jaxpr/reduce_scatter | solution.py:41
  1798.9 668.7 %while.36 = (s32[]{:T(128)}, f32[64,128]{1,0:T(8,128)S(1)}, f32[64,128]{1,0:T(8,128)S(1)}, s32[]{:T(128)}, f32[64,128]{1,0:T(8,128)S(1)}, /*index=5*/f32[128,128...) while((s32[]{:T(128)}, f32[64,128]{1,0:T(8,128)S(1)}, ...), condition=%wide.region_4.5_spmd.clone, body=%wide.region_3.4_spmd.clone.sunk | while | flops 138461696 | bytes 7995759 | solution.py:76
  1801.3 3.7 collective-permute-done.1
  1805.7 77.0 %all-gather.6.cloned.1.call-done = f32[2048,128]{1,0:T(8,128)} async-done(((f32[64,128]{1,0:T(8,128)}), f32[2048,128]{1,0:T(8,128)}) %all-gather.6.cloned.1.call-update) | async-done | bytes 1048592 | tf_op jit(solution)/shard_map/while/body/eval_jaxpr/all_gather | solution.py:67
  1882.6 2.5 fusion.59
  1888.0 1.8 collective-permute-done.1
  1890.5 75.3 %all-gather.6.cloned.1.call-done = f32[2048,128]{1,0:T(8,128)} async-done(((f32[64,128]{1,0:T(8,128)}), f32[2048,128]{1,0:T(8,128)}) %all-gather.6.cloned.1.call-update) | async-done | bytes 1048592 | tf_op jit(solution)/shard_map/while/body/eval_jaxpr/all_gather | solution.py:67
  1965.8 2.5 fusion.59
  1971.2 1.8 collective-permute-done.1
  1973.6 75.3 %all-gather.6.cloned.1.call-done = f32[2048,128]{1,0:T(8,128)} async-done(((f32[64,128]{1,0:T(8,128)}), f32[2048,128]{1,0:T(8,128)}) %all-gather.6.cloned.1.call-update) | async-done | bytes 1048592 | tf_op jit(solution)/shard_map/while/body/eval_jaxpr/all_gather | solution.py:67
  2048.9 2.5 fusion.59
  2054.3 1.8 collective-permute-done.1
  2056.8 75.3 %all-gather.6.cloned.1.call-done = f32[2048,128]{1,0:T(8,128)} async-done(((f32[64,128]{1,0:T(8,128)}), f32[2048,128]{1,0:T(8,128)}) %all-gather.6.cloned.1.call-update) | async-done | bytes 1048592 | tf_op jit(solution)/shard_map/while/body/eval_jaxpr/all_gather | solution.py:67
  2132.0 2.5 fusion.59
  2137.4 1.8 collective-permute-done.1
  2139.9 75.3 %all-gather.6.cloned.1.call-done = f32[2048,128]{1,0:T(8,128)} async-done(((f32[64,128]{1,0:T(8,128)}), f32[2048,128]{1,0:T(8,128)}) %all-gather.6.cloned.1.call-update) | async-done | bytes 1048592 | tf_op jit(solution)/shard_map/while/body/eval_jaxpr/all_gather | solution.py:67
  2215.2 2.5 fusion.59
  2220.6 1.8 collective-permute-done.1
  2223.0 75.3 %all-gather.6.cloned.1.call-done = f32[2048,128]{1,0:T(8,128)} async-done(((f32[64,128]{1,0:T(8,128)}), f32[2048,128]{1,0:T(8,128)}) %all-gather.6.cloned.1.call-update) | async-done | bytes 1048592 | tf_op jit(solution)/shard_map/while/body/eval_jaxpr/all_gather | solution.py:67
  2298.3 2.5 fusion.59
  2306.1 75.3 %all-gather.6.cloned.1.call-done = f32[2048,128]{1,0:T(8,128)} async-done(((f32[64,128]{1,0:T(8,128)}), f32[2048,128]{1,0:T(8,128)}) %all-gather.6.cloned.1.call-update) | async-done | bytes 1048592 | tf_op jit(solution)/shard_map/while/body/eval_jaxpr/all_gather | solution.py:67
  2381.4 2.5 fusion.59
  2389.3 75.3 %all-gather.6.cloned.1.call-done = f32[2048,128]{1,0:T(8,128)} async-done(((f32[64,128]{1,0:T(8,128)}), f32[2048,128]{1,0:T(8,128)}) %all-gather.6.cloned.1.call-update) | async-done | bytes 1048592 | tf_op jit(solution)/shard_map/while/body/eval_jaxpr/all_gather | solution.py:67
  2464.5 2.5 fusion.59
  (156 shorter events, 95.5 us)
Async XLA Ops:
  7.8 221.9 %reduce-scatter.2.cloned.1.call-start = ((), (), s32[]{:S(2)}) async-start(), calls=%async_computation.1 | async-start | bytes 1081344 | tf_op jit(solution)/shard_map/while/body/eval_jaxpr/reduce_scatter | solution.py:41
  229.7 2.3 collective-permute-start
  232.1 221.5 %reduce-scatter.2.cloned.1.call-start = ((), (), s32[]{:S(2)}) async-start(), calls=%async_computation.1 | async-start | bytes 1081344 | tf_op jit(solution)/shard_map/while/body/eval_jaxpr/reduce_scatter | solution.py:41
  453.6 2.3 collective-permute-start
  455.9 221.5 %reduce-scatter.2.cloned.1.call-start = ((), (), s32[]{:S(2)}) async-start(), calls=%async_computation.1 | async-start | bytes 1081344 | tf_op jit(solution)/shard_map/while/body/eval_jaxpr/reduce_scatter | solution.py:41
  677.4 2.3 collective-permute-start
  679.7 221.4 %reduce-scatter.2.cloned.1.call-start = ((), (), s32[]{:S(2)}) async-start(), calls=%async_computation.1 | async-start | bytes 1081344 | tf_op jit(solution)/shard_map/while/body/eval_jaxpr/reduce_scatter | solution.py:41
  901.2 2.3 collective-permute-start
  903.5 221.5 %reduce-scatter.2.cloned.1.call-start = ((), (), s32[]{:S(2)}) async-start(), calls=%async_computation.1 | async-start | bytes 1081344 | tf_op jit(solution)/shard_map/while/body/eval_jaxpr/reduce_scatter | solution.py:41
  1125.0 2.3 collective-permute-start
  1127.3 221.6 %reduce-scatter.2.cloned.1.call-start = ((), (), s32[]{:S(2)}) async-start(), calls=%async_computation.1 | async-start | bytes 1081344 | tf_op jit(solution)/shard_map/while/body/eval_jaxpr/reduce_scatter | solution.py:41
  1348.9 2.3 collective-permute-start
  1351.2 221.5 %reduce-scatter.2.cloned.1.call-start = ((), (), s32[]{:S(2)}) async-start(), calls=%async_computation.1 | async-start | bytes 1081344 | tf_op jit(solution)/shard_map/while/body/eval_jaxpr/reduce_scatter | solution.py:41
  1572.7 2.3 collective-permute-start
  1575.1 221.4 %reduce-scatter.2.cloned.1.call-start = ((), (), s32[]{:S(2)}) async-start(), calls=%async_computation.1 | async-start | bytes 1081344 | tf_op jit(solution)/shard_map/while/body/eval_jaxpr/reduce_scatter | solution.py:41
  1796.5 2.3 collective-permute-start
  1798.9 83.8 %all-gather.6.cloned.1.call-start = ((), (), s32[]{:S(2)}) async-start(), calls=%async_computation.2 | async-start | bytes 1081344 | tf_op jit(solution)/shard_map/while/body/eval_jaxpr/all_gather | solution.py:67
  1800.0 5.0 collective-permute-start.1
  1885.6 80.1 %all-gather.6.cloned.1.call-start = ((), (), s32[]{:S(2)}) async-start(), calls=%async_computation.2 | async-start | bytes 1081344 | tf_op jit(solution)/shard_map/while/body/eval_jaxpr/all_gather | solution.py:67
  1886.7 3.1 collective-permute-start.1
  1968.8 80.1 %all-gather.6.cloned.1.call-start = ((), (), s32[]{:S(2)}) async-start(), calls=%async_computation.2 | async-start | bytes 1081344 | tf_op jit(solution)/shard_map/while/body/eval_jaxpr/all_gather | solution.py:67
  1969.9 3.1 collective-permute-start.1
  2051.9 80.1 %all-gather.6.cloned.1.call-start = ((), (), s32[]{:S(2)}) async-start(), calls=%async_computation.2 | async-start | bytes 1081344 | tf_op jit(solution)/shard_map/while/body/eval_jaxpr/all_gather | solution.py:67
  2053.0 3.1 collective-permute-start.1
  2135.0 80.1 %all-gather.6.cloned.1.call-start = ((), (), s32[]{:S(2)}) async-start(), calls=%async_computation.2 | async-start | bytes 1081344 | tf_op jit(solution)/shard_map/while/body/eval_jaxpr/all_gather | solution.py:67
  2136.1 3.1 collective-permute-start.1
  2218.2 80.1 %all-gather.6.cloned.1.call-start = ((), (), s32[]{:S(2)}) async-start(), calls=%async_computation.2 | async-start | bytes 1081344 | tf_op jit(solution)/shard_map/while/body/eval_jaxpr/all_gather | solution.py:67
  2219.3 3.1 collective-permute-start.1
  2301.3 80.1 %all-gather.6.cloned.1.call-start = ((), (), s32[]{:S(2)}) async-start(), calls=%async_computation.2 | async-start | bytes 1081344 | tf_op jit(solution)/shard_map/while/body/eval_jaxpr/all_gather | solution.py:67
  2302.4 3.1 collective-permute-start.1
  2384.4 80.1 %all-gather.6.cloned.1.call-start = ((), (), s32[]{:S(2)}) async-start(), calls=%async_computation.2 | async-start | bytes 1081344 | tf_op jit(solution)/shard_map/while/body/eval_jaxpr/all_gather | solution.py:67
  2385.5 3.1 collective-permute-start.1
  (19 other events, 26.8 us)
Sparse Core Ops, SparseCore 0:
  13.5 216.1 reduce-scatter.1
  237.8 215.7 reduce-scatter.1
  461.6 215.7 reduce-scatter.1
  685.5 215.6 reduce-scatter.1
  909.2 215.7 reduce-scatter.1
  1133.0 215.8 reduce-scatter.1
  1357.0 215.7 reduce-scatter.1
  1580.8 215.6 reduce-scatter.1
  1805.8 76.8 all-gather.5
  1890.6 75.1 all-gather.5
  1973.7 75.1 all-gather.5
  2056.9 75.1 all-gather.5
  2140.0 75.1 all-gather.5
  2223.1 75.1 all-gather.5
  2306.2 75.1 all-gather.5
  2389.4 75.1 all-gather.5
where the time goes:
time: 2480 us; the launch traced here: 2470 us
  waiting for transfers between devices  2360 us (95%)
  matrix products  63.1 us (3%)
    reduce_scatter x8, waiting for transfers between devices, forward_step(): lax.psum_scatter(jnp.einsum('kc,kra->cra', onehot, terms, precision=highe...  1730 us
    all_gather x8, waiting for transfers between devices, backward_step(): lax.all_gather(arrived[None], 'col', axis=0, tiled=True)  604 us
  transfers between devices with their start and end apart: 32, of which 32 were waited for; matrix products, arithmetic and copies ran while one was open for 0% of the time, Pallas kernels for 0%

commit v1 on v0

v1 whole, which is shorter than its diff:
```python
import functools

import jax
import jax.numpy as jnp
from jax import lax
from jax.experimental import pallas as pl
from jax.experimental.pallas import tpu as pltpu
from jax.sharding import Mesh
from jax.sharding import PartitionSpec as P

LEVELS, YH, YL, Z = 8, 2, 2, 8
GROUP = YL * Z
SUPS = YH * GROUP
NB, BLOCK, LOADS = 8, 128, 64
ROWS = LOADS // GROUP
AXES = ("chain", "yh", "yl", "z")
MEMBERS = ("yl", "z")
F32, BF16 = jnp.float32, jnp.bfloat16
VMEM = pl.BlockSpec(memory_space=pltpu.VMEM)
SMEM = pl.BlockSpec(memory_space=pltpu.SMEM)
PARAMS = pltpu.CompilerParams(vmem_limit_bytes=20 << 20)
PIECE = jax.ShapeDtypeStruct((GROUP, ROWS, BLOCK), F32)


def split(value):
    high = value.astype(BF16)
    return high, (value - high.astype(F32)).astype(BF16)


def split_kernel(source, high, low):
    high[...], low[...] = split(source[...])


def split_weights(weights):
    shape = jax.ShapeDtypeStruct((GROUP, BLOCK, NB * BLOCK), BF16)
    spec = pl.BlockSpec((2, BLOCK, NB * BLOCK), lambda i: (i, 0, 0))
    return pl.pallas_call(
        split_kernel, grid=(GROUP // 2,), in_specs=[spec], out_specs=[spec, spec], out_shape=[shape, shape], name="split_weights"
    )(weights)


def forward_kernel(step, arrivals, table, residue, *refs):
    arrived, (high, low, residue_out, own, other, total) = refs[:arrivals], refs[arrivals:]
    current = residue[...]
    for piece in arrived:
        current = current - piece[...]
    residue_out[...] = current

    @pl.when(table[GROUP, 0] == step)
    def _():
        total[...] = jnp.zeros_like(total)
        for sup in range(GROUP):
            left = jnp.concatenate(split(residue_out[sup]), axis=0)
            terms = jnp.dot(left, high[sup], preferred_element_type=F32) + jnp.dot(left, low[sup], preferred_element_type=F32)
            for k in range(NB):
                total[table[sup, k]] += terms[:, k * BLOCK : (k + 1) * BLOCK]
        summed = total[:, :ROWS] + total[:, ROWS:]
        own[...] = summed[:GROUP]
        other[...] = summed[GROUP:]


def forward_step(step, table, residue, arrived, high, low):
    return pl.pallas_call(
        functools.partial(forward_kernel, step, len(arrived)),
        in_specs=[SMEM] + [VMEM] * (3 + len(arrived)),
        out_specs=[VMEM] * 3,
        out_shape=[PIECE] * 3,
        scratch_shapes=[pltpu.VMEM((SUPS, 2 * ROWS, BLOCK), F32)],
        compiler_params=PARAMS,
        name=f"forward_{step}",
    )(table, residue, *arrived, high, low)


def backward_kernel(level, table, before, base, own, other, high, low, answer, picked):
    @pl.when(table[GROUP, 0] != level)
    def _():
        answer[...] = before[...]

    @pl.when(table[GROUP, 0] == level)
    def _():
        for half, source in enumerate((own, other)):
            value = source[...]
            top = value.astype(BF16).astype(F32)
            picked[half * GROUP : (half + 1) * GROUP, :ROWS] = top
            picked[half * GROUP : (half + 1) * GROUP, ROWS:] = value - top
        contract = (((1,), (1,)), ((), ()))
        for sup in range(GROUP):
            left = jnp.concatenate([picked[table[sup, k]] for k in range(NB)], axis=1).astype(BF16)
            terms = lax.dot_general(left, high[sup], contract, preferred_element_type=F32)
            terms += lax.dot_general(left, low[sup], contract, preferred_element_type=F32)
            answer[sup] = base[sup] - (terms[:ROWS] + terms[ROWS:])


def backward_step(level, table, before, base, own, other, high, low):
    return pl.pallas_call(
        functools.partial(backward_kernel, level),
        in_specs=[SMEM] + [VMEM] * 6,
        out_specs=VMEM,
        out_shape=PIECE,
        scratch_shapes=[pltpu.VMEM((SUPS, 2 * ROWS, BLOCK), F32)],
        compiler_params=PARAMS,
        name=f"backward_{level}",
    )(table, before, base, own, other, high, low)


def diagonal_kernel(residue, inverse, solved, base):
    highest = lax.Precision.HIGHEST
    for sup in range(GROUP):
        value = lax.dot_general(residue[sup], inverse[sup], (((1,), (1,)), ((), ())), precision=highest, preferred_element_type=F32)
        solved[sup] = value
        base[sup] = jnp.dot(value, inverse[sup], precision=highest, preferred_element_type=F32)


def diagonal(residue, inverse):
    return pl.pallas_call(
        diagonal_kernel, in_specs=[VMEM] * 2, out_specs=[VMEM] * 2, out_shape=[PIECE] * 2, compiler_params=PARAMS, name="diagonal"
    )(residue, inverse)


def index(chain, yh, yl, z):
    return ((chain * YH + yh) * YL + yl) * Z + z


def hop(value, source, target, cross):
    pairs = [
        (index(source, yh, yl, z), index(target, yh ^ cross, yl ^ cross, z)) for yh in range(YH) for yl in range(YL) for z in range(Z)
    ]
    return lax.ppermute(value, AXES, pairs)


def body(rhs, inverse, factor, pattern):
    highest = lax.Precision.HIGHEST
    place, side = lax.axis_index("chain"), lax.axis_index("yh")
    member = lax.axis_index("yl") * Z + lax.axis_index("z")
    last = place == LEVELS - 1
    diag, blocks = inverse[0, 0], factor[0, 0]

    with jax.named_scope("prepare"):
        square = jnp.einsum("ca,cb->ab", diag, diag, precision=highest)
        folded = jnp.einsum("kac,cb->bka", blocks, diag, precision=highest)
        closing = jnp.zeros((BLOCK, NB, BLOCK), F32).at[:, 0, :].set(square)
        own_weights = jnp.where(last, closing, folded).reshape(BLOCK, NB * BLOCK)
        own_targets = jnp.where(last, side * GROUP + member, pattern[0, 0]) ^ (side * GROUP)

    with jax.named_scope("gather"):
        weights = lax.all_gather(own_weights, MEMBERS, axis=0)
        targets = lax.all_gather(own_targets, MEMBERS, axis=0)
        diags = lax.all_gather(diag, MEMBERS, axis=0)
        table = jnp.concatenate([targets, jnp.full((1, NB), place, jnp.int32)], axis=0)

    def swapped(value):
        return jnp.where(side == 1, jnp.roll(value, LOADS // 2, axis=0), value)

    with jax.named_scope("spread_rhs"):
        residue = lax.all_to_all(swapped(rhs[0, 0]).reshape(GROUP, ROWS, BLOCK), MEMBERS, 0, 0)

    high, low = split_weights(weights)

    arrived = ()
    for step in range(LEVELS):
        residue, own, other = forward_step(step, table, residue, arrived, high, low)
        if step < LEVELS - 1:
            arrived = (hop(own, step, step + 1, 0), hop(other, step, step + 1, 1))

    solved, base = diagonal(residue, diags)
    answer = own
    for level in range(LEVELS - 2, -1, -1):
        arrived = (hop(answer, level + 1, level, 0), hop(answer, level + 1, level, 1))
        answer = backward_step(level, table, answer, base, *arrived, high, low)

    with jax.named_scope("collect"):
        both = jnp.concatenate([solved, answer], axis=1)
        home = lax.all_to_all(both, MEMBERS, 0, 0)
        outputs = [swapped(home[:, i * ROWS : (i + 1) * ROWS].reshape(LOADS, BLOCK)) for i in range(2)]
    return outputs[0][None, None], outputs[1][None, None]


def solution(mesh):
    fine = Mesh(mesh.devices.reshape(LEVELS, YH, YL, Z), AXES)
    column = ("yh", "yl", "z")
    specs = [P("chain", column, *([None] * rank)) for rank in (2, 2, 3, 1)]
    return jax.shard_map(body, mesh=fine, in_specs=tuple(specs), out_specs=(specs[0], specs[0]), check_vma=False)
```

time: 2480 us -> 276 us (0.11)
  waiting for transfers between devices: 2360 us -> 137 us
  matrix products: 63.1 us -> 2.61 us
  blocking collectives: 0 us -> 44.5 us
  Pallas kernels: 0 us -> 31.2 us
    reduce_scatter x8 -> x0, waiting for transfers between devices: 1730 us -> none  [forward_step(): lax.psum_scatter(jnp.einsum('kc,kra->cra', onehot, terms, precision=highe...]
    all_gather x8 -> x2, waiting for transfers between devices: 604 us -> 91.8 us  [the longest x1 58.6 us: body(): weights = lax.all_gather(own_weights, MEMBERS, axis=0)]
    dot_general x48 -> x2, matrix products: 63.1 us -> 2.61 us  [the longest x1 1.4 us: body(): folded = jnp.einsum('kac,cb->bka', blocks, diag, precision=highest)]
    all_gather x0 -> x1, blocking collectives: none -> 32 us  [body(): targets = lax.all_gather(own_targets, MEMBERS, axis=0)]
    pallas_call x0 -> x17, Pallas kernels: none -> 31.2 us  [the longest x1 9.04 us: split_weights(): pl.pallas_call(split_kernel, grid=(GROUP // 2,), in_specs=[spec], out_spe...]
  transfers between devices with their start and end apart: 32 -> 31, of which waited for: 32 -> 5; matrix products, arithmetic and copies ran while one was open for 0% -> 1% of each run, Pallas kernels for 0% -> 9%
where the time goes in v1:
time: 276 us; the launch traced here: 275 us
  waiting for transfers between devices  137 us (50%)
  blocking collectives  44.5 us (16%)
  starting transfers between devices  31.3 us (11%)
  Pallas kernels  31.2 us (11%)
  between operations  14.6 us (5%)
  local copies, waits for them, and re-layouts  11.8 us (4%)
    all_gather x1, waiting for transfers between devices, body(): weights = lax.all_gather(own_weights, MEMBERS, axis=0)  58.6 us
    ppermute x28, waiting for transfers between devices, hop(): return lax.ppermute(value, AXES, pairs)  44.1 us
    all_gather x1, waiting for transfers between devices, body(): diags = lax.all_gather(diag, MEMBERS, axis=0)  33.2 us
    all_gather x1, blocking collectives, body(): targets = lax.all_gather(own_targets, MEMBERS, axis=0)  32 us
    ppermute x28, starting transfers between devices, hop(): return lax.ppermute(value, AXES, pairs)  21.3 us
    all_to_all x1, blocking collectives, body(): home = lax.all_to_all(both, MEMBERS, 0, 0)  12.5 us
    unnamed x12, local copies, waits for them, and re-layouts  9.99 us
    all_to_all x1, starting transfers between devices, body(): lax.all_to_all(swapped(rhs[0, 0]).reshape(GROUP, ROWS, BLOCK), MEMBERS, 0...  9.94 us
  transfers between devices with their start and end apart: 31, of which 5 were waited for; matrix products, arithmetic and copies ran while one was open for 1% of the time, Pallas kernels for 9%

profile of v1, /device:TPU:24, one launch (start us, length us, event | category | flops | bytes accessed | tf_op | source)
XLA Modules:
  0.0 274.6 jit_solution(4324625551362297808)
XLA Ops:
  7.2 1.2 convolution_bitcast_fusion
  8.5 1.4 convolution_select_fusion
  9.9 1.0 copy.14
  13.0 9.9 %all-to-all-start = ((f32[16,4,128]{2,1,0:T(4,128)}), f32[16,4,128]{2,1,0:T(4,128)S(1)}, u32[]{:S(2)}, u32[]{:S(2)}) async-start(f32[16,4,128]{2,1,0:T(4,128)} %bitcast.29), calls=%async_computation | async-start | bytes 65536 | tf_op jit(solution)/shard_map/spread_rhs/all_to_all | solution.py:155
  23.6 32.0 %all-gather = s32[16,1,8]{2,1,0:T(1,128)S(1)} all-gather(s32[1,1,8]{2,1,0:T(1,128)S(1)} %fusion.3), channel_id=2, replica_groups=mesh['chain'=8,'yh'=2,'yl'=2,'z'=8] {'yl','z'}, dimensions={0}, use_global_device_ids=true | all-gather | bytes 544 | tf_op jit(solution)/shard_map/gather/all_gather | solution.py:147
  55.7 58.6 %all-gather.5.cloned.1.call-done.source = f32[16,128,1024]{2,1,0:T(8,128)} async-done(((f32[1,128,1024]{2,1,0:T(8,128)}), f32[16,128,1024]{2,1,0:T(8,128)}) %all-gather.5.cloned.1.call-update) | async-done | bytes 8388624 | tf_op jit(solution)/shard_map/gather/all_gather | solution.py:146
  114.3 9.0 %split_weights.1 = (bf16[16,128,1024]{2,1,0:T(8,128)(2,1)}, bf16[16,128,1024]{2,1,0:T(8,128)(2,1)}) custom-call(f32[16,128,1024]{2,1,0:T(8,128)} %all-gather.5.cloned.1.call-done.source), custom_call_target="tpu_custom_call" | custom-call | tf_op jit(solution)/shard_map/split_weights/pallas_call | solution.py:37
  123.3 2.2 copy-done.1
  125.5 2.2 copy-done.3
  127.7 2.0 forward_0.1
  129.7 1.3 collective-permute-start
  131.0 1.5 collective-permute-start.1
  132.5 1.6 collective-permute-done.1.refs_1_
  136.2 0.8 forward_2.1
  138.3 0.8 forward_3.1
  146.8 1.5 forward_7.1
  149.7 33.2 %all-gather.7.cloned.1.call-done = f32[16,1,128,128]{3,2,1,0:T(8,128)} async-done(((f32[1,1,128,128]{3,2,1,0:T(8,128)}), f32[16,1,128,128]{3,2,1,0:T(8,128)}) %all-gather.7.cloned.1.call-update) | async-done | bytes 1048592 | tf_op jit(solution)/shard_map/gather/all_gather | solution.py:148
  182.9 1.2 copy-done.5
  184.1 6.6 %diagonal.1 = (f32[16,4,128]{2,1,0:T(4,128)S(1)}, f32[16,4,128]{2,1,0:T(4,128)S(1)}) custom-call(f32[16,4,128]{2,1,0:T(4,128)S(1)} %get-tuple-element.64.residue, f32[16,128,128]{2,1,0:T(8,128)S(1)} %bitcast.30), custom_call_target="tpu_custom_call" | custom-call | tf_op jit(solution)/shard_map/diagonal/pallas_call | solution.py:115
  190.7 2.2 copy-done.2
  192.9 2.2 copy-done.4
  197.2 0.8 backward_5.1.before
  199.4 0.8 backward_4.1.before
  201.5 0.8 backward_3.1.before
  203.6 0.8 backward_2.1.before
  205.7 0.8 backward_1.1.before
  206.5 1.3 collective-permute-start.26
  207.8 1.3 collective-permute-start.27
  209.1 39.3 %collective-permute-done.26.own = f32[16,4,128]{2,1,0:T(4,128)S(1)} collective-permute-done((f32[16,4,128]{2,1,0:T(4,128)S(1)}, f32[16,4,128]{2,1,0:T(4,128)S(1)}, u32[]{:S(2)}, u32[]{:S(2)}) %collective-permute-start.26) | collective-permute-done | bytes 32800 | tf_op jit(solution)/shard_map/ppermute | solution.py:128
  248.4 3.1 %collective-permute-done.27.other = f32[16,4,128]{2,1,0:T(4,128)S(1)} collective-permute-done((f32[16,4,128]{2,1,0:T(4,128)S(1)}, f32[16,4,128]{2,1,0:T(4,128)S(1)}, u32[]{:S(2)}, u32[]{:S(2)}) %collective-permute-start.27) | collective-permute-done | bytes 32800 | tf_op jit(solution)/shard_map/ppermute | solution.py:128
  251.5 3.0 %backward_0.1 = f32[16,4,128]{2,1,0:T(4,128)S(1)} custom-call(s32[17,8]{1,0:T(8,128)S(1)} %concatenate.42.table, f32[16,4,128]{2,1,0:T(4,128)S(1)} %backward_1.1.before, f32[16,4,128]{2,1,0:T(4,128)S(1)} %get-tuple-element.67.base, f32[16,4,128]{2,1,0:T(4,128)S(1)} %collective-permute-done.26.own, f32[16,4,128]{2,1,0:T(4,128)S(1)} %collective-permute-done.27.other, ...), custom_call_target="tpu_custom_call" | custom-call | tf_op jit(solution)/shard_map/backward_0/pallas_call | solution.py:95
  254.6 12.5 %all_to_all.10 = f32[16,8,128]{2,1,0:T(8,128)S(1)} all-to-all(f32[16,8,128]{2,1,0:T(8,128)S(1)} %pad_maximum_fusion), channel_id=1, replica_groups=mesh['chain'=8,'yh'=2,'yl'=2,'z'=8] {'yl','z'}, dimensions={0} | all-to-all | bytes 131072 | tf_op jit(solution)/shard_map/collect/all_to_all | solution.py:173
  (75 shorter events, 23.3 us)
Async XLA Ops:
  7.2 107.1 %all-gather.5.cloned.1.call-start = ((), (), s32[]{:S(2)}) async-start(), calls=%async_computation.2 | async-start | bytes 8912896 | tf_op jit(solution)/shard_map/gather/all_gather | solution.py:146
  10.9 172.0 %all-gather.7.cloned.1.call-start = ((), (), s32[]{:S(2)}) async-start(), calls=%async_computation.3 | async-start | bytes 1114112 | tf_op jit(solution)/shard_map/gather/all_gather | solution.py:148
  13.0 110.3 %all-to-all-start = ((f32[16,4,128]{2,1,0:T(4,128)}), f32[16,4,128]{2,1,0:T(4,128)S(1)}, u32[]{:S(2)}, u32[]{:S(2)}) async-start(f32[16,4,128]{2,1,0:T(4,128)} %bitcast.29), calls=%async_computation | async-start | bytes 65536 | tf_op jit(solution)/shard_map/spread_rhs/all_to_all | solution.py:155
  129.7 2.8 %collective-permute-start = (f32[16,4,128]{2,1,0:T(4,128)S(1)}, f32[16,4,128]{2,1,0:T(4,128)S(1)}, u32[]{:S(2)}, u32[]{:S(2)}) collective-permute-start(f32[16,4,128]{2,1,0:T(4,128)S(1)} %get-tuple-element.44), channel_id=1, source_target_pairs={{0,32},{1,33},{2,34},{3,35},{4,36},{5,37},{6,38},{7,39},{8,40},{9,... | collective-permute-start | bytes 98312 | tf_op jit(solution)/shard_map/ppermute | solution.py:128
  131.0 3.1 %collective-permute-start.1 = (f32[16,4,128]{2,1,0:T(4,128)S(1)}, f32[16,4,128]{2,1,0:T(4,128)S(1)}, u32[]{:S(2)}, u32[]{:S(2)}) collective-permute-start(f32[16,4,128]{2,1,0:T(4,128)S(1)} %get-tuple-element.45), channel_id=1, source_target_pairs={{0,56},{1,57},{2,58},{3,59},{4,60},{5,61},{6,62},{7,63},{8,48},{9,... | collective-permute-start | bytes 98312 | tf_op jit(solution)/shard_map/ppermute | solution.py:128
  134.9 1.3 collective-permute-start.2
  135.5 0.7 collective-permute-start.3
  137.0 1.3 collective-permute-start.4
  137.7 0.7 collective-permute-start.5
  139.1 1.3 collective-permute-start.6
  139.8 0.7 collective-permute-start.7
  141.2 1.3 collective-permute-start.8
  141.9 0.7 collective-permute-start.9
  143.4 1.3 collective-permute-start.10
  144.0 0.7 collective-permute-start.11
  145.5 1.3 collective-permute-start.12
  146.1 0.7 collective-permute-start.13
  148.4 42.4 %collective-permute-start.14 = (f32[16,4,128]{2,1,0:T(4,128)S(1)}, f32[16,4,128]{2,1,0:T(4,128)S(1)}, u32[]{:S(2)}, u32[]{:S(2)}) collective-permute-start(f32[16,4,128]{2,1,0:T(4,128)S(1)} %get-tuple-element.66.before), channel_id=1, source_target_pairs={{224,192},{225,193},{226,194},{227,195},{228,196},{229,197},{230,1... | collective-permute-start | bytes 98312 | tf_op jit(solution)/shard_map/ppermute | solution.py:128
  149.0 41.7 %collective-permute-start.15 = (f32[16,4,128]{2,1,0:T(4,128)S(1)}, f32[16,4,128]{2,1,0:T(4,128)S(1)}, u32[]{:S(2)}, u32[]{:S(2)}) collective-permute-start(f32[16,4,128]{2,1,0:T(4,128)S(1)} %get-tuple-element.66.before), channel_id=1, source_target_pairs={{224,216},{225,217},{226,218},{227,219},{228,220},{229,221},{230,2... | collective-permute-start | bytes 98312 | tf_op jit(solution)/shard_map/ppermute | solution.py:128
  190.7 2.2 copy-start.2
  195.9 1.3 collective-permute-start.16
  196.6 0.7 collective-permute-start.17
  198.0 1.3 collective-permute-start.18
  198.7 0.7 collective-permute-start.19
  200.1 1.3 collective-permute-start.20
  200.8 0.7 collective-permute-start.21
  202.3 1.3 collective-permute-start.22
  202.9 0.7 collective-permute-start.23
  204.4 1.3 collective-permute-start.24
  205.0 0.7 collective-permute-start.25
  206.5 41.9 %collective-permute-start.26 = (f32[16,4,128]{2,1,0:T(4,128)S(1)}, f32[16,4,128]{2,1,0:T(4,128)S(1)}, u32[]{:S(2)}, u32[]{:S(2)}) collective-permute-start(f32[16,4,128]{2,1,0:T(4,128)S(1)} %backward_1.1.before), channel_id=1, source_target_pairs={{32,0},{33,1},{34,2},{35,3},{36,4},{37,5},{38,6},{39,7},{40,8},{41... | collective-permute-start | bytes 98312 | tf_op jit(solution)/shard_map/ppermute | solution.py:128
  207.8 43.7 %collective-permute-start.27 = (f32[16,4,128]{2,1,0:T(4,128)S(1)}, f32[16,4,128]{2,1,0:T(4,128)S(1)}, u32[]{:S(2)}, u32[]{:S(2)}) collective-permute-start(f32[16,4,128]{2,1,0:T(4,128)S(1)} %backward_1.1.before), channel_id=1, source_target_pairs={{32,24},{33,25},{34,26},{35,27},{36,28},{37,29},{38,30},{39,31},{4... | collective-permute-start | bytes 98312 | tf_op jit(solution)/shard_map/ppermute | solution.py:128
  (5 other events, 9.1 us)
Sparse Core Ops, SparseCore 0:
  11.0 103.2 all-gather.4
  116.1 66.7 all-gather.6

commit v2 on v1

v2 whole, which is shorter than its diff:
```python
import functools

import jax
import jax.numpy as jnp
from jax import lax
from jax.experimental import pallas as pl
from jax.experimental.pallas import tpu as pltpu
from jax.sharding import Mesh
from jax.sharding import PartitionSpec as P

LEVELS, Y, Z = 8, 4, 8
CLASS = 2 * Z
NB, BLOCK, LOADS = 8, 128, 64
ROWS = LOADS // Z
WIDE = NB * BLOCK
AXES = ("chain", "y", "z")
F32, BF16, I32 = jnp.float32, jnp.bfloat16, jnp.int32
VMEM = pl.BlockSpec(memory_space=pltpu.VMEM)
SMEM = pl.BlockSpec(memory_space=pltpu.SMEM)
PARAMS = pltpu.CompilerParams(vmem_limit_bytes=24 << 20)
PIECE = jax.ShapeDtypeStruct((CLASS, ROWS, BLOCK), F32)
GROUPS = (
    ((0, 0), (0, 1), (-1, 0), (1, 0), (-1, 1), (1, 1)),
    ((-2, 0), (2, 0), (-2, 1), (2, 1)),
    ((-3, 0), (3, 0), (-3, 1), (3, 1), (-4, 0), (4, 1)),
)


def split(value):
    high = value.astype(BF16)
    return high, (value - high.astype(F32)).astype(BF16)


def split_kernel(count, *refs):
    high, low = refs[count:]
    for i, source in enumerate(refs[:count]):
        high[i], low[i] = split(source[...])


def split_weights(pieces):
    shape = jax.ShapeDtypeStruct((len(pieces), BLOCK, WIDE + BLOCK), BF16)
    return pl.pallas_call(
        functools.partial(split_kernel, len(pieces)),
        in_specs=[VMEM] * len(pieces),
        out_specs=[VMEM] * 2,
        out_shape=[shape] * 2,
        compiler_params=PARAMS,
        name="split_weights",
    )(*pieces)


def supernodes(table, weights):
    for group, (high, low) in zip(GROUPS, zip(weights[::2], weights[1::2])):
        for i, (away, slot) in enumerate(group):
            yield lax.rem(table[CLASS, 1] + (Z + away), Z) * 2 + slot, high.at[i], low.at[i]


def forward_kernel(step, arrivals, table, residue, *refs):
    arrived, weights, (residue_out, own, other, total) = refs[:arrivals], refs[arrivals:-4], refs[-4:]
    current = residue[...]
    for piece in arrived:
        current = current - piece[...]
    residue_out[...] = current

    @pl.when(table[CLASS, 0] == step)
    def _():
        total[...] = jnp.zeros_like(total)
        for sup, high, low in supernodes(table, weights):
            left = jnp.concatenate(split(residue_out[sup]), axis=0)
            terms = jnp.dot(left, high[:, :WIDE], preferred_element_type=F32) + jnp.dot(left, low[:, :WIDE], preferred_element_type=F32)
            summed = terms[:ROWS] + terms[ROWS:]
            for k in range(NB):
                total[table[sup, k]] += summed[:, k * BLOCK : (k + 1) * BLOCK]
        own[...] = total[:CLASS]
        other[...] = total[CLASS:]


def forward_step(step, table, residue, arrived, weights):
    return pl.pallas_call(
        functools.partial(forward_kernel, step, len(arrived)),
        in_specs=[SMEM] + [VMEM] * (1 + len(arrived) + len(weights)),
        out_specs=[VMEM] * 3,
        out_shape=[PIECE] * 3,
        scratch_shapes=[pltpu.VMEM((2 * CLASS, ROWS, BLOCK), F32)],
        compiler_params=PARAMS,
        name=f"forward_{step}",
    )(table, residue, *arrived, *weights)


CONTRACT_LAST = (((1,), (1,)), ((), ()))


def backward_kernel(level, table, before, base, own, other, *refs):
    weights, (answer, picked) = refs[:-2], refs[-2:]

    @pl.when(table[CLASS, 0] != level)
    def _():
        answer[...] = before[...]

    @pl.when(table[CLASS, 0] == level)
    def _():
        for half, source in enumerate((own, other)):
            value = source[...]
            top = value.astype(BF16).astype(F32)
            picked[half * CLASS : (half + 1) * CLASS, :ROWS] = top
            picked[half * CLASS : (half + 1) * CLASS, ROWS:] = value - top
        for sup, high, low in supernodes(table, weights):
            left = jnp.concatenate([picked[table[sup, k]] for k in range(NB)], axis=1).astype(BF16)
            terms = lax.dot_general(left, high[:, :WIDE], CONTRACT_LAST, preferred_element_type=F32)
            terms += lax.dot_general(left, low[:, :WIDE], CONTRACT_LAST, preferred_element_type=F32)
            answer[sup] = base[sup] - (terms[:ROWS] + terms[ROWS:])


def backward_step(level, table, before, base, own, other, weights):
    return pl.pallas_call(
        functools.partial(backward_kernel, level),
        in_specs=[SMEM] + [VMEM] * (4 + len(weights)),
        out_specs=VMEM,
        out_shape=PIECE,
        scratch_shapes=[pltpu.VMEM((2 * CLASS, 2 * ROWS, BLOCK), F32)],
        compiler_params=PARAMS,
        name=f"backward_{level}",
    )(table, before, base, own, other, *weights)


def diagonal_kernel(table, residue, *refs):
    weights, (solved, base) = refs[:-2], refs[-2:]
    for sup, high, low in supernodes(table, weights):
        left = jnp.concatenate(split(residue[sup]), axis=0)
        terms = jnp.dot(left, high[:, WIDE:], preferred_element_type=F32) + jnp.dot(left, low[:, WIDE:], preferred_element_type=F32)
        value = terms[:ROWS] + terms[ROWS:]
        solved[sup] = value
        left = jnp.concatenate(split(value), axis=0)
        terms = lax.dot_general(left, high[:, WIDE:], CONTRACT_LAST, preferred_element_type=F32)
        terms += lax.dot_general(left, low[:, WIDE:], CONTRACT_LAST, preferred_element_type=F32)
        base[sup] = terms[:ROWS] + terms[ROWS:]


def diagonal(table, residue, weights):
    return pl.pallas_call(
        diagonal_kernel,
        in_specs=[SMEM] + [VMEM] * (1 + len(weights)),
        out_specs=[VMEM] * 2,
        out_shape=[PIECE] * 2,
        compiler_params=PARAMS,
        name="diagonal",
    )(table, residue, *weights)


def index(chain, y, z):
    return (chain * Y + y) * Z + z


def seat(level, side):
    return side if level % 2 == 0 else Y - 1 - side


def hop(value, source, target, cross):
    pairs = [(index(source, seat(source, side), z), index(target, seat(target, side ^ cross), z)) for side in range(2) for z in range(Z)]
    return lax.ppermute(value, AXES, pairs)


def ring(value, steps):
    pairs = [
        (index(level, seat(level, side), z), index(level, seat(level, side), (z + steps) % Z))
        for level in range(LEVELS)
        for side in range(2)
        for z in range(Z)
    ]
    return lax.ppermute(value, AXES, pairs)


def seated(value, back=False):
    pairs = [
        (index(level, Y - 1 - seat(level, side), z), index(level, seat(level, side), z))
        for level in range(LEVELS)
        for side in range(2)
        for z in range(Z)
    ]
    return lax.ppermute(value, AXES, [pair[::-1] for pair in pairs] if back else pairs)


def body(rhs, inverse, factor, pattern):
    highest = lax.Precision.HIGHEST
    place, row, member = lax.axis_index("chain"), lax.axis_index("y"), lax.axis_index("z")
    last = place == LEVELS - 1
    odd = place % 2
    active = (row >= Y // 2) == (odd == 1)
    side = ((row == 1) | (row == 2)).astype(I32)
    diag, blocks = inverse[0, 0], factor[0, 0]

    with jax.named_scope("prepare"):
        square = jnp.einsum("ca,cb->ab", diag, diag, precision=highest)
        folded = jnp.einsum("kac,cb->bka", blocks, diag, precision=highest)
        closing = jnp.zeros((BLOCK, NB, BLOCK), F32).at[:, 0, :].set(square)
        weight_a = jnp.concatenate([jnp.where(last, closing, folded).reshape(BLOCK, WIDE), diag.T], axis=1)
        there, along = pattern[0, 0] // Z, pattern[0, 0] % Z
        there_side = ((there == 1) | (there == 2)).astype(I32)
        there_slot = ((there >= Y // 2) == (odd == 1)).astype(I32)
        targets = (there_side ^ side) * CLASS + along * 2 + there_slot
        targets = jnp.where(last, member * 2 + 1 - active.astype(I32), targets)
        small_a = jnp.concatenate([rhs[0, 0], jnp.zeros((8, BLOCK), F32).at[0, :NB].set(targets.astype(F32))], axis=0)

    with jax.named_scope("gather"):
        weight_b = seated(weight_a)
        small_b = seated(small_a)
        left_a, right_a = ring(weight_a, 1), ring(weight_a, -1)
        left_b, right_b = ring(weight_b, 1), ring(weight_b, -1)
        pieces = [[weight_a, weight_b, left_a, right_a, left_b, right_b]]
        for _ in range(2):
            left_a, right_a = ring(left_a, 1), ring(right_a, -1)
            left_b, right_b = ring(left_b, 1), ring(right_b, -1)
            pieces.append([left_a, right_a, left_b, right_b])
        pieces[2] += [ring(left_a, 1), ring(right_b, -1)]
        weights = [part for group in pieces for part in split_weights(group)]

    with jax.named_scope("spread_rhs"):
        marks = jnp.concatenate([small_a[LOADS : LOADS + 1], small_b[LOADS : LOADS + 1], jnp.zeros((6, BLOCK), F32)], axis=0)
        parts = [small_a[:LOADS].reshape(Z, ROWS, BLOCK), small_b[:LOADS].reshape(Z, ROWS, BLOCK), jnp.broadcast_to(marks, (Z, 8, BLOCK))]
        mine = lax.all_to_all(jnp.concatenate(parts, axis=1), "z", 0, 0)
        residue = mine[:, : 2 * ROWS].reshape(CLASS, ROWS, BLOCK)
        table = mine[:, 2 * ROWS : 2 * ROWS + 2, :NB].reshape(CLASS, NB).astype(I32)
        final = jnp.zeros((1, NB), I32).at[0, 0].set(jnp.where(active, place, -1)).at[0, 1].set(member)
        table = jnp.concatenate([table, final], axis=0)

    arrived = ()
    for step in range(LEVELS):
        residue, own, other = forward_step(step, table, residue, arrived, weights)
        if step < LEVELS - 1:
            arrived = (hop(other, step, step + 1, 1), hop(own, step, step + 1, 0))

    solved, base = diagonal(table, residue, weights)
    answer = own
    for level in range(LEVELS - 2, -1, -1):
        other = hop(answer, level + 1, level, 1)
        own = hop(answer, level + 1, level, 0)
        answer = backward_step(level, table, answer, base, own, other, weights)

    with jax.named_scope("collect"):
        both = jnp.concatenate([solved.reshape(Z, 2 * ROWS, BLOCK), answer.reshape(Z, 2 * ROWS, BLOCK)], axis=1)
        home = lax.all_to_all(both, "z", 0, 0).reshape(Z, 2, 2, ROWS, BLOCK).transpose(2, 1, 0, 3, 4).reshape(2, 2, LOADS, BLOCK)
        result = jnp.where(active, home[0], seated(home[1], back=True))
    return result[0][None, None], result[1][None, None]


def solution(mesh):
    fine = Mesh(mesh.devices.reshape(LEVELS, Y, Z), AXES)
    column = ("y", "z")
    specs = [P("chain", column, *([None] * rank)) for rank in (2, 2, 3, 1)]
    return jax.shard_map(body, mesh=fine, in_specs=tuple(specs), out_specs=(specs[0], specs[0]), check_vma=False)
```

time: 276 us -> 240 us (0.87)
  starting transfers between devices: 31.3 us -> 75.4 us
  blocking collectives: 44.5 us -> 12.6 us
  waiting for transfers between devices: 137 us -> 115 us
  between operations: 14.6 us -> 2.11 us
  Pallas kernels: 31.2 us -> 21.1 us
  local copies, waits for them, and re-layouts: 11.8 us -> 4.68 us
  other arithmetic: 1.96 us -> 4.74 us
    ppermute x0 -> x17, waiting for transfers between devices: none -> 112 us  [the longest x3 112 us: seated(): lax.ppermute(value, AXES, [pair[::-1] for pair in pairs] if back else pairs)]
    all_gather x2 -> x0, waiting for transfers between devices: 91.8 us -> none  [the longest x1 58.6 us: body(): weights = lax.all_gather(own_weights, MEMBERS, axis=0)]
    ppermute x0 -> x17, starting transfers between devices: none -> 52.8 us  [the longest x3 34.4 us: seated(): lax.ppermute(value, AXES, [pair[::-1] for pair in pairs] if back else pairs)]
    ppermute x28, waiting for transfers between devices: 44.1 us -> 0.1 us  [hop(): return lax.ppermute(value, AXES, pairs)]
    all_gather x1 -> x0, blocking collectives: 32 us -> none  [body(): targets = lax.all_gather(own_targets, MEMBERS, axis=0)]
    unnamed x12 -> x7, local copies, waits for them, and re-layouts: 9.99 us -> 0.95 us
    pallas_call x2 -> x4, Pallas kernels: 15.6 us -> 8.75 us  [the longest x3 6.39 us: split_weights(): pl.pallas_call(functools.partial(split_kernel, len(pieces)), in_specs=[VM...]
    all_to_all x1, starting transfers between devices: 9.94 us -> 3.99 us  [body(): mine = lax.all_to_all(jnp.concatenate(parts, axis=1), 'z', 0, 0)]
  transfers between devices with their start and end apart: 31 -> 46, of which waited for: 5 -> 4; matrix products, arithmetic and copies ran while one was open for 1% -> 3% of each run, Pallas kernels for 9% -> 3%
where the time goes in v2:
time: 240 us; the launch traced here: 239 us
  waiting for transfers between devices  115 us (48%)
  starting transfers between devices  75.4 us (31%)
  Pallas kernels  21.1 us (9%)
  blocking collectives  12.6 us (5%)
  other arithmetic  4.74 us (2%)
  local copies, waits for them, and re-layouts  4.68 us (2%)
  matrix products  2.62 us (1%)
    ppermute x3, waiting for transfers between devices, seated(): lax.ppermute(value, AXES, [pair[::-1] for pair in pairs] if back else pairs)  112 us
    ppermute x3, starting transfers between devices, seated(): lax.ppermute(value, AXES, [pair[::-1] for pair in pairs] if back else pairs)  34.4 us
    ppermute x28, starting transfers between devices, hop(): return lax.ppermute(value, AXES, pairs)  18.6 us
    ppermute x14, starting transfers between devices, ring(): return lax.ppermute(value, AXES, pairs)  18.4 us
    all_to_all x1, blocking collectives, body(): lax.all_to_all(both, 'z', 0, 0).reshape(Z, 2, 2, ROWS, BLOCK)  12.6 us
    pallas_call x8, Pallas kernels, forward_step(): pl.pallas_call(functools.partial(forward_kernel, step, len(arrived)), in_...  6.81 us
    pallas_call x3, Pallas kernels, split_weights(): pl.pallas_call(functools.partial(split_kernel, len(pieces)), in_specs=[VM...  6.39 us
    pallas_call x7, Pallas kernels, backward_step(): pl.pallas_call(functools.partial(backward_kernel, level), in_specs=[SMEM]...  5.5 us
  transfers between devices with their start and end apart: 46, of which 4 were waited for; matrix products, arithmetic and copies ran while one was open for 3% of the time, Pallas kernels for 3%

profile of v2, /device:TPU:24, one launch (start us, length us, event | category | flops | bytes accessed | tf_op | source)
XLA Modules:
  0.0 238.6 jit_solution(9547912593349929129)
XLA Ops:
  0.6 1.2 convolution_bitcast_fusion
  1.9 0.9 copy.31
  2.9 1.4 convolution_select_fusion
  4.5 3.9 %collective-permute-start.1 = (f32[128,1152]{1,0:T(8,128)S(1)}, f32[128,1152]{1,0:T(8,128)S(1)}, u32[]{:S(2)}, u32[]{:S(2)}) collective-permute-start(f32[128,1152]{1,0:T(8,128)S(1)} %pad_maximum_fusion.refs_0_), channel_id=1, source_target_pairs={{24,0},{25,1},{26,2},{27,3},{28,4},{29,5},{30,6},{31,7},{16,8},{17... | collective-permute-start | bytes 1769480 | tf_op jit(solution)/shard_map/gather/ppermute | solution.py:180
  9.1 6.6 %collective-permute-done.1.refs_1_ = f32[128,1152]{1,0:T(8,128)S(1)} collective-permute-done((f32[128,1152]{1,0:T(8,128)S(1)}, f32[128,1152]{1,0:T(8,128)S(1)}, u32[]{:S(2)}, u32[]{:S(2)}) %collective-permute-start.1) | collective-permute-done | bytes 589856 | tf_op jit(solution)/shard_map/gather/ppermute | solution.py:180
  17.2 1.5 collective-permute-start.6
  18.7 1.5 collective-permute-start.4
  20.2 1.5 collective-permute-start.9
  21.7 1.5 collective-permute-start.7
  23.2 1.5 collective-permute-start.10
  24.7 1.5 collective-permute-start.8
  26.2 1.5 collective-permute-start.13
  27.7 29.2 %collective-permute-start = (f32[72,128]{1,0:T(8,128)S(1)}, f32[72,128]{1,0:T(8,128)S(1)}, u32[]{:S(2)}, u32[]{:S(2)}) collective-permute-start(f32[72,128]{1,0:T(8,128)S(1)} %pad_maximum_fusion.3), channel_id=1, source_target_pairs={{24,0},{25,1},{26,2},{27,3},{28,4},{29,5},{30,6},{31,7},{16,8},{17... | collective-permute-start | bytes 110600 | tf_op jit(solution)/shard_map/gather/ppermute | solution.py:180
  56.9 1.5 collective-permute-done
  58.5 1.5 collective-permute-start.11
  60.0 1.5 collective-permute-start.14
  61.5 1.5 collective-permute-start.12
  63.0 1.5 collective-permute-start.15
  65.1 4.0 %all-to-all-start = ((f32[8,24,128]{2,1,0:T(8,128)}), f32[8,24,128]{2,1,0:T(8,128)}, u32[]{:S(2)}, u32[]{:S(2)}) async-start(f32[8,24,128]{2,1,0:T(8,128)} %pad_maximum_fusion.2), calls=%async_computation | async-start | bytes 196608 | tf_op jit(solution)/shard_map/spread_rhs/all_to_all | solution.py:220
  71.7 1.9 fusion.10
  73.6 1.3 scatter.16
  74.9 3.4 %all-to-all-done = f32[8,24,128]{2,1,0:T(8,128)} async-done(((f32[8,24,128]{2,1,0:T(8,128)}), f32[8,24,128]{2,1,0:T(8,128)}, u32[]{:S(2)}, u32[]{:S(2)}) %all-to-all-start) | async-done | bytes 98336 | tf_op jit(solution)/shard_map/spread_rhs/all_to_all | solution.py:220
  79.9 1.7 split_weights.3
  81.7 2.0 split_weights.4
  83.7 2.6 %split_weights.5 = (bf16[6,128,1152]{2,1,0:T(8,128)(2,1)S(1)}, bf16[6,128,1152]{2,1,0:T(8,128)(2,1)S(1)}) custom-call(f32[128,1152]{1,0:T(8,128)} %collective-permute-done.10.refs_0_, f32[128,1152]{1,0:T(8,128)} %collective-permute-done.11.refs_1_, f32[128,1152]{1,0:T(8,128)} %collective-permute-done.12.refs_2_, ...), custom_call_target="tpu_custom_call" | custom-call | tf_op jit(solution)/shard_map/gather/split_weights/pallas_call | solution.py:42
  97.0 0.9 forward_5.1
  101.4 1.4 forward_7.1
  104.1 2.4 diagonal.1
  117.2 1.0 backward_1.1.before
  120.3 12.6 %all_to_all.10 = f32[8,32,128]{2,1,0:T(8,128)S(1)} all-to-all(f32[8,32,128]{2,1,0:T(8,128)S(1)} %pad_maximum_fusion.1), channel_id=1, replica_groups=mesh['chain'=8,'y'=4,'z'=8] {'z'}, dimensions={0} | all-to-all | bytes 262144 | tf_op jit(solution)/shard_map/collect/all_to_all | solution.py:241
  132.9 1.3 collective-permute-start.44
  134.2 103.8 %collective-permute-done.44 = f32[2,64,128]{2,1,0:T(8,128)S(1)} collective-permute-done((f32[2,64,128]{2,1,0:T(8,128)S(1)}, f32[2,64,128]{2,1,0:T(8,128)S(1)}, u32[]{:S(2)}, u32[]{:S(2)}) %collective-permute-start.44) | collective-permute-done | bytes 65568 | tf_op jit(solution)/shard_map/collect/ppermute | solution.py:180
  (117 shorter events, 35.1 us)
Async XLA Ops:
  4.5 11.3 %collective-permute-start.1 = (f32[128,1152]{1,0:T(8,128)S(1)}, f32[128,1152]{1,0:T(8,128)S(1)}, u32[]{:S(2)}, u32[]{:S(2)}) collective-permute-start(f32[128,1152]{1,0:T(8,128)S(1)} %pad_maximum_fusion.refs_0_), channel_id=1, source_target_pairs={{24,0},{25,1},{26,2},{27,3},{28,4},{29,5},{30,6},{31,7},{16,8},{17... | collective-permute-start | bytes 1769480 | tf_op jit(solution)/shard_map/gather/ppermute | solution.py:180
  8.4 8.8 %collective-permute-start.2 = (f32[128,1152]{1,0:T(8,128)S(1)}, f32[128,1152]{1,0:T(8,128)S(1)}, u32[]{:S(2)}, u32[]{:S(2)}) collective-permute-start(f32[128,1152]{1,0:T(8,128)S(1)} %pad_maximum_fusion.refs_0_), channel_id=1, source_target_pairs={{0,1},{1,2},{2,3},{3,4},{4,5},{5,6},{6,7},{7,0},{8,9},{9,10},{10,1... | collective-permute-start | bytes 1769480 | tf_op jit(solution)/shard_map/gather/ppermute | solution.py:170
  15.8 4.4 %collective-permute-start.5 = (f32[128,1152]{1,0:T(8,128)S(1)}, f32[128,1152]{1,0:T(8,128)S(1)}, u32[]{:S(2)}, u32[]{:S(2)}) collective-permute-start(f32[128,1152]{1,0:T(8,128)S(1)} %collective-permute-done.1.refs_1_), channel_id=1, source_target_pairs={{0,7},{1,0},{2,1},{3,2},{4,3},{5,4},{6,5},{7,6},{8,15},{9,8},{10,9... | collective-permute-start | bytes 1769480 | tf_op jit(solution)/shard_map/gather/ppermute | solution.py:170
  16.5 5.2 %collective-permute-start.3 = (f32[128,1152]{1,0:T(8,128)S(1)}, f32[128,1152]{1,0:T(8,128)S(1)}, u32[]{:S(2)}, u32[]{:S(2)}) collective-permute-start(f32[128,1152]{1,0:T(8,128)S(1)} %pad_maximum_fusion.refs_0_), channel_id=1, source_target_pairs={{0,7},{1,0},{2,1},{3,2},{4,3},{5,4},{6,5},{7,6},{8,15},{9,8},{10,9... | collective-permute-start | bytes 1769480 | tf_op jit(solution)/shard_map/gather/ppermute | solution.py:170
  17.2 6.0 %collective-permute-start.6 = (f32[128,1152]{1,0:T(8,128)S(1)}, f32[128,1152]{1,0:T(8,128)}, u32[]{:S(2)}, u32[]{:S(2)}) collective-permute-start(f32[128,1152]{1,0:T(8,128)S(1)} %collective-permute-done.2.refs_2_), channel_id=1, source_target_pairs={{0,1},{1,2},{2,3},{3,4},{4,5},{5,6},{6,7},{7,0},{8,9},{9,10},{10,1... | collective-permute-start | bytes 1769480 | tf_op jit(solution)/shard_map/gather/ppermute | solution.py:170
  18.7 6.0 %collective-permute-start.4 = (f32[128,1152]{1,0:T(8,128)S(1)}, f32[128,1152]{1,0:T(8,128)}, u32[]{:S(2)}, u32[]{:S(2)}) collective-permute-start(f32[128,1152]{1,0:T(8,128)S(1)} %collective-permute-done.1.refs_1_), channel_id=1, source_target_pairs={{0,1},{1,2},{2,3},{3,4},{4,5},{5,6},{6,7},{7,0},{8,9},{9,10},{10,1... | collective-permute-start | bytes 1769480 | tf_op jit(solution)/shard_map/gather/ppermute | solution.py:170
  20.2 6.0 %collective-permute-start.9 = (f32[128,1152]{1,0:T(8,128)S(1)}, f32[128,1152]{1,0:T(8,128)}, u32[]{:S(2)}, u32[]{:S(2)}) collective-permute-start(f32[128,1152]{1,0:T(8,128)S(1)} %collective-permute-done.5.refs_5_), channel_id=1, source_target_pairs={{0,7},{1,0},{2,1},{3,2},{4,3},{5,4},{6,5},{7,6},{8,15},{9,8},{10,9... | collective-permute-start | bytes 1769480 | tf_op jit(solution)/shard_map/gather/ppermute | solution.py:170
  21.7 36.8 %collective-permute-start.7 = (f32[128,1152]{1,0:T(8,128)S(1)}, f32[128,1152]{1,0:T(8,128)}, u32[]{:S(2)}, u32[]{:S(2)}) collective-permute-start(f32[128,1152]{1,0:T(8,128)S(1)} %collective-permute-done.3.refs_3_), channel_id=1, source_target_pairs={{0,7},{1,0},{2,1},{3,2},{4,3},{5,4},{6,5},{7,6},{8,15},{9,8},{10,9... | collective-permute-start | bytes 1769480 | tf_op jit(solution)/shard_map/gather/ppermute | solution.py:170
  23.2 36.8 %collective-permute-start.10 = (f32[128,1152]{1,0:T(8,128)}, f32[128,1152]{1,0:T(8,128)}, u32[]{:S(2)}, u32[]{:S(2)}) collective-permute-start(f32[128,1152]{1,0:T(8,128)} %collective-permute-done.6.refs_0_), channel_id=1, source_target_pairs={{0,1},{1,2},{2,3},{3,4},{4,5},{5,6},{6,7},{7,0},{8,9},{9,10},{10,1... | collective-permute-start | bytes 1769480 | tf_op jit(solution)/shard_map/gather/ppermute | solution.py:170
  24.7 36.8 %collective-permute-start.8 = (f32[128,1152]{1,0:T(8,128)}, f32[128,1152]{1,0:T(8,128)}, u32[]{:S(2)}, u32[]{:S(2)}) collective-permute-start(f32[128,1152]{1,0:T(8,128)} %collective-permute-done.4.refs_4_), channel_id=1, source_target_pairs={{0,1},{1,2},{2,3},{3,4},{4,5},{5,6},{6,7},{7,0},{8,9},{9,10},{10,1... | collective-permute-start | bytes 1769480 | tf_op jit(solution)/shard_map/gather/ppermute | solution.py:170
  26.2 36.8 %collective-permute-start.13 = (f32[128,1152]{1,0:T(8,128)}, f32[128,1152]{1,0:T(8,128)}, u32[]{:S(2)}, u32[]{:S(2)}) collective-permute-start(f32[128,1152]{1,0:T(8,128)} %collective-permute-done.9.refs_3_), channel_id=1, source_target_pairs={{0,7},{1,0},{2,1},{3,2},{4,3},{5,4},{6,5},{7,6},{8,15},{9,8},{10,9... | collective-permute-start | bytes 1769480 | tf_op jit(solution)/shard_map/gather/ppermute | solution.py:170
  27.7 30.8 %collective-permute-start = (f32[72,128]{1,0:T(8,128)S(1)}, f32[72,128]{1,0:T(8,128)S(1)}, u32[]{:S(2)}, u32[]{:S(2)}) collective-permute-start(f32[72,128]{1,0:T(8,128)S(1)} %pad_maximum_fusion.3), channel_id=1, source_target_pairs={{24,0},{25,1},{26,2},{27,3},{28,4},{29,5},{30,6},{31,7},{16,8},{17... | collective-permute-start | bytes 110600 | tf_op jit(solution)/shard_map/gather/ppermute | solution.py:180
  58.5 25.2 %collective-permute-start.11 = (f32[128,1152]{1,0:T(8,128)}, f32[128,1152]{1,0:T(8,128)}, u32[]{:S(2)}, u32[]{:S(2)}) collective-permute-start(f32[128,1152]{1,0:T(8,128)} %collective-permute-done.7.refs_1_), channel_id=1, source_target_pairs={{0,7},{1,0},{2,1},{3,2},{4,3},{5,4},{6,5},{7,6},{8,15},{9,8},{10,9... | collective-permute-start | bytes 1769480 | tf_op jit(solution)/shard_map/gather/ppermute | solution.py:170
  60.0 23.7 %collective-permute-start.14 = (f32[128,1152]{1,0:T(8,128)}, f32[128,1152]{1,0:T(8,128)}, u32[]{:S(2)}, u32[]{:S(2)}) collective-permute-start(f32[128,1152]{1,0:T(8,128)} %collective-permute-done.10.refs_0_), channel_id=1, source_target_pairs={{0,1},{1,2},{2,3},{3,4},{4,5},{5,6},{6,7},{7,0},{8,9},{9,10},{10,1... | collective-permute-start | bytes 1769480 | tf_op jit(solution)/shard_map/gather/ppermute | solution.py:170
  61.5 22.2 %collective-permute-start.12 = (f32[128,1152]{1,0:T(8,128)}, f32[128,1152]{1,0:T(8,128)}, u32[]{:S(2)}, u32[]{:S(2)}) collective-permute-start(f32[128,1152]{1,0:T(8,128)} %collective-permute-done.8.refs_2_), channel_id=1, source_target_pairs={{0,1},{1,2},{2,3},{3,4},{4,5},{5,6},{6,7},{7,0},{8,9},{9,10},{10,1... | collective-permute-start | bytes 1769480 | tf_op jit(solution)/shard_map/gather/ppermute | solution.py:170
  63.0 20.7 %collective-permute-start.15 = (f32[128,1152]{1,0:T(8,128)}, f32[128,1152]{1,0:T(8,128)}, u32[]{:S(2)}, u32[]{:S(2)}) collective-permute-start(f32[128,1152]{1,0:T(8,128)} %collective-permute-done.13.refs_3_), channel_id=1, source_target_pairs={{0,7},{1,0},{2,1},{3,2},{4,3},{5,4},{6,5},{7,6},{8,15},{9,8},{10,9... | collective-permute-start | bytes 1769480 | tf_op jit(solution)/shard_map/gather/ppermute | solution.py:170
  65.1 13.2 %all-to-all-start = ((f32[8,24,128]{2,1,0:T(8,128)}), f32[8,24,128]{2,1,0:T(8,128)}, u32[]{:S(2)}, u32[]{:S(2)}) async-start(f32[8,24,128]{2,1,0:T(8,128)} %pad_maximum_fusion.2), calls=%async_computation | async-start | bytes 196608 | tf_op jit(solution)/shard_map/spread_rhs/all_to_all | solution.py:220
  87.1 1.3 collective-permute-start.16
  89.2 1.3 collective-permute-start.18
  91.4 1.3 collective-permute-start.20
  93.5 1.3 collective-permute-start.22
  95.6 1.3 collective-permute-start.24
  97.9 1.3 collective-permute-start.26
  100.1 1.3 collective-permute-start.28
  102.8 3.7 %collective-permute-start.31 = (f32[16,8,128]{2,1,0:T(8,128)S(1)}, f32[16,8,128]{2,1,0:T(8,128)S(1)}, u32[]{:S(2)}, u32[]{:S(2)}) collective-permute-start(f32[16,8,128]{2,1,0:T(8,128)S(1)} %get-tuple-element.110.before), channel_id=1, source_target_pairs={{248,200},{249,201},{250,202},{251,203},{252,204},{253,205},{254,2... | collective-permute-start | bytes 196616 | tf_op jit(solution)/shard_map/ppermute | solution.py:160
  103.5 3.1 %collective-permute-start.30 = (f32[16,8,128]{2,1,0:T(8,128)S(1)}, f32[16,8,128]{2,1,0:T(8,128)S(1)}, u32[]{:S(2)}, u32[]{:S(2)}) collective-permute-start(f32[16,8,128]{2,1,0:T(8,128)S(1)} %get-tuple-element.110.before), channel_id=1, source_target_pairs={{248,192},{249,193},{250,194},{251,195},{252,196},{253,197},{254,1... | collective-permute-start | bytes 196616 | tf_op jit(solution)/shard_map/ppermute | solution.py:160
  107.3 1.3 collective-permute-start.33
  109.4 1.3 collective-permute-start.35
  111.6 1.3 collective-permute-start.37
  113.7 1.3 collective-permute-start.39
  115.8 1.3 collective-permute-start.41
  132.9 105.1 %collective-permute-start.44 = (f32[2,64,128]{2,1,0:T(8,128)S(1)}, f32[2,64,128]{2,1,0:T(8,128)S(1)}, u32[]{:S(2)}, u32[]{:S(2)}) collective-permute-start(f32[2,64,128]{2,1,0:T(8,128)S(1)} %slice_bitcast_fusion), channel_id=1, source_target_pairs={{0,24},{1,25},{2,26},{3,27},{4,28},{5,29},{6,30},{7,31},{8,16},{9,... | collective-permute-start | bytes 196616 | tf_op jit(solution)/shard_map/collect/ppermute | solution.py:180
  (17 other events, 57.1 us)

commit v3 on v2

v3 whole, which is shorter than its diff:
```python
import functools

import jax
import jax.numpy as jnp
from jax import lax
from jax.experimental import pallas as pl
from jax.experimental.pallas import tpu as pltpu
from jax.sharding import Mesh
from jax.sharding import PartitionSpec as P

LEVELS, Y, Z = 8, 4, 8
CLASS = 2 * Z
NB, BLOCK, LOADS = 8, 128, 64
ROWS = LOADS // Z
WIDE = NB * BLOCK
AXES = ("chain", "y", "z")
TEAMS = [[y * Z + z for y in (side, Y - 1 - side) for z in range(Z)] for side in range(2)]
F32, BF16, I32 = jnp.float32, jnp.bfloat16, jnp.int32
VMEM = pl.BlockSpec(memory_space=pltpu.VMEM)
SMEM = pl.BlockSpec(memory_space=pltpu.SMEM)
ANY = pl.BlockSpec(memory_space=pl.ANY)
PARAMS = pltpu.CompilerParams(vmem_limit_bytes=24 << 20)
PIECE = jax.ShapeDtypeStruct((CLASS, ROWS, BLOCK), F32)
PACKED = jax.ShapeDtypeStruct((BLOCK, WIDE + BLOCK), F32)
GROUPS = (
    ((0, 0), (0, 1), (-1, 0), (1, 0), (-1, 1), (1, 1)),
    ((-2, 0), (2, 0), (-2, 1), (2, 1)),
    ((-3, 0), (3, 0), (-3, 1), (3, 1), (-4, 0), (4, 1)),
)
HIGHEST = lax.Precision.HIGHEST
CONTRACT_LAST = (((1,), (1,)), ((), ()))


def half_of(row):
    return (row >= Y // 2).astype(I32) if hasattr(row, "astype") else int(row >= Y // 2)


def side_of(row):
    return ((row == 1) | (row == 2)).astype(I32)


def prepare_kernel(pattern, rhs, inverse, factor, weights, spread):
    place, row, member = lax.axis_index("chain"), lax.axis_index("y"), lax.axis_index("z")
    last = place == LEVELS - 1
    side = side_of(row)
    turned = inverse[...].T
    weights[:, WIDE:] = turned

    @pl.when(last)
    def _():
        weights[:, :BLOCK] = jnp.dot(turned, inverse[...], precision=HIGHEST, preferred_element_type=F32)
        weights[:, BLOCK:WIDE] = jnp.zeros((BLOCK, WIDE - BLOCK), F32)

    @pl.when(jnp.logical_not(last))
    def _():
        for k in range(NB):
            weights[:, k * BLOCK : (k + 1) * BLOCK] = lax.dot_general(
                turned, factor[k], CONTRACT_LAST, precision=HIGHEST, preferred_element_type=F32
            )

    lane = lax.broadcasted_iota(I32, (8, BLOCK), 1)
    marks = jnp.zeros((8, BLOCK), F32)
    for k in range(NB):
        target = pattern[0, k]
        there = lax.div(target, Z)
        number = (side_of(there) ^ side) * CLASS + half_of(there) * Z + lax.rem(target, Z)
        number = jnp.where(last, half_of(row) * Z + member, number)
        marks = jnp.where(lane == k, number.astype(F32), marks)
    for i in range(CLASS):
        spread[i, :ROWS] = rhs[(i % Z) * ROWS : (i % Z + 1) * ROWS]
        spread[i, ROWS:] = marks


def prepare(pattern, rhs, inverse, factor):
    return pl.pallas_call(
        prepare_kernel,
        in_specs=[SMEM] + [VMEM] * 3,
        out_specs=[VMEM] * 2,
        out_shape=[PACKED, jax.ShapeDtypeStruct((CLASS, 2 * ROWS, BLOCK), F32)],
        compiler_params=PARAMS,
        name="prepare",
    )(pattern, rhs, inverse, factor)


def receive_kernel(mine, passed, residue, table, passed_out):
    residue[...] = mine[:, :ROWS]
    table[...] = mine[:, ROWS].astype(I32)


def receive(mine, passed):
    return pl.pallas_call(
        receive_kernel,
        in_specs=[VMEM, ANY],
        out_specs=[VMEM, VMEM, ANY],
        out_shape=[PIECE, jax.ShapeDtypeStruct((CLASS, BLOCK), I32), PACKED],
        input_output_aliases={1: 2},
        compiler_params=PARAMS,
        name="receive",
    )(mine, passed)


def split(value):
    high = value.astype(BF16)
    return high, (value - high.astype(F32)).astype(BF16)


def split_kernel(count, *refs):
    high, low = refs[count:]
    for i, source in enumerate(refs[:count]):
        high[i], low[i] = split(source[...])


def split_weights(pieces):
    shape = jax.ShapeDtypeStruct((len(pieces), BLOCK, WIDE + BLOCK), BF16)
    return pl.pallas_call(
        functools.partial(split_kernel, len(pieces)),
        in_specs=[VMEM] * len(pieces),
        out_specs=[VMEM] * 2,
        out_shape=[shape] * 2,
        compiler_params=PARAMS,
        cost_estimate=pl.CostEstimate(flops=0, transcendentals=0, bytes_accessed=8 * len(pieces) * BLOCK * (WIDE + BLOCK)),
        name="split_weights",
    )(*pieces)


def supernodes(weights):
    member, odd = lax.axis_index("z"), lax.rem(lax.axis_index("chain"), 2)
    for group, (high, low) in zip(GROUPS, zip(weights[::2], weights[1::2])):
        for i, (away, other) in enumerate(group):
            yield (odd ^ other) * Z + lax.rem(member + (Z + away), Z), high.at[i], low.at[i]


def active(level):
    return (lax.axis_index("chain") == level) & (half_of(lax.axis_index("y")) == level % 2)


def forward_kernel(step, arrivals, table, residue, *refs):
    arrived, weights, (residue_out, own, other, total) = refs[:arrivals], refs[arrivals:-4], refs[-4:]

    @pl.when(jnp.logical_not(active(step)))
    def _():
        residue_out[...] = residue[...]

    @pl.when(active(step))
    def _():
        current = residue[...]
        for piece in arrived:
            current = current - piece[...]
        residue_out[...] = current
        total[...] = jnp.zeros_like(total)
        for sup, high, low in supernodes(weights):
            left = jnp.concatenate(split(residue_out[sup]), axis=0)
            terms = jnp.dot(left, high[:, :WIDE], preferred_element_type=F32) + jnp.dot(left, low[:, :WIDE], preferred_element_type=F32)
            summed = terms[:ROWS] + terms[ROWS:]
            for k in range(NB):
                total[table[sup, k]] += summed[:, k * BLOCK : (k + 1) * BLOCK]
        own[...] = total[:CLASS]
        other[...] = total[CLASS:]


def forward_step(step, table, residue, arrived, weights):
    return pl.pallas_call(
        functools.partial(forward_kernel, step, len(arrived)),
        in_specs=[SMEM] + [VMEM] * (1 + len(arrived) + len(weights)),
        out_specs=[VMEM] * 3,
        out_shape=[PIECE] * 3,
        scratch_shapes=[pltpu.VMEM((2 * CLASS, ROWS, BLOCK), F32)],
        compiler_params=PARAMS,
        name=f"forward_{step}",
    )(table, residue, *arrived, *weights)


def backward_kernel(level, table, before, base, own, other, *refs):
    weights, (answer, picked) = refs[:-2], refs[-2:]

    @pl.when(jnp.logical_not(active(level)))
    def _():
        answer[...] = before[...]

    @pl.when(active(level))
    def _():
        for half, source in enumerate((own, other)):
            picked[half * CLASS : (half + 1) * CLASS] = jnp.concatenate(split(source[...]), axis=1)
        for sup, high, low in supernodes(weights):
            left = jnp.concatenate([picked[table[sup, k]] for k in range(NB)], axis=1)
            terms = lax.dot_general(left, high[:, :WIDE], CONTRACT_LAST, preferred_element_type=F32)
            terms += lax.dot_general(left, low[:, :WIDE], CONTRACT_LAST, preferred_element_type=F32)
            answer[sup] = base[sup] - (terms[:ROWS] + terms[ROWS:])


def backward_step(level, table, before, base, own, other, weights):
    return pl.pallas_call(
        functools.partial(backward_kernel, level),
        in_specs=[SMEM] + [VMEM] * (4 + len(weights)),
        out_specs=VMEM,
        out_shape=PIECE,
        scratch_shapes=[pltpu.VMEM((2 * CLASS, 2 * ROWS, BLOCK), BF16)],
        compiler_params=PARAMS,
        name=f"backward_{level}",
    )(table, before, base, own, other, *weights)


def diagonal_kernel(residue, *refs):
    weights, (solved, base) = refs[:-2], refs[-2:]
    for sup, high, low in supernodes(weights):
        left = jnp.concatenate(split(residue[sup]), axis=0)
        terms = jnp.dot(left, high[:, WIDE:], preferred_element_type=F32) + jnp.dot(left, low[:, WIDE:], preferred_element_type=F32)
        value = terms[:ROWS] + terms[ROWS:]
        solved[sup] = value
        left = jnp.concatenate(split(value), axis=0)
        terms = lax.dot_general(left, high[:, WIDE:], CONTRACT_LAST, preferred_element_type=F32)
        terms += lax.dot_general(left, low[:, WIDE:], CONTRACT_LAST, preferred_element_type=F32)
        base[sup] = terms[:ROWS] + terms[ROWS:]


def diagonal(residue, weights):
    return pl.pallas_call(
        diagonal_kernel,
        in_specs=[VMEM] * (1 + len(weights)),
        out_specs=[VMEM] * 2,
        out_shape=[PIECE] * 2,
        compiler_params=PARAMS,
        name="diagonal",
    )(residue, *weights)


def index(chain, y, z):
    return (chain * Y + y) * Z + z


def seat(level, side):
    return side if level % 2 == 0 else Y - 1 - side


def hop(value, source, target, cross):
    both = [(first, first + target - source) for first in (source % 4, source % 4 + 4)]
    pairs = [
        (index(first, seat(first, side), z), index(second, seat(second, side ^ cross), z))
        for first, second in both
        if 0 <= second < LEVELS
        for side in range(2)
        for z in range(Z)
    ]
    return lax.ppermute(value, AXES, pairs)


def ring(value, steps, native=False):
    pairs = []
    for level in range(LEVELS):
        for side in range(2):
            row = seat(level, side)
            source = Y - 1 - row if native else row
            pairs += [(index(level, source, z), index(level, row, (z + steps) % Z)) for z in range(Z)]
    return lax.ppermute(value, AXES, pairs)


def exchange(value):
    return lax.all_to_all(value, ("y", "z"), 0, 0, axis_index_groups=TEAMS)


def body(rhs, inverse, factor, pattern):
    weight_a, spread = prepare(pattern[0], rhs[0, 0], inverse[0, 0], factor[0, 0])

    with jax.named_scope("gather"):
        left_a, right_a = ring(weight_a, 1), ring(weight_a, -1)
        weight_b, left_b, right_b = ring(weight_a, 0, True), ring(weight_a, 1, True), ring(weight_a, -1, True)
        residue, table, left_a = receive(exchange(spread), left_a)
        table = table[:, :NB]
        pieces = [[weight_a, weight_b, left_a, right_a, left_b, right_b]]
        for _ in range(2):
            left_a, right_a = ring(left_a, 1), ring(right_a, -1)
            left_b, right_b = ring(left_b, 1), ring(right_b, -1)
            pieces.append([left_a, right_a, left_b, right_b])
        pieces[2] += [ring(left_a, 1), ring(right_b, -1)]
        weights = [part for group in pieces for part in split_weights(group)]

    arrived = ()
    for step in range(LEVELS):
        residue, own, other = forward_step(step, table, residue, arrived, weights)
        if step < LEVELS - 1:
            arrived = (hop(other, step, step + 1, 1), hop(own, step, step + 1, 0))

    solved, base = diagonal(residue, weights)
    answer = own
    for level in range(LEVELS - 2, -1, -1):
        other = hop(answer, level + 1, level, 1)
        own = hop(answer, level + 1, level, 0)
        answer = backward_step(level, table, answer, base, own, other, weights)

    with jax.named_scope("collect"):
        home = exchange(jnp.concatenate([solved, answer], axis=1))
        home = jnp.where(lax.axis_index("chain") % 2 == 1, home[Z:], home[:Z])
    return home[:, :ROWS].reshape(1, 1, LOADS, BLOCK), home[:, ROWS:].reshape(1, 1, LOADS, BLOCK)


def solution(mesh):
    fine = Mesh(mesh.devices.reshape(LEVELS, Y, Z), AXES)
    column = ("y", "z")
    specs = [P("chain", column, *([None] * rank)) for rank in (2, 2, 3, 1)]
    return jax.shard_map(body, mesh=fine, in_specs=tuple(specs), out_specs=(specs[0], specs[0]), check_vma=False)
```

time: 240 us -> 226 us (0.942)
  starting transfers between devices: 75.4 us -> 179 us
  waiting for transfers between devices: 115 us -> 20.7 us
  blocking collectives: 12.6 us -> 0 us
  other arithmetic: 4.74 us -> 0.67 us
  Pallas kernels: 21.1 us -> 17.2 us
  matrix products: 2.62 us -> 0 us
    all_to_all x1 -> x2, starting transfers between devices: 3.99 us -> 120 us  [exchange(): return lax.all_to_all(value, ('y', 'z'), 0, 0, axis_index_groups=TEAMS)]
    ppermute x3 -> x0, waiting for transfers between devices: 112 us -> none  [seated(): lax.ppermute(value, AXES, [pair[::-1] for pair in pairs] if back else pairs)]
    ppermute x3 -> x0, starting transfers between devices: 34.4 us -> none  [seated(): lax.ppermute(value, AXES, [pair[::-1] for pair in pairs] if back else pairs)]
    ppermute x14 -> x15, starting transfers between devices: 18.4 us -> 40.8 us  [ring(): return lax.ppermute(value, AXES, pairs)]
    all_to_all x1 -> x0, blocking collectives: 12.6 us -> none  [body(): lax.all_to_all(both, 'z', 0, 0).reshape(Z, 2, 2, ROWS, BLOCK)]
    ppermute x14 -> x15, waiting for transfers between devices: 0.04 us -> 10.9 us  [ring(): return lax.ppermute(value, AXES, pairs)]
    all_to_all x1 -> x2, waiting for transfers between devices: 3.4 us -> 9.68 us  [exchange(): return lax.all_to_all(value, ('y', 'z'), 0, 0, axis_index_groups=TEAMS)]
    pallas_call x3, Pallas kernels: 6.39 us -> 1.78 us  [split_weights(): pl.pallas_call(functools.partial(split_kernel, len(pieces)), in_specs=[VM...]
  transfers between devices with their start and end apart: 46 -> 45, of which waited for: 4 -> 4; matrix products, arithmetic and copies ran while one was open for 3% -> 0% of each run, Pallas kernels for 3% -> 1%
where the time goes in v3:
time: 226 us; the launch traced here: 223 us
  starting transfers between devices  179 us (79%)
  waiting for transfers between devices  20.7 us (9%)
  Pallas kernels  17.2 us (8%)
  local copies, waits for them, and re-layouts  3.92 us (2%)
    all_to_all x2, starting transfers between devices, exchange(): return lax.all_to_all(value, ('y', 'z'), 0, 0, axis_index_groups=TEAMS)  120 us
    ppermute x15, starting transfers between devices, ring(): return lax.ppermute(value, AXES, pairs)  40.8 us
    ppermute x28, starting transfers between devices, hop(): return lax.ppermute(value, AXES, pairs)  18.6 us
    ppermute x15, waiting for transfers between devices, ring(): return lax.ppermute(value, AXES, pairs)  10.9 us
    all_to_all x2, waiting for transfers between devices, exchange(): return lax.all_to_all(value, ('y', 'z'), 0, 0, axis_index_groups=TEAMS)  9.68 us
    pallas_call x8, Pallas kernels, forward_step(): pl.pallas_call(functools.partial(forward_kernel, step, len(arrived)), in_...  6.38 us
    pallas_call x7, Pallas kernels, backward_step(): pl.pallas_call(functools.partial(backward_kernel, level), in_specs=[SMEM]...  4.89 us
  transfers between devices with their start and end apart: 45, of which 4 were waited for; matrix products, arithmetic and copies ran while one was open for 0% of the time, Pallas kernels for 1%

profile of v3, /device:TPU:24, one launch (start us, length us, event | category | flops | bytes accessed | tf_op | source)
XLA Modules:
  0.0 223.5 jit_solution(1939818880167632941)
XLA Ops:
  0.6 1.0 copy-done
  1.7 0.8 copy-done.1
  2.5 0.8 copy-done.2
  3.9 2.5 %prepare.1 = (f32[128,1152]{1,0:T(8,128)S(1)}, f32[16,16,128]{2,1,0:T(8,128)}) custom-call(s32[1,8]{1,0:T(1,128)S(1)} %bitcast.27, f32[64,128]{1,0:T(8,128)S(1)} %bitcast.26, f32[128,128]{1,0:T(8,128)S(1)} %bitcast.25, f32[8,128,128]{2,1,0:T(8,128)S(1)} %bitcast.24), custom_call_target="tpu_custom_call" | custom-call | tf_op jit(solution)/shard_map/prepare/pallas_call | solution.py:75
  7.2 8.7 %collective-permute-start.4 = (f32[128,1152]{1,0:T(8,128)S(1)}, f32[128,1152]{1,0:T(8,128)S(1)}, u32[]{:S(2)}, u32[]{:S(2)}) collective-permute-start(f32[128,1152]{1,0:T(8,128)S(1)} %get-tuple-element.39.refs_0_), channel_id=1, source_target_pairs={{24,7},{25,0},{26,1},{27,2},{28,3},{29,4},{30,5},{31,6},{16,15},{1... | collective-permute-start | bytes 1769480 | tf_op jit(solution)/shard_map/gather/ppermute | solution.py:254
  15.9 8.5 %all-to-all-start = ((f32[16,16,128]{2,1,0:T(8,128)}), f32[16,16,128]{2,1,0:T(8,128)S(1)}, u32[]{:S(2)}, u32[]{:S(2)}) async-start(f32[16,16,128]{2,1,0:T(8,128)} %get-tuple-element.38), calls=%async_computation | async-start | bytes 262144 | tf_op jit(solution)/shard_map/gather/all_to_all | solution.py:258
  25.1 4.7 %collective-permute-start.3 = (f32[128,1152]{1,0:T(8,128)S(1)}, f32[128,1152]{1,0:T(8,128)S(1)}, u32[]{:S(2)}, u32[]{:S(2)}) collective-permute-start(f32[128,1152]{1,0:T(8,128)S(1)} %get-tuple-element.39.refs_0_), channel_id=1, source_target_pairs={{24,1},{25,2},{26,3},{27,4},{28,5},{29,6},{30,7},{31,0},{16,9},{17... | collective-permute-start | bytes 1769480 | tf_op jit(solution)/shard_map/gather/ppermute | solution.py:254
  29.8 2.1 all-to-all-done.mine
  32.0 0.7 collective-permute-start.5
  32.7 0.7 collective-permute-start.8
  33.4 0.7 collective-permute-start.6
  34.1 6.4 %collective-permute-done.3.refs_4_ = f32[128,1152]{1,0:T(8,128)S(1)} collective-permute-done((f32[128,1152]{1,0:T(8,128)S(1)}, f32[128,1152]{1,0:T(8,128)S(1)}, u32[]{:S(2)}, u32[]{:S(2)}) %collective-permute-start.3) | collective-permute-done | bytes 589856 | tf_op jit(solution)/shard_map/gather/ppermute | solution.py:254
  41.2 0.7 collective-permute-start.9
  42.0 0.7 collective-permute-start.12
  42.7 19.0 %collective-permute-start.1 = (f32[128,1152]{1,0:T(8,128)S(1)}, f32[128,1152]{1,0:T(8,128)S(1)}, u32[]{:S(2)}, u32[]{:S(2)}) collective-permute-start(f32[128,1152]{1,0:T(8,128)S(1)} %get-tuple-element.39.refs_0_), channel_id=1, source_target_pairs={{24,0},{25,1},{26,2},{27,3},{28,4},{29,5},{30,6},{31,7},{16,8},{17... | collective-permute-start | bytes 1769480 | tf_op jit(solution)/shard_map/gather/ppermute | solution.py:254
  61.7 0.7 collective-permute-start.10
  62.4 0.7 collective-permute-start.11
  63.1 0.7 collective-permute-start.13
  63.8 0.7 collective-permute-start.14
  64.6 4.5 %collective-permute-done.1.refs_1_ = f32[128,1152]{1,0:T(8,128)S(1)} collective-permute-done((f32[128,1152]{1,0:T(8,128)S(1)}, f32[128,1152]{1,0:T(8,128)S(1)}, u32[]{:S(2)}, u32[]{:S(2)}) %collective-permute-start.1) | collective-permute-done | bytes 589856 | tf_op jit(solution)/shard_map/gather/ppermute | solution.py:254
  83.3 0.9 forward_6.1
  85.5 1.3 forward_7.1
  88.2 1.6 diagonal.1
  89.9 0.7 backward_6.1.before
  91.9 0.7 backward_5.1.before
  94.0 0.7 backward_4.1.before
  96.1 0.7 backward_3.1.before
  98.2 0.7 backward_2.1.before
  100.2 0.7 backward_1.1.before
  102.3 0.7 backward_0.1
  103.7 111.6 %all-to-all-start.1 = ((f32[16,16,128]{2,1,0:T(8,128)}), f32[16,16,128]{2,1,0:T(8,128)S(1)}, u32[]{:S(2)}, u32[]{:S(2)}) async-start(f32[16,16,128]{2,1,0:T(8,128)} %pad_maximum_fusion), calls=%async_computation.1 | async-start | bytes 262144 | tf_op jit(solution)/shard_map/collect/all_to_all | solution.py:258
  215.3 7.6 %all-to-all-done.1 = f32[16,16,128]{2,1,0:T(8,128)S(1)} async-done(((f32[16,16,128]{2,1,0:T(8,128)}), f32[16,16,128]{2,1,0:T(8,128)S(1)}, u32[]{:S(2)}, u32[]{:S(2)}) %all-to-all-start.1) | async-done | bytes 131104 | tf_op jit(solution)/shard_map/collect/all_to_all | solution.py:258
  (90 shorter events, 28.7 us)
Async XLA Ops:
  6.5 25.5 %collective-permute-start = (f32[128,1152]{1,0:T(8,128)S(1)}, f32[128,1152]{1,0:T(8,128)S(1)}, u32[]{:S(2)}, u32[]{:S(2)}) collective-permute-start(f32[128,1152]{1,0:T(8,128)S(1)} %get-tuple-element.39.refs_0_), channel_id=1, source_target_pairs={{0,1},{1,2},{2,3},{3,4},{4,5},{5,6},{6,7},{7,0},{8,9},{9,10},{10,1... | collective-permute-start | bytes 1769480 | tf_op jit(solution)/shard_map/gather/ppermute | solution.py:254
  7.2 25.5 %collective-permute-start.4 = (f32[128,1152]{1,0:T(8,128)S(1)}, f32[128,1152]{1,0:T(8,128)S(1)}, u32[]{:S(2)}, u32[]{:S(2)}) collective-permute-start(f32[128,1152]{1,0:T(8,128)S(1)} %get-tuple-element.39.refs_0_), channel_id=1, source_target_pairs={{24,7},{25,0},{26,1},{27,2},{28,3},{29,4},{30,5},{31,6},{16,15},{1... | collective-permute-start | bytes 1769480 | tf_op jit(solution)/shard_map/gather/ppermute | solution.py:254
  15.9 16.1 %all-to-all-start = ((f32[16,16,128]{2,1,0:T(8,128)}), f32[16,16,128]{2,1,0:T(8,128)S(1)}, u32[]{:S(2)}, u32[]{:S(2)}) async-start(f32[16,16,128]{2,1,0:T(8,128)} %get-tuple-element.38), calls=%async_computation | async-start | bytes 262144 | tf_op jit(solution)/shard_map/gather/all_to_all | solution.py:258
  24.4 9.0 %collective-permute-start.2 = (f32[128,1152]{1,0:T(8,128)S(1)}, f32[128,1152]{1,0:T(8,128)S(1)}, u32[]{:S(2)}, u32[]{:S(2)}) collective-permute-start(f32[128,1152]{1,0:T(8,128)S(1)} %get-tuple-element.39.refs_0_), channel_id=1, source_target_pairs={{0,7},{1,0},{2,1},{3,2},{4,3},{5,4},{6,5},{7,6},{8,15},{9,8},{10,9... | collective-permute-start | bytes 1769480 | tf_op jit(solution)/shard_map/gather/ppermute | solution.py:254
  25.1 15.5 %collective-permute-start.3 = (f32[128,1152]{1,0:T(8,128)S(1)}, f32[128,1152]{1,0:T(8,128)S(1)}, u32[]{:S(2)}, u32[]{:S(2)}) collective-permute-start(f32[128,1152]{1,0:T(8,128)S(1)} %get-tuple-element.39.refs_0_), channel_id=1, source_target_pairs={{24,1},{25,2},{26,3},{27,4},{28,5},{29,6},{30,7},{31,0},{16,9},{17... | collective-permute-start | bytes 1769480 | tf_op jit(solution)/shard_map/gather/ppermute | solution.py:254
  32.0 9.3 %collective-permute-start.5 = (f32[128,1152]{1,0:T(8,128)S(1)}, f32[128,1152]{1,0:T(8,128)S(1)}, u32[]{:S(2)}, u32[]{:S(2)}) collective-permute-start(f32[128,1152]{1,0:T(8,128)S(1)} %get-tuple-element.42.refs_2_), channel_id=1, source_target_pairs={{0,1},{1,2},{2,3},{3,4},{4,5},{5,6},{6,7},{7,0},{8,9},{9,10},{10,1... | collective-permute-start | bytes 1769480 | tf_op jit(solution)/shard_map/gather/ppermute | solution.py:254
  32.7 9.3 %collective-permute-start.8 = (f32[128,1152]{1,0:T(8,128)S(1)}, f32[128,1152]{1,0:T(8,128)S(1)}, u32[]{:S(2)}, u32[]{:S(2)}) collective-permute-start(f32[128,1152]{1,0:T(8,128)S(1)} %collective-permute-done.4.refs_5_), channel_id=1, source_target_pairs={{0,7},{1,0},{2,1},{3,2},{4,3},{5,4},{6,5},{7,6},{8,15},{9,8},{10,9... | collective-permute-start | bytes 1769480 | tf_op jit(solution)/shard_map/gather/ppermute | solution.py:254
  33.4 28.3 %collective-permute-start.6 = (f32[128,1152]{1,0:T(8,128)S(1)}, f32[128,1152]{1,0:T(8,128)S(1)}, u32[]{:S(2)}, u32[]{:S(2)}) collective-permute-start(f32[128,1152]{1,0:T(8,128)S(1)} %collective-permute-done.2.refs_3_), channel_id=1, source_target_pairs={{0,7},{1,0},{2,1},{3,2},{4,3},{5,4},{6,5},{7,6},{8,15},{9,8},{10,9... | collective-permute-start | bytes 1769480 | tf_op jit(solution)/shard_map/gather/ppermute | solution.py:254
  40.5 21.9 %collective-permute-start.7 = (f32[128,1152]{1,0:T(8,128)S(1)}, f32[128,1152]{1,0:T(8,128)S(1)}, u32[]{:S(2)}, u32[]{:S(2)}) collective-permute-start(f32[128,1152]{1,0:T(8,128)S(1)} %collective-permute-done.3.refs_4_), channel_id=1, source_target_pairs={{0,1},{1,2},{2,3},{3,4},{4,5},{5,6},{6,7},{7,0},{8,9},{9,10},{10,1... | collective-permute-start | bytes 1769480 | tf_op jit(solution)/shard_map/gather/ppermute | solution.py:254
  41.2 21.9 %collective-permute-start.9 = (f32[128,1152]{1,0:T(8,128)S(1)}, f32[128,1152]{1,0:T(8,128)S(1)}, u32[]{:S(2)}, u32[]{:S(2)}) collective-permute-start(f32[128,1152]{1,0:T(8,128)S(1)} %collective-permute-done.5.refs_0_), channel_id=1, source_target_pairs={{0,1},{1,2},{2,3},{3,4},{4,5},{5,6},{6,7},{7,0},{8,9},{9,10},{10,1... | collective-permute-start | bytes 1769480 | tf_op jit(solution)/shard_map/gather/ppermute | solution.py:254
  42.0 21.9 %collective-permute-start.12 = (f32[128,1152]{1,0:T(8,128)S(1)}, f32[128,1152]{1,0:T(8,128)S(1)}, u32[]{:S(2)}, u32[]{:S(2)}) collective-permute-start(f32[128,1152]{1,0:T(8,128)S(1)} %collective-permute-done.8.refs_3_), channel_id=1, source_target_pairs={{0,7},{1,0},{2,1},{3,2},{4,3},{5,4},{6,5},{7,6},{8,15},{9,8},{10,9... | collective-permute-start | bytes 1769480 | tf_op jit(solution)/shard_map/gather/ppermute | solution.py:254
  42.7 26.4 %collective-permute-start.1 = (f32[128,1152]{1,0:T(8,128)S(1)}, f32[128,1152]{1,0:T(8,128)S(1)}, u32[]{:S(2)}, u32[]{:S(2)}) collective-permute-start(f32[128,1152]{1,0:T(8,128)S(1)} %get-tuple-element.39.refs_0_), channel_id=1, source_target_pairs={{24,0},{25,1},{26,2},{27,3},{28,4},{29,5},{30,6},{31,7},{16,8},{17... | collective-permute-start | bytes 1769480 | tf_op jit(solution)/shard_map/gather/ppermute | solution.py:254
  61.7 8.5 %collective-permute-start.10 = (f32[128,1152]{1,0:T(8,128)S(1)}, f32[128,1152]{1,0:T(8,128)S(1)}, u32[]{:S(2)}, u32[]{:S(2)}) collective-permute-start(f32[128,1152]{1,0:T(8,128)S(1)} %collective-permute-done.6.refs_1_), channel_id=1, source_target_pairs={{0,7},{1,0},{2,1},{3,2},{4,3},{5,4},{6,5},{7,6},{8,15},{9,8},{10,9... | collective-permute-start | bytes 1769480 | tf_op jit(solution)/shard_map/gather/ppermute | solution.py:254
  62.4 7.7 %collective-permute-start.11 = (f32[128,1152]{1,0:T(8,128)S(1)}, f32[128,1152]{1,0:T(8,128)S(1)}, u32[]{:S(2)}, u32[]{:S(2)}) collective-permute-start(f32[128,1152]{1,0:T(8,128)S(1)} %collective-permute-done.7.refs_2_), channel_id=1, source_target_pairs={{0,1},{1,2},{2,3},{3,4},{4,5},{5,6},{6,7},{7,0},{8,9},{9,10},{10,1... | collective-permute-start | bytes 1769480 | tf_op jit(solution)/shard_map/gather/ppermute | solution.py:254
  63.1 7.0 %collective-permute-start.13 = (f32[128,1152]{1,0:T(8,128)S(1)}, f32[128,1152]{1,0:T(8,128)S(1)}, u32[]{:S(2)}, u32[]{:S(2)}) collective-permute-start(f32[128,1152]{1,0:T(8,128)S(1)} %collective-permute-done.9.refs_0_), channel_id=1, source_target_pairs={{0,1},{1,2},{2,3},{3,4},{4,5},{5,6},{6,7},{7,0},{8,9},{9,10},{10,1... | collective-permute-start | bytes 1769480 | tf_op jit(solution)/shard_map/gather/ppermute | solution.py:254
  63.8 6.3 %collective-permute-start.14 = (f32[128,1152]{1,0:T(8,128)S(1)}, f32[128,1152]{1,0:T(8,128)S(1)}, u32[]{:S(2)}, u32[]{:S(2)}) collective-permute-start(f32[128,1152]{1,0:T(8,128)S(1)} %collective-permute-done.12.refs_3_), channel_id=1, source_target_pairs={{0,7},{1,0},{2,1},{3,2},{4,3},{5,4},{6,5},{7,6},{8,15},{9,8},{10,9... | collective-permute-start | bytes 1769480 | tf_op jit(solution)/shard_map/gather/ppermute | solution.py:254
  71.6 1.3 collective-permute-start.15
  73.6 1.3 collective-permute-start.17
  75.7 1.3 collective-permute-start.19
  77.8 1.3 collective-permute-start.21
  79.9 1.3 collective-permute-start.23
  81.9 1.3 collective-permute-start.25
  84.2 1.3 collective-permute-start.27
  86.9 3.0 %collective-permute-start.29 = (f32[16,8,128]{2,1,0:T(8,128)S(1)}, f32[16,8,128]{2,1,0:T(8,128)S(1)}, u32[]{:S(2)}, u32[]{:S(2)}) collective-permute-start(f32[16,8,128]{2,1,0:T(8,128)S(1)} %get-tuple-element.72.before), channel_id=1, source_target_pairs={{120,64},{121,65},{122,66},{123,67},{124,68},{125,69},{126,70},{12... | collective-permute-start | bytes 196616 | tf_op jit(solution)/shard_map/ppermute | solution.py:244
  87.5 2.3 %collective-permute-start.30 = (f32[16,8,128]{2,1,0:T(8,128)S(1)}, f32[16,8,128]{2,1,0:T(8,128)S(1)}, u32[]{:S(2)}, u32[]{:S(2)}) collective-permute-start(f32[16,8,128]{2,1,0:T(8,128)S(1)} %get-tuple-element.72.before), channel_id=1, source_target_pairs={{120,72},{121,73},{122,74},{123,75},{124,76},{125,77},{126,78},{12... | collective-permute-start | bytes 196616 | tf_op jit(solution)/shard_map/ppermute | solution.py:244
  90.6 1.3 collective-permute-start.31
  92.6 1.3 collective-permute-start.33
  94.7 1.3 collective-permute-start.35
  96.8 1.3 collective-permute-start.37
  98.9 1.3 collective-permute-start.39
  100.9 1.3 collective-permute-start.41
  103.7 119.1 %all-to-all-start.1 = ((f32[16,16,128]{2,1,0:T(8,128)}), f32[16,16,128]{2,1,0:T(8,128)S(1)}, u32[]{:S(2)}, u32[]{:S(2)}) async-start(f32[16,16,128]{2,1,0:T(8,128)} %pad_maximum_fusion), calls=%async_computation.1 | async-start | bytes 262144 | tf_op jit(solution)/shard_map/collect/all_to_all | solution.py:258
  (17 other events, 12.2 us)

commit v4 on v3

v4 whole, which is shorter than its diff:
```python
import functools

import jax
import jax.numpy as jnp
from jax import lax
from jax.experimental import pallas as pl
from jax.experimental.pallas import tpu as pltpu
from jax.sharding import Mesh
from jax.sharding import PartitionSpec as P

LEVELS, Y, Z = 8, 4, 8
CLASS = 2 * Z
NB, BLOCK, LOADS = 8, 128, 64
ROWS = LOADS // Z
WIDE = NB * BLOCK
AXES = ("chain", "y", "z")
TEAMS = [[y * Z + z for y in (side, Y - 1 - side) for z in range(Z)] for side in range(2)]
F32, BF16, I32 = jnp.float32, jnp.bfloat16, jnp.int32
VMEM = pl.BlockSpec(memory_space=pltpu.VMEM)
SMEM = pl.BlockSpec(memory_space=pltpu.SMEM)
HBM = pl.BlockSpec(memory_space=pltpu.HBM)
PARAMS = pltpu.CompilerParams(vmem_limit_bytes=24 << 20)
PIECE = jax.ShapeDtypeStruct((CLASS, ROWS, BLOCK), F32)
PACKED = jax.ShapeDtypeStruct((BLOCK + ROWS, WIDE + BLOCK), F32)
GROUPS = (
    ((0, 0), (0, 1), (-1, 0), (1, 0), (-1, 1), (1, 1)),
    ((-2, 0), (2, 0), (-2, 1), (2, 1)),
    ((-3, 0), (3, 0), (-3, 1), (3, 1), (-4, 0), (4, 1)),
)
HIGHEST = lax.Precision.HIGHEST
CONTRACT_LAST = (((1,), (1,)), ((), ()))


def half_at(level):
    return (level + level // 2) % 2


def half_of(row):
    return (row >= Y // 2).astype(I32) if hasattr(row, "astype") else int(row >= Y // 2)


def side_of(row):
    return ((row == 1) | (row == 2)).astype(I32)


def prepare_kernel(pattern_far, rhs_far, inverse_far, factor_far, piece, pattern, rhs, inverse, factor, arrival):
    copies = [
        pltpu.make_async_copy(source, target, arrival.at[i])
        for i, (source, target) in enumerate(((inverse_far, inverse), (factor_far, factor), (rhs_far, rhs), (pattern_far, pattern)))
    ]
    for copy in copies:
        copy.start()
    place, row, member = lax.axis_index("chain"), lax.axis_index("y"), lax.axis_index("z")
    last = place == LEVELS - 1
    side = side_of(row)
    copies[0].wait()
    turned = inverse[...].T
    piece[:BLOCK, WIDE:] = turned
    copies[1].wait()

    @pl.when(last)
    def _():
        piece[:BLOCK, :BLOCK] = jnp.dot(turned, inverse[...], precision=HIGHEST, preferred_element_type=F32)
        piece[:BLOCK, BLOCK:WIDE] = jnp.zeros((BLOCK, WIDE - BLOCK), F32)

    @pl.when(jnp.logical_not(last))
    def _():
        for k in range(NB):
            piece[:BLOCK, k * BLOCK : (k + 1) * BLOCK] = lax.dot_general(
                turned, factor[k], CONTRACT_LAST, precision=HIGHEST, preferred_element_type=F32
            )

    copies[2].wait()
    copies[3].wait()
    lane = lax.broadcasted_iota(I32, (8, BLOCK), 1)
    marks = jnp.zeros((8, BLOCK), F32)
    for k in range(NB):
        target = pattern[0, k]
        there = lax.div(target, Z)
        seat_number = (side_of(there) ^ side) * CLASS + half_of(there) * Z + lax.rem(target, Z)
        seat_number = jnp.where(last, half_of(row) * Z + member, seat_number)
        marks = jnp.where(lane == k, seat_number.astype(F32), marks)
    piece[BLOCK:, WIDE:] = marks
    for i in range(Z):
        piece[BLOCK:, i * BLOCK : (i + 1) * BLOCK] = rhs[i * ROWS : (i + 1) * ROWS]


def prepare(pattern, rhs, inverse, factor):
    return pl.pallas_call(
        prepare_kernel,
        in_specs=[HBM] * 4,
        out_specs=VMEM,
        out_shape=PACKED,
        scratch_shapes=[
            pltpu.SMEM((1, NB), I32),
            pltpu.VMEM((LOADS, BLOCK), F32),
            pltpu.VMEM((BLOCK, BLOCK), F32),
            pltpu.VMEM((NB, BLOCK, BLOCK), F32),
            pltpu.SemaphoreType.DMA((4,)),
        ],
        compiler_params=PARAMS,
        name="prepare",
    )(pattern, rhs, inverse, factor)


def split(value):
    high = value.astype(BF16)
    return high, (value - high.astype(F32)).astype(BF16)


def split_kernel(count, *refs):
    high, low = refs[count:]
    for i, source in enumerate(refs[:count]):
        high[i], low[i] = split(source[:BLOCK, :WIDE])


def split_weights(pieces):
    shape = jax.ShapeDtypeStruct((len(pieces), BLOCK, WIDE), BF16)
    return pl.pallas_call(
        functools.partial(split_kernel, len(pieces)),
        in_specs=[VMEM] * len(pieces),
        out_specs=[VMEM] * 2,
        out_shape=[shape] * 2,
        compiler_params=PARAMS,
        cost_estimate=pl.CostEstimate(flops=0, transcendentals=0, bytes_accessed=8 * len(pieces) * BLOCK * WIDE),
        name="split_weights",
    )(*pieces)


def number(away, other):
    member = lax.axis_index("z")
    return (half_at(lax.axis_index("chain")) ^ other) * Z + lax.rem(member + (Z + away), Z)


ORDER = [step for group in GROUPS for step in group]


def receive_kernel(*refs):
    pieces, (residue, table) = refs[:-2], refs[-2:]
    mine = pl.ds(pl.multiple_of(lax.axis_index("z") * BLOCK, BLOCK), BLOCK)
    for step, piece in zip(ORDER, pieces):
        residue[number(*step)] = piece[BLOCK:, mine]
        table[number(*step)] = piece[BLOCK:, WIDE:].astype(I32)


def receive(pieces):
    return pl.pallas_call(
        receive_kernel,
        in_specs=[VMEM] * len(pieces),
        out_specs=[VMEM, VMEM],
        out_shape=[PIECE, jax.ShapeDtypeStruct(PIECE.shape, I32)],
        compiler_params=PARAMS,
        name="receive",
    )(*pieces)


def supernodes(weights):
    for group, (high, low) in zip(GROUPS, zip(weights[::2], weights[1::2])):
        for i, (away, other) in enumerate(group):
            yield number(away, other), high.at[i], low.at[i]


def active(level):
    return (lax.axis_index("chain") == level) & (half_of(lax.axis_index("y")) == half_at(level))


def forward_kernel(step, arrivals, table, residue, *refs):
    arrived, weights, (residue_out, own, other, total) = refs[:arrivals], refs[arrivals:-4], refs[-4:]

    @pl.when(jnp.logical_not(active(step)))
    def _():
        residue_out[...] = residue[...]

    @pl.when(active(step))
    def _():
        current = residue[...]
        for piece in arrived:
            current = current - piece[...]
        residue_out[...] = current
        if step < LEVELS - 1:
            total[...] = jnp.zeros_like(total)
        for sup, high, low in supernodes(weights):
            left = jnp.concatenate(split(residue_out[sup]), axis=0)
            if step == LEVELS - 1:
                terms = jnp.dot(left, high[:, :BLOCK], preferred_element_type=F32) + jnp.dot(left, low[:, :BLOCK], preferred_element_type=F32)
                own[sup] = terms[:ROWS] + terms[ROWS:]
                continue
            terms = jnp.dot(left, high[...], preferred_element_type=F32) + jnp.dot(left, low[...], preferred_element_type=F32)
            summed = terms[:ROWS] + terms[ROWS:]
            for k in range(NB):
                total[table[sup, k]] += summed[:, k * BLOCK : (k + 1) * BLOCK]
        if step < LEVELS - 1:
            own[...] = total[:CLASS]
            other[...] = total[CLASS:]


def forward_step(step, table, residue, arrived, weights):
    return pl.pallas_call(
        functools.partial(forward_kernel, step, len(arrived)),
        in_specs=[SMEM] + [VMEM] * (1 + len(arrived) + len(weights)),
        out_specs=[VMEM] * 3,
        out_shape=[PIECE] * 3,
        scratch_shapes=[pltpu.VMEM((2 * CLASS, ROWS, BLOCK), F32)],
        compiler_params=PARAMS,
        name=f"forward_{step}",
    )(table, residue, *arrived, *weights)


def turn_kernel(*refs):
    for source, target in zip(refs[:6], refs[6:]):
        for i in range(source.shape[0]):
            for k in range(NB):
                target[i, k * BLOCK : (k + 1) * BLOCK] = source[i, :, k * BLOCK : (k + 1) * BLOCK].T


def turn(weights):
    return pl.pallas_call(
        turn_kernel,
        in_specs=[VMEM] * len(weights),
        out_specs=[VMEM] * len(weights),
        out_shape=[jax.ShapeDtypeStruct((part.shape[0], WIDE, BLOCK), BF16) for part in weights],
        compiler_params=PARAMS,
        name="turn",
    )(*weights)


def backward_kernel(level, table, before, base, own, other, *refs):
    weights, (answer, picked) = refs[:-2], refs[-2:]

    @pl.when(jnp.logical_not(active(level)))
    def _():
        answer[...] = before[...]

    @pl.when(active(level))
    def _():
        for half, source in enumerate((own, other)):
            picked[half * CLASS : (half + 1) * CLASS] = jnp.concatenate(split(source[...]), axis=1)
        for sup, high, low in supernodes(weights):
            left = jnp.concatenate([picked[table[sup, k]] for k in range(NB)], axis=1)
            terms = jnp.dot(left, high[...], preferred_element_type=F32) + jnp.dot(left, low[...], preferred_element_type=F32)
            answer[sup] = base[sup] - (terms[:ROWS] + terms[ROWS:])


def backward_step(level, table, before, base, own, other, weights):
    return pl.pallas_call(
        functools.partial(backward_kernel, level),
        in_specs=[SMEM] + [VMEM] * (4 + len(weights)),
        out_specs=VMEM,
        out_shape=PIECE,
        scratch_shapes=[pltpu.VMEM((2 * CLASS, 2 * ROWS, BLOCK), BF16)],
        compiler_params=PARAMS,
        name=f"backward_{level}",
    )(table, before, base, own, other, *weights)


def double(left, right, dims):
    terms = 0.0
    for part in split(right):
        terms += lax.dot_general(jnp.concatenate(split(left), axis=0), part, dims, preferred_element_type=F32)
    return terms[:ROWS] + terms[ROWS:]


def diagonal_kernel(residue, *refs):
    pieces, (solved, base) = refs[:-2], refs[-2:]
    for step, piece in zip(ORDER, pieces):
        sup, turned = number(*step), piece[:BLOCK, WIDE:]
        value = double(residue[sup], turned, (((1,), (0,)), ((), ())))
        solved[sup] = value
        base[sup] = double(value, turned, CONTRACT_LAST)


def diagonal(residue, pieces):
    return pl.pallas_call(
        diagonal_kernel,
        in_specs=[VMEM] * (1 + len(pieces)),
        out_specs=[VMEM] * 2,
        out_shape=[PIECE] * 2,
        compiler_params=PARAMS,
        name="diagonal",
    )(residue, *pieces)


def index(chain, y, z):
    return (chain * Y + y) * Z + z


def seat(level, side):
    return side if half_at(level) == 0 else Y - 1 - side


def hop(value, source, target, cross):
    both = [(first, first + target - source) for first in (source % 4, source % 4 + 4)]
    pairs = [
        (index(first, seat(first, side), z), index(second, seat(second, side ^ cross), z))
        for first, second in both
        if 0 <= second < LEVELS
        for side in range(2)
        for z in range(Z)
    ]
    return lax.ppermute(value, AXES, pairs)


def ring(value, steps, native=False):
    pairs = []
    for level in range(LEVELS):
        for side in range(2):
            row = seat(level, side)
            source = Y - 1 - row if native else row
            pairs += [(index(level, source, z), index(level, row, (z + steps) % Z)) for z in range(Z)]
    return lax.ppermute(value, AXES, pairs)


def exchange(value):
    return lax.all_to_all(value, ("y", "z"), 0, 0, axis_index_groups=TEAMS)


def body(rhs, inverse, factor, pattern):
    weight_a = prepare(pattern[0], rhs[0, 0], inverse[0, 0], factor[0, 0])

    with jax.named_scope("gather"):
        left_a, right_a = ring(weight_a, 1), ring(weight_a, -1)
        weight_b, left_b, right_b = [ring(weight_a, steps, True) for steps in (0, 1, -1)]
        pieces = [[weight_a, weight_b, left_a, right_a, left_b, right_b]]
        for _ in range(2):
            left_a, right_a, left_b, right_b = ring(left_a, 1), ring(right_a, -1), ring(left_b, 1), ring(right_b, -1)
            pieces.append([left_a, right_a, left_b, right_b])
        pieces[2] += [ring(left_a, 1), ring(right_b, -1)]
        weights = [part for group in pieces for part in split_weights(group)]
        pieces = [piece for group in pieces for piece in group]
        residue, table = receive(pieces)
        table = table[:, 0, :NB]

    arrived = ()
    for step in range(LEVELS):
        residue, own, other = forward_step(step, table, residue, arrived, weights)
        if step < LEVELS - 1:
            arrived = (hop(other, step, step + 1, 1), hop(own, step, step + 1, 0))

    solved, base = diagonal(residue, pieces)
    turned = turn(weights)
    answer = own
    for level in range(LEVELS - 2, -1, -1):
        other = hop(answer, level + 1, level, 1)
        own = hop(answer, level + 1, level, 0)
        answer = backward_step(level, table, answer, base, own, other, turned)

    with jax.named_scope("collect"):
        home = exchange(jnp.concatenate([solved, answer], axis=1))
        home = jnp.where(half_at(lax.axis_index("chain")) == 1, home[Z:], home[:Z])
    return home[:, :ROWS].reshape(1, 1, LOADS, BLOCK), home[:, ROWS:].reshape(1, 1, LOADS, BLOCK)


def solution(mesh):
    fine = Mesh(mesh.devices.reshape(LEVELS, Y, Z), AXES)
    column = ("y", "z")
    specs = [P("chain", column, *([None] * rank)) for rank in (2, 2, 3, 1)]
    return jax.shard_map(body, mesh=fine, in_specs=tuple(specs), out_specs=(specs[0], specs[0]), check_vma=False)
```

time: 226 us -> 209 us (0.925)
  starting transfers between devices: 179 us -> 158 us
  waiting for transfers between devices: 20.7 us -> 23.8 us
    all_to_all x2 -> x1, starting transfers between devices: 120 us -> 100 us  [exchange(): return lax.all_to_all(value, ('y', 'z'), 0, 0, axis_index_groups=TEAMS)]
    ppermute x15, waiting for transfers between devices: 10.9 us -> 16.1 us  [ring(): return lax.ppermute(value, AXES, pairs)]
    all_to_all x2 -> x1, waiting for transfers between devices: 9.68 us -> 7.55 us  [exchange(): return lax.all_to_all(value, ('y', 'z'), 0, 0, axis_index_groups=TEAMS)]
    pallas_call x3 -> x4, Pallas kernels: 4.2 us -> 5.47 us  [the longest x1 2.21 us: turn(): pl.pallas_call(turn_kernel, in_specs=[VMEM] * len(weights), out_specs=[VM...]
  transfers between devices with their start and end apart: 45 -> 44, of which waited for: 4 -> 3; matrix products, arithmetic and copies ran while one was open for 0% -> 0% of each run, Pallas kernels for 1% -> 2%
where the time goes in v4:
time: 209 us; the launch traced here: 206 us
  starting transfers between devices  158 us (76%)
  waiting for transfers between devices  23.8 us (11%)
  Pallas kernels  18.3 us (9%)
  local copies, waits for them, and re-layouts  3.92 us (2%)
    all_to_all x1, starting transfers between devices, exchange(): return lax.all_to_all(value, ('y', 'z'), 0, 0, axis_index_groups=TEAMS)  100 us
    ppermute x15, starting transfers between devices, ring(): return lax.ppermute(value, AXES, pairs)  39.2 us
    ppermute x28, starting transfers between devices, hop(): return lax.ppermute(value, AXES, pairs)  18.8 us
    ppermute x15, waiting for transfers between devices, ring(): return lax.ppermute(value, AXES, pairs)  16.1 us
    all_to_all x1, waiting for transfers between devices, exchange(): return lax.all_to_all(value, ('y', 'z'), 0, 0, axis_index_groups=TEAMS)  7.55 us
    pallas_call x8, Pallas kernels, forward_step(): pl.pallas_call(functools.partial(forward_kernel, step, len(arrived)), in_...  6.16 us
    pallas_call x7, Pallas kernels, backward_step(): pl.pallas_call(functools.partial(backward_kernel, level), in_specs=[SMEM]...  5.11 us
  transfers between devices with their start and end apart: 44, of which 3 were waited for; matrix products, arithmetic and copies ran while one was open for 0% of the time, Pallas kernels for 2%

profile of v4, /device:TPU:24, one launch (start us, length us, event | category | flops | bytes accessed | tf_op | source)
XLA Modules:
  0.0 206.5 jit_solution(12132890333483430604)
XLA Ops:
  0.6 1.0 copy-done
  1.7 0.8 copy-done.1
  2.5 0.8 copy-done.2
  3.9 1.6 prepare.1.refs_0_
  5.5 0.7 collective-permute-start.1
  6.2 8.7 %collective-permute-start.4 = (f32[136,1152]{1,0:T(8,128)S(1)}, f32[136,1152]{1,0:T(8,128)S(1)}, u32[]{:S(2)}, u32[]{:S(2)}) collective-permute-start(f32[136,1152]{1,0:T(8,128)S(1)} %prepare.1.refs_0_), channel_id=1, source_target_pairs={{24,7},{25,0},{26,1},{27,2},{28,3},{29,4},{30,5},{31,6},{16,15},{1... | collective-permute-start | bytes 1880072 | tf_op jit(solution)/shard_map/gather/ppermute | solution.py:310
  14.9 0.7 collective-permute-start.2
  15.6 1.3 collective-permute-start.3
  16.9 0.7 collective-permute-start.5
  17.6 11.2 %collective-permute-done.4.refs_5_ = f32[136,1152]{1,0:T(8,128)S(1)} collective-permute-done((f32[136,1152]{1,0:T(8,128)S(1)}, f32[136,1152]{1,0:T(8,128)S(1)}, u32[]{:S(2)}, u32[]{:S(2)}) %collective-permute-start.4) | collective-permute-done | bytes 626720 | tf_op jit(solution)/shard_map/gather/ppermute | solution.py:310
  29.6 0.7 collective-permute-start.6
  30.3 0.7 collective-permute-start.7
  31.0 0.7 collective-permute-start.9
  31.8 0.7 collective-permute-start.12
  32.5 20.8 %collective-permute-start = (f32[136,1152]{1,0:T(8,128)S(1)}, f32[136,1152]{1,0:T(8,128)S(1)}, u32[]{:S(2)}, u32[]{:S(2)}) collective-permute-start(f32[136,1152]{1,0:T(8,128)S(1)} %prepare.1.refs_0_), channel_id=1, source_target_pairs={{24,0},{25,1},{26,2},{27,3},{28,4},{29,5},{30,6},{31,7},{16,8},{17... | collective-permute-start | bytes 1880072 | tf_op jit(solution)/shard_map/gather/ppermute | solution.py:310
  53.3 0.7 collective-permute-start.10
  54.0 0.7 collective-permute-start.11
  54.8 0.7 collective-permute-start.13
  55.5 0.7 collective-permute-start.14
  56.2 4.9 %collective-permute-done.refs_1_ = f32[136,1152]{1,0:T(8,128)S(1)} collective-permute-done((f32[136,1152]{1,0:T(8,128)S(1)}, f32[136,1152]{1,0:T(8,128)S(1)}, u32[]{:S(2)}, u32[]{:S(2)}) %collective-permute-start) | collective-permute-done | bytes 626720 | tf_op jit(solution)/shard_map/gather/ppermute | solution.py:310
  74.4 0.8 collective-permute-start.26
  77.4 1.3 forward_7.1
  80.0 2.2 %turn.1 = (bf16[6,1024,128]{2,1,0:T(8,128)(2,1)S(1)}, bf16[6,1024,128]{2,1,0:T(8,128)(2,1)S(1)}, bf16[4,1024,128]{2,1,0:T(8,128)(2,1)S(1)}, bf16[4,1024,128]{2,1...) custom-call(bf16[6,128,1024]{2,1,0:T(8,128)(2,1)S(1)} %get-tuple-element.43.refs_0_.refs_2_, ...), custom_call_target="tpu_custom_call" | custom-call | tf_op jit(solution)/shard_map/turn/pallas_call | solution.py:217
  82.2 1.6 diagonal.1
  83.9 0.7 backward_6.1.before
  88.1 0.7 backward_4.1.before
  90.1 0.7 backward_3.1.before
  92.2 0.7 backward_2.1.before
  94.3 0.9 backward_1.1.before
  96.6 0.7 backward_0.1
  97.9 100.4 %all-to-all-start = ((f32[16,16,128]{2,1,0:T(8,128)}), f32[16,16,128]{2,1,0:T(8,128)S(1)}, u32[]{:S(2)}, u32[]{:S(2)}) async-start(f32[16,16,128]{2,1,0:T(8,128)} %pad_maximum_fusion), calls=%async_computation | async-start | bytes 262144 | tf_op jit(solution)/shard_map/collect/all_to_all | solution.py:314
  198.3 7.6 %all-to-all-done = f32[16,16,128]{2,1,0:T(8,128)S(1)} async-done(((f32[16,16,128]{2,1,0:T(8,128)}), f32[16,16,128]{2,1,0:T(8,128)S(1)}, u32[]{:S(2)}, u32[]{:S(2)}) %all-to-all-start) | async-done | bytes 131104 | tf_op jit(solution)/shard_map/collect/all_to_all | solution.py:314
  (90 shorter events, 27.8 us)
Async XLA Ops:
  5.5 11.4 %collective-permute-start.1 = (f32[136,1152]{1,0:T(8,128)S(1)}, f32[136,1152]{1,0:T(8,128)S(1)}, u32[]{:S(2)}, u32[]{:S(2)}) collective-permute-start(f32[136,1152]{1,0:T(8,128)S(1)} %prepare.1.refs_0_), channel_id=1, source_target_pairs={{0,1},{1,2},{2,3},{3,4},{4,5},{5,6},{6,7},{7,0},{8,9},{9,10},{10,1... | collective-permute-start | bytes 1880072 | tf_op jit(solution)/shard_map/gather/ppermute | solution.py:310
  6.2 22.7 %collective-permute-start.4 = (f32[136,1152]{1,0:T(8,128)S(1)}, f32[136,1152]{1,0:T(8,128)S(1)}, u32[]{:S(2)}, u32[]{:S(2)}) collective-permute-start(f32[136,1152]{1,0:T(8,128)S(1)} %prepare.1.refs_0_), channel_id=1, source_target_pairs={{24,7},{25,0},{26,1},{27,2},{28,3},{29,4},{30,5},{31,6},{16,15},{1... | collective-permute-start | bytes 1880072 | tf_op jit(solution)/shard_map/gather/ppermute | solution.py:310
  14.9 14.7 %collective-permute-start.2 = (f32[136,1152]{1,0:T(8,128)S(1)}, f32[136,1152]{1,0:T(8,128)S(1)}, u32[]{:S(2)}, u32[]{:S(2)}) collective-permute-start(f32[136,1152]{1,0:T(8,128)S(1)} %prepare.1.refs_0_), channel_id=1, source_target_pairs={{0,7},{1,0},{2,1},{3,2},{4,3},{5,4},{6,5},{7,6},{8,15},{9,8},{10,9... | collective-permute-start | bytes 1880072 | tf_op jit(solution)/shard_map/gather/ppermute | solution.py:310
  15.6 14.7 %collective-permute-start.3 = (f32[136,1152]{1,0:T(8,128)S(1)}, f32[136,1152]{1,0:T(8,128)S(1)}, u32[]{:S(2)}, u32[]{:S(2)}) collective-permute-start(f32[136,1152]{1,0:T(8,128)S(1)} %prepare.1.refs_0_), channel_id=1, source_target_pairs={{24,1},{25,2},{26,3},{27,4},{28,5},{29,6},{30,7},{31,0},{16,9},{17... | collective-permute-start | bytes 1880072 | tf_op jit(solution)/shard_map/gather/ppermute | solution.py:310
  16.9 14.1 %collective-permute-start.5 = (f32[136,1152]{1,0:T(8,128)S(1)}, f32[136,1152]{1,0:T(8,128)S(1)}, u32[]{:S(2)}, u32[]{:S(2)}) collective-permute-start(f32[136,1152]{1,0:T(8,128)S(1)} %collective-permute-done.1.refs_2_), channel_id=1, source_target_pairs={{0,1},{1,2},{2,3},{3,4},{4,5},{5,6},{6,7},{7,0},{8,9},{9,10},{10,1... | collective-permute-start | bytes 1880072 | tf_op jit(solution)/shard_map/gather/ppermute | solution.py:310
  28.9 2.9 %collective-permute-start.8 = (f32[136,1152]{1,0:T(8,128)S(1)}, f32[136,1152]{1,0:T(8,128)S(1)}, u32[]{:S(2)}, u32[]{:S(2)}) collective-permute-start(f32[136,1152]{1,0:T(8,128)S(1)} %collective-permute-done.4.refs_5_), channel_id=1, source_target_pairs={{0,7},{1,0},{2,1},{3,2},{4,3},{5,4},{6,5},{7,6},{8,15},{9,8},{10,9... | collective-permute-start | bytes 1880072 | tf_op jit(solution)/shard_map/gather/ppermute | solution.py:310
  29.6 23.7 %collective-permute-start.6 = (f32[136,1152]{1,0:T(8,128)S(1)}, f32[136,1152]{1,0:T(8,128)S(1)}, u32[]{:S(2)}, u32[]{:S(2)}) collective-permute-start(f32[136,1152]{1,0:T(8,128)S(1)} %collective-permute-done.2.refs_3_), channel_id=1, source_target_pairs={{0,7},{1,0},{2,1},{3,2},{4,3},{5,4},{6,5},{7,6},{8,15},{9,8},{10,9... | collective-permute-start | bytes 1880072 | tf_op jit(solution)/shard_map/gather/ppermute | solution.py:310
  30.3 23.7 %collective-permute-start.7 = (f32[136,1152]{1,0:T(8,128)S(1)}, f32[136,1152]{1,0:T(8,128)S(1)}, u32[]{:S(2)}, u32[]{:S(2)}) collective-permute-start(f32[136,1152]{1,0:T(8,128)S(1)} %collective-permute-done.3.refs_4_), channel_id=1, source_target_pairs={{0,1},{1,2},{2,3},{3,4},{4,5},{5,6},{6,7},{7,0},{8,9},{9,10},{10,1... | collective-permute-start | bytes 1880072 | tf_op jit(solution)/shard_map/gather/ppermute | solution.py:310
  31.0 23.7 %collective-permute-start.9 = (f32[136,1152]{1,0:T(8,128)S(1)}, f32[136,1152]{1,0:T(8,128)S(1)}, u32[]{:S(2)}, u32[]{:S(2)}) collective-permute-start(f32[136,1152]{1,0:T(8,128)S(1)} %collective-permute-done.5.refs_6_.refs_0_), channel_id=1, source_target_pairs={{0,1},{1,2},{2,3},{3,4},{4,5},{5,6},{6,7},{7,0},{8,9},{9,10},{10,1... | collective-permute-start | bytes 1880072 | tf_op jit(solution)/shard_map/gather/ppermute | solution.py:310
  31.8 23.7 %collective-permute-start.12 = (f32[136,1152]{1,0:T(8,128)S(1)}, f32[136,1152]{1,0:T(8,128)S(1)}, u32[]{:S(2)}, u32[]{:S(2)}) collective-permute-start(f32[136,1152]{1,0:T(8,128)S(1)} %collective-permute-done.8.refs_9_.refs_3_), channel_id=1, source_target_pairs={{0,7},{1,0},{2,1},{3,2},{4,3},{5,4},{6,5},{7,6},{8,15},{9,8},{10,9... | collective-permute-start | bytes 1880072 | tf_op jit(solution)/shard_map/gather/ppermute | solution.py:310
  32.5 28.6 %collective-permute-start = (f32[136,1152]{1,0:T(8,128)S(1)}, f32[136,1152]{1,0:T(8,128)S(1)}, u32[]{:S(2)}, u32[]{:S(2)}) collective-permute-start(f32[136,1152]{1,0:T(8,128)S(1)} %prepare.1.refs_0_), channel_id=1, source_target_pairs={{24,0},{25,1},{26,2},{27,3},{28,4},{29,5},{30,6},{31,7},{16,8},{17... | collective-permute-start | bytes 1880072 | tf_op jit(solution)/shard_map/gather/ppermute | solution.py:310
  53.3 8.7 %collective-permute-start.10 = (f32[136,1152]{1,0:T(8,128)S(1)}, f32[136,1152]{1,0:T(8,128)S(1)}, u32[]{:S(2)}, u32[]{:S(2)}) collective-permute-start(f32[136,1152]{1,0:T(8,128)S(1)} %collective-permute-done.6.refs_7_.refs_1_), channel_id=1, source_target_pairs={{0,7},{1,0},{2,1},{3,2},{4,3},{5,4},{6,5},{7,6},{8,15},{9,8},{10,9... | collective-permute-start | bytes 1880072 | tf_op jit(solution)/shard_map/gather/ppermute | solution.py:310
  54.0 8.0 %collective-permute-start.11 = (f32[136,1152]{1,0:T(8,128)S(1)}, f32[136,1152]{1,0:T(8,128)S(1)}, u32[]{:S(2)}, u32[]{:S(2)}) collective-permute-start(f32[136,1152]{1,0:T(8,128)S(1)} %collective-permute-done.7.refs_8_.refs_2_), channel_id=1, source_target_pairs={{0,1},{1,2},{2,3},{3,4},{4,5},{5,6},{6,7},{7,0},{8,9},{9,10},{10,1... | collective-permute-start | bytes 1880072 | tf_op jit(solution)/shard_map/gather/ppermute | solution.py:310
  54.8 7.3 %collective-permute-start.13 = (f32[136,1152]{1,0:T(8,128)S(1)}, f32[136,1152]{1,0:T(8,128)S(1)}, u32[]{:S(2)}, u32[]{:S(2)}) collective-permute-start(f32[136,1152]{1,0:T(8,128)S(1)} %collective-permute-done.9.refs_10_.refs_0_), channel_id=1, source_target_pairs={{0,1},{1,2},{2,3},{3,4},{4,5},{5,6},{6,7},{7,0},{8,9},{9,10},{10,1... | collective-permute-start | bytes 1880072 | tf_op jit(solution)/shard_map/gather/ppermute | solution.py:310
  55.5 6.6 %collective-permute-start.14 = (f32[136,1152]{1,0:T(8,128)S(1)}, f32[136,1152]{1,0:T(8,128)S(1)}, u32[]{:S(2)}, u32[]{:S(2)}) collective-permute-start(f32[136,1152]{1,0:T(8,128)S(1)} %collective-permute-done.12.refs_13_.refs_3_), channel_id=1, source_target_pairs={{0,7},{1,0},{2,1},{3,2},{4,3},{5,4},{6,5},{7,6},{8,15},{9,8},{10,9... | collective-permute-start | bytes 1880072 | tf_op jit(solution)/shard_map/gather/ppermute | solution.py:310
  63.4 1.3 collective-permute-start.15
  65.5 1.3 collective-permute-start.17
  67.6 1.3 collective-permute-start.19
  69.6 1.3 collective-permute-start.21
  71.7 1.3 collective-permute-start.23
  73.8 1.5 collective-permute-start.25
  74.4 0.9 collective-permute-start.26
  76.0 1.3 collective-permute-start.27
  78.7 5.2 %collective-permute-start.29 = (f32[16,8,128]{2,1,0:T(8,128)S(1)}, f32[16,8,128]{2,1,0:T(8,128)S(1)}, u32[]{:S(2)}, u32[]{:S(2)}) collective-permute-start(f32[16,8,128]{2,1,0:T(8,128)S(1)} %get-tuple-element.72.before), channel_id=1, source_target_pairs={{96,88},{97,89},{98,90},{99,91},{100,92},{101,93},{102,94},{103,95... | collective-permute-start | bytes 196616 | tf_op jit(solution)/shard_map/ppermute | solution.py:300
  79.3 4.5 %collective-permute-start.30 = (f32[16,8,128]{2,1,0:T(8,128)S(1)}, f32[16,8,128]{2,1,0:T(8,128)S(1)}, u32[]{:S(2)}, u32[]{:S(2)}) collective-permute-start(f32[16,8,128]{2,1,0:T(8,128)S(1)} %get-tuple-element.72.before), channel_id=1, source_target_pairs={{96,80},{97,81},{98,82},{99,83},{100,84},{101,85},{102,86},{103,87... | collective-permute-start | bytes 196616 | tf_op jit(solution)/shard_map/ppermute | solution.py:300
  84.6 1.3 collective-permute-start.31
  86.7 1.3 collective-permute-start.33
  88.8 1.3 collective-permute-start.35
  90.8 1.3 collective-permute-start.37
  92.9 1.3 collective-permute-start.39
  95.2 1.3 collective-permute-start.41
  97.9 107.9 %all-to-all-start = ((f32[16,16,128]{2,1,0:T(8,128)}), f32[16,16,128]{2,1,0:T(8,128)S(1)}, u32[]{:S(2)}, u32[]{:S(2)}) async-start(f32[16,16,128]{2,1,0:T(8,128)} %pad_maximum_fusion), calls=%async_computation | async-start | bytes 262144 | tf_op jit(solution)/shard_map/collect/all_to_all | solution.py:314
  (16 other events, 11.5 us)

commit v5 on v4

--- a/solution.py
+++ b/solution.py
@@ -14,7 +14,6 @@
 ROWS = LOADS // Z
 WIDE = NB * BLOCK
 AXES = ("chain", "y", "z")
-TEAMS = [[y * Z + z for y in (side, Y - 1 - side) for z in range(Z)] for side in range(2)]
 F32, BF16, I32 = jnp.float32, jnp.bfloat16, jnp.int32
 VMEM = pl.BlockSpec(memory_space=pltpu.VMEM)
 SMEM = pl.BlockSpec(memory_space=pltpu.SMEM)
@@ -225,7 +224,7 @@
 
 
 def backward_kernel(level, table, before, base, own, other, *refs):
-    weights, (answer, picked) = refs[:-2], refs[-2:]
+    weights, (answer, picked) = refs[:6], refs[-2:]
 
     @pl.when(jnp.logical_not(active(level)))
     def _():
@@ -239,6 +238,64 @@
             left = jnp.concatenate([picked[table[sup, k]] for k in range(NB)], axis=1)
             terms = jnp.dot(left, high[...], preferred_element_type=F32) + jnp.dot(left, low[...], preferred_element_type=F32)
             answer[sup] = base[sup] - (terms[:ROWS] + terms[ROWS:])
+
+
+def last_backward_kernel(table, before, base, own, other, *refs):
+    solved, both, answer, picked = refs[6:]
+    backward_kernel(0, table, before, base, own, other, *refs[:6], answer, picked)
+    for i in range(CLASS):
+        start = i // Z * 2 * ROWS
+        both[i % Z, start : start + ROWS] = solved[i]
+        both[i % Z, start + ROWS : start + 2 * ROWS] = answer[i]
+
+
+def last_backward_step(table, before, base, own, other, weights, solved):
+    return pl.pallas_call(
+        last_backward_kernel,
+        in_specs=[SMEM] + [VMEM] * (5 + len(weights)),
+        out_specs=VMEM,
+        out_shape=jax.ShapeDtypeStruct((Z, 4 * ROWS, BLOCK), F32),
+        scratch_shapes=[pltpu.VMEM(PIECE.shape, F32), pltpu.VMEM((2 * CLASS, 2 * ROWS, BLOCK), BF16)],
+        compiler_params=PARAMS,
+        name="backward_0",
+    )(table, before, base, own, other, *weights, solved)
+
+
+def part_kernel(halves, home, kept, moved):
+    half = halves[0]
+    for target, chosen in ((kept, half), (moved, 1 - half)):
+        for member in range(Z):
+            for i in range(2):
+                rows = pl.ds(pl.multiple_of((chosen * 2 + i) * ROWS, ROWS), ROWS)
+                target[i, member * ROWS : (member + 1) * ROWS] = home[member, rows]
+
+
+def part(halves, home):
+    shape = jax.ShapeDtypeStruct((2, LOADS, BLOCK), F32)
+    return pl.pallas_call(
+        part_kernel, in_specs=[SMEM, VMEM], out_specs=[VMEM] * 2, out_shape=[shape] * 2, compiler_params=PARAMS, name="part"
+    )(halves, home)
+
+
+def finish_kernel(kept, moved, first, second):
+    here = half_of(lax.axis_index("y")) == half_at(lax.axis_index("chain"))
+
+    @pl.when(here)
+    def _():
+        first[...] = kept[0]
+        second[...] = kept[1]
+
+    @pl.when(jnp.logical_not(here))
+    def _():
+        first[...] = moved[0]
+        second[...] = moved[1]
+
+
+def finish(kept, moved):
+    shape = jax.ShapeDtypeStruct((LOADS, BLOCK), F32)
+    return pl.pallas_call(
+        finish_kernel, in_specs=[VMEM] * 2, out_specs=[VMEM] * 2, out_shape=[shape] * 2, compiler_params=PARAMS, name="finish"
+    )(kept, moved)
 
 
 def backward_step(level, table, before, base, own, other, weights):
@@ -300,22 +357,19 @@
     return lax.ppermute(value, AXES, pairs)
 
 
-def ring(value, steps, native=False):
+def ring(value, steps, native=False, back=False):
     pairs = []
     for level in range(LEVELS):
         for side in range(2):
             row = seat(level, side)
             source = Y - 1 - row if native else row
-            pairs += [(index(level, source, z), index(level, row, (z + steps) % Z)) for z in range(Z)]
+            pairs += [(index(level, source, z), index(level, row, (z + steps) % Z))[:: -1 if back else 1] for z in range(Z)]
     return lax.ppermute(value, AXES, pairs)
 
 
-def exchange(value):
-    return lax.all_to_all(value, ("y", "z"), 0, 0, axis_index_groups=TEAMS)
-
-
 def body(rhs, inverse, factor, pattern):
-    weight_a = prepare(pattern[0], rhs[0, 0], inverse[0, 0], factor[0, 0])
+    arguments = [pltpu.with_memory_space_constraint(value, pltpu.HBM) for value in (pattern[0], rhs[0, 0], inverse[0, 0], factor[0, 0])]
+    weight_a = prepare(*arguments)
 
     with jax.named_scope("gather"):
         left_a, right_a = ring(weight_a, 1), ring(weight_a, -1)
@@ -342,12 +396,15 @@
     for level in range(LEVELS - 2, -1, -1):
         other = hop(answer, level + 1, level, 1)
         own = hop(answer, level + 1, level, 0)
-        answer = backward_step(level, table, answer, base, own, other, turned)
+        if level:
+            answer = backward_step(level, table, answer, base, own, other, turned)
+        else:
+            both = last_backward_step(table, answer, base, own, other, turned, solved)
 
     with jax.named_scope("collect"):
-        home = exchange(jnp.concatenate([solved, answer], axis=1))
-        home = jnp.where(half_at(lax.axis_index("chain")) == 1, home[Z:], home[:Z])
-    return home[:, :ROWS].reshape(1, 1, LOADS, BLOCK), home[:, ROWS:].reshape(1, 1, LOADS, BLOCK)
+        kept, moved = part(half_at(lax.axis_index("chain"))[None], lax.all_to_all(both, "z", 0, 0))
+        first, second = finish(kept, ring(moved, 0, True, True))
+    return first[None, None], second[None, None]
 
 
 def solution(mesh):

time: 209 us -> 202 us (0.967)
  starting transfers between devices: 158 us -> 63.8 us
  waiting for transfers between devices: 23.8 us -> 115 us
  local copies, waits for them, and re-layouts: 3.92 us -> 0.01 us
  Pallas kernels: 18.3 us -> 20.4 us
    all_to_all x1, starting transfers between devices: 100 us -> 4.5 us  [body(): lax.all_to_all(both, 'z', 0, 0)]
    ppermute x15 -> x16, waiting for transfers between devices: 16.1 us -> 106 us  [ring(): return lax.ppermute(value, AXES, pairs)]
    unnamed x8 -> x0, local copies, waits for them, and re-layouts: 3.29 us -> none
    ppermute x15 -> x16, starting transfers between devices: 39.2 us -> 40.6 us  [ring(): return lax.ppermute(value, AXES, pairs)]
    pallas_call x7 -> x6, Pallas kernels: 5.11 us -> 4.41 us  [backward_step(): pl.pallas_call(functools.partial(backward_kernel, level), in_specs=[SMEM]...]
  transfers between devices with their start and end apart: 44 -> 45, of which waited for: 3 -> 4; matrix products, arithmetic and copies ran while one was open for 0% -> 0% of each run, Pallas kernels for 2% -> 2%
where the time goes in v5:
time: 202 us; the launch traced here: 201 us
  waiting for transfers between devices  115 us (57%)
  starting transfers between devices  63.8 us (32%)
  Pallas kernels  20.4 us (10%)
    ppermute x16, waiting for transfers between devices, ring(): return lax.ppermute(value, AXES, pairs)  106 us
    ppermute x16, starting transfers between devices, ring(): return lax.ppermute(value, AXES, pairs)  40.6 us
    ppermute x28, starting transfers between devices, hop(): return lax.ppermute(value, AXES, pairs)  18.8 us
    all_to_all x1, waiting for transfers between devices, body(): lax.all_to_all(both, 'z', 0, 0)  9.08 us
    pallas_call x8, Pallas kernels, forward_step(): pl.pallas_call(functools.partial(forward_kernel, step, len(arrived)), in_...  6.16 us
    all_to_all x1, starting transfers between devices, body(): lax.all_to_all(both, 'z', 0, 0)  4.5 us
    pallas_call x6, Pallas kernels, backward_step(): pl.pallas_call(functools.partial(backward_kernel, level), in_specs=[SMEM]...  4.41 us
  transfers between devices with their start and end apart: 45, of which 4 were waited for; matrix products, arithmetic and copies ran while one was open for 0% of the time, Pallas kernels for 2%

profile of v5, /device:TPU:24, one launch (start us, length us, event | category | flops | bytes accessed | tf_op | source)
XLA Modules:
  0.0 201.2 jit_solution(5339258657649835873)
XLA Ops:
  0.6 2.4 %prepare.1.refs_0_ = f32[136,1152]{1,0:T(8,128)S(1)} custom-call(s32[1,8]{1,0:T(1,128)} %bitcast.26, f32[64,128]{1,0:T(8,128)} %bitcast.25, f32[128,128]{1,0:T(8,128)} %bitcast.24, f32[8,128,128]{2,1,0:T(8,128)} %bitcast.23), custom_call_target="tpu_custom_call" | custom-call | tf_op jit(solution)/shard_map/prepare/pallas_call | solution.py:88
  3.0 7.5 %collective-permute-start.4 = (f32[136,1152]{1,0:T(8,128)S(1)}, f32[136,1152]{1,0:T(8,128)S(1)}, u32[]{:S(2)}, u32[]{:S(2)}) collective-permute-start(f32[136,1152]{1,0:T(8,128)S(1)} %prepare.1.refs_0_), channel_id=1, source_target_pairs={{24,7},{25,0},{26,1},{27,2},{28,3},{29,4},{30,5},{31,6},{16,15},{1... | collective-permute-start | bytes 1880072 | tf_op jit(solution)/shard_map/gather/ppermute | solution.py:367
  10.5 0.7 collective-permute-start.1
  11.2 1.3 collective-permute-start.3
  12.5 0.7 collective-permute-start.2
  13.3 7.9 %collective-permute-done.4.refs_5_ = f32[136,1152]{1,0:T(8,128)S(1)} collective-permute-done((f32[136,1152]{1,0:T(8,128)S(1)}, f32[136,1152]{1,0:T(8,128)S(1)}, u32[]{:S(2)}, u32[]{:S(2)}) %collective-permute-start.4) | collective-permute-done | bytes 626720 | tf_op jit(solution)/shard_map/gather/ppermute | solution.py:367
  21.9 0.7 collective-permute-start.5
  22.6 0.7 collective-permute-start.7
  23.3 0.7 collective-permute-start.6
  24.0 0.7 collective-permute-start.12
  24.7 0.7 collective-permute-start.9
  25.4 22.1 %collective-permute-start = (f32[136,1152]{1,0:T(8,128)S(1)}, f32[136,1152]{1,0:T(8,128)S(1)}, u32[]{:S(2)}, u32[]{:S(2)}) collective-permute-start(f32[136,1152]{1,0:T(8,128)S(1)} %prepare.1.refs_0_), channel_id=1, source_target_pairs={{24,0},{25,1},{26,2},{27,3},{28,4},{29,5},{30,6},{31,7},{16,8},{17... | collective-permute-start | bytes 1880072 | tf_op jit(solution)/shard_map/gather/ppermute | solution.py:367
  47.5 0.7 collective-permute-start.11
  48.3 0.7 collective-permute-start.10
  49.0 0.7 collective-permute-start.14
  49.7 0.7 collective-permute-start.13
  50.4 4.9 %collective-permute-done.refs_1_ = f32[136,1152]{1,0:T(8,128)S(1)} collective-permute-done((f32[136,1152]{1,0:T(8,128)S(1)}, f32[136,1152]{1,0:T(8,128)S(1)}, u32[]{:S(2)}, u32[]{:S(2)}) %collective-permute-start) | collective-permute-done | bytes 626720 | tf_op jit(solution)/shard_map/gather/ppermute | solution.py:367
  68.7 0.8 collective-permute-start.26
  71.6 1.3 forward_7.1
  74.2 2.2 %turn.1 = (bf16[6,1024,128]{2,1,0:T(8,128)(2,1)S(1)}, bf16[6,1024,128]{2,1,0:T(8,128)(2,1)S(1)}, bf16[4,1024,128]{2,1,0:T(8,128)(2,1)S(1)}, bf16[4,1024,128]{2,1...) custom-call(bf16[6,128,1024]{2,1,0:T(8,128)(2,1)S(1)} %get-tuple-element.47.refs_0_.refs_2_, ...), custom_call_target="tpu_custom_call" | custom-call | tf_op jit(solution)/shard_map/turn/pallas_call | solution.py:216
  76.5 1.6 diagonal.1
  78.1 0.7 backward_6.1.before
  80.2 0.7 backward_5.1.before
  82.3 0.7 backward_4.1.before
  84.4 0.7 backward_3.1.before
  86.4 0.7 backward_2.1.before
  88.5 0.9 backward_1.1.before
  90.8 1.4 backward_0.1
  92.2 4.5 %all-to-all-start = ((f32[8,32,128]{2,1,0:T(8,128)}), f32[8,32,128]{2,1,0:T(8,128)S(1)}, u32[]{:S(2)}, u32[]{:S(2)}) async-start(f32[8,32,128]{2,1,0:T(8,128)} %backward_0.1), calls=%async_computation | async-start | bytes 262144 | tf_op jit(solution)/shard_map/collect/all_to_all | solution.py:405
  96.7 9.1 %all-to-all-done.home = f32[8,32,128]{2,1,0:T(8,128)S(1)} async-done(((f32[8,32,128]{2,1,0:T(8,128)}), f32[8,32,128]{2,1,0:T(8,128)S(1)}, u32[]{:S(2)}, u32[]{:S(2)}) %all-to-all-start) | async-done | bytes 131104 | tf_op jit(solution)/shard_map/collect/all_to_all | solution.py:405
  105.8 1.3 collective-permute-start.43
  107.1 93.5 %collective-permute-done.43.moved = f32[2,64,128]{2,1,0:T(8,128)S(1)} collective-permute-done((f32[2,64,128]{2,1,0:T(8,128)S(1)}, f32[2,64,128]{2,1,0:T(8,128)S(1)}, u32[]{:S(2)}, u32[]{:S(2)}) %collective-permute-start.43) | collective-permute-done | bytes 65568 | tf_op jit(solution)/shard_map/collect/ppermute | solution.py:367
  (83 shorter events, 25.8 us)
Async XLA Ops:
  3.0 18.1 %collective-permute-start.4 = (f32[136,1152]{1,0:T(8,128)S(1)}, f32[136,1152]{1,0:T(8,128)S(1)}, u32[]{:S(2)}, u32[]{:S(2)}) collective-permute-start(f32[136,1152]{1,0:T(8,128)S(1)} %prepare.1.refs_0_), channel_id=1, source_target_pairs={{24,7},{25,0},{26,1},{27,2},{28,3},{29,4},{30,5},{31,6},{16,15},{1... | collective-permute-start | bytes 1880072 | tf_op jit(solution)/shard_map/gather/ppermute | solution.py:367
  10.5 11.4 %collective-permute-start.1 = (f32[136,1152]{1,0:T(8,128)S(1)}, f32[136,1152]{1,0:T(8,128)S(1)}, u32[]{:S(2)}, u32[]{:S(2)}) collective-permute-start(f32[136,1152]{1,0:T(8,128)S(1)} %prepare.1.refs_0_), channel_id=1, source_target_pairs={{0,1},{1,2},{2,3},{3,4},{4,5},{5,6},{6,7},{7,0},{8,9},{9,10},{10,1... | collective-permute-start | bytes 1880072 | tf_op jit(solution)/shard_map/gather/ppermute | solution.py:367
  11.2 11.4 %collective-permute-start.3 = (f32[136,1152]{1,0:T(8,128)S(1)}, f32[136,1152]{1,0:T(8,128)S(1)}, u32[]{:S(2)}, u32[]{:S(2)}) collective-permute-start(f32[136,1152]{1,0:T(8,128)S(1)} %prepare.1.refs_0_), channel_id=1, source_target_pairs={{24,1},{25,2},{26,3},{27,4},{28,5},{29,6},{30,7},{31,0},{16,9},{17... | collective-permute-start | bytes 1880072 | tf_op jit(solution)/shard_map/gather/ppermute | solution.py:367
  12.5 10.7 %collective-permute-start.2 = (f32[136,1152]{1,0:T(8,128)S(1)}, f32[136,1152]{1,0:T(8,128)S(1)}, u32[]{:S(2)}, u32[]{:S(2)}) collective-permute-start(f32[136,1152]{1,0:T(8,128)S(1)} %prepare.1.refs_0_), channel_id=1, source_target_pairs={{0,7},{1,0},{2,1},{3,2},{4,3},{5,4},{6,5},{7,6},{8,15},{9,8},{10,9... | collective-permute-start | bytes 1880072 | tf_op jit(solution)/shard_map/gather/ppermute | solution.py:367
  21.1 2.9 %collective-permute-start.8 = (f32[136,1152]{1,0:T(8,128)S(1)}, f32[136,1152]{1,0:T(8,128)S(1)}, u32[]{:S(2)}, u32[]{:S(2)}) collective-permute-start(f32[136,1152]{1,0:T(8,128)S(1)} %collective-permute-done.4.refs_5_), channel_id=1, source_target_pairs={{0,7},{1,0},{2,1},{3,2},{4,3},{5,4},{6,5},{7,6},{8,15},{9,8},{10,9... | collective-permute-start | bytes 1880072 | tf_op jit(solution)/shard_map/gather/ppermute | solution.py:367
  21.9 2.9 %collective-permute-start.5 = (f32[136,1152]{1,0:T(8,128)S(1)}, f32[136,1152]{1,0:T(8,128)S(1)}, u32[]{:S(2)}, u32[]{:S(2)}) collective-permute-start(f32[136,1152]{1,0:T(8,128)S(1)} %collective-permute-done.1.refs_2_), channel_id=1, source_target_pairs={{0,1},{1,2},{2,3},{3,4},{4,5},{5,6},{6,7},{7,0},{8,9},{9,10},{10,1... | collective-permute-start | bytes 1880072 | tf_op jit(solution)/shard_map/gather/ppermute | solution.py:367
  22.6 25.0 %collective-permute-start.7 = (f32[136,1152]{1,0:T(8,128)S(1)}, f32[136,1152]{1,0:T(8,128)S(1)}, u32[]{:S(2)}, u32[]{:S(2)}) collective-permute-start(f32[136,1152]{1,0:T(8,128)S(1)} %collective-permute-done.3.refs_4_), channel_id=1, source_target_pairs={{0,1},{1,2},{2,3},{3,4},{4,5},{5,6},{6,7},{7,0},{8,9},{9,10},{10,1... | collective-permute-start | bytes 1880072 | tf_op jit(solution)/shard_map/gather/ppermute | solution.py:367
  23.3 25.0 %collective-permute-start.6 = (f32[136,1152]{1,0:T(8,128)S(1)}, f32[136,1152]{1,0:T(8,128)S(1)}, u32[]{:S(2)}, u32[]{:S(2)}) collective-permute-start(f32[136,1152]{1,0:T(8,128)S(1)} %collective-permute-done.2.refs_3_), channel_id=1, source_target_pairs={{0,7},{1,0},{2,1},{3,2},{4,3},{5,4},{6,5},{7,6},{8,15},{9,8},{10,9... | collective-permute-start | bytes 1880072 | tf_op jit(solution)/shard_map/gather/ppermute | solution.py:367
  24.0 25.0 %collective-permute-start.12 = (f32[136,1152]{1,0:T(8,128)S(1)}, f32[136,1152]{1,0:T(8,128)S(1)}, u32[]{:S(2)}, u32[]{:S(2)}) collective-permute-start(f32[136,1152]{1,0:T(8,128)S(1)} %collective-permute-done.8.refs_9_.refs_3_), channel_id=1, source_target_pairs={{0,7},{1,0},{2,1},{3,2},{4,3},{5,4},{6,5},{7,6},{8,15},{9,8},{10,9... | collective-permute-start | bytes 1880072 | tf_op jit(solution)/shard_map/gather/ppermute | solution.py:367
  24.7 25.0 %collective-permute-start.9 = (f32[136,1152]{1,0:T(8,128)S(1)}, f32[136,1152]{1,0:T(8,128)S(1)}, u32[]{:S(2)}, u32[]{:S(2)}) collective-permute-start(f32[136,1152]{1,0:T(8,128)S(1)} %collective-permute-done.5.refs_6_.refs_0_), channel_id=1, source_target_pairs={{0,1},{1,2},{2,3},{3,4},{4,5},{5,6},{6,7},{7,0},{8,9},{9,10},{10,1... | collective-permute-start | bytes 1880072 | tf_op jit(solution)/shard_map/gather/ppermute | solution.py:367
  25.4 29.8 %collective-permute-start = (f32[136,1152]{1,0:T(8,128)S(1)}, f32[136,1152]{1,0:T(8,128)S(1)}, u32[]{:S(2)}, u32[]{:S(2)}) collective-permute-start(f32[136,1152]{1,0:T(8,128)S(1)} %prepare.1.refs_0_), channel_id=1, source_target_pairs={{24,0},{25,1},{26,2},{27,3},{28,4},{29,5},{30,6},{31,7},{16,8},{17... | collective-permute-start | bytes 1880072 | tf_op jit(solution)/shard_map/gather/ppermute | solution.py:367
  47.5 8.7 %collective-permute-start.11 = (f32[136,1152]{1,0:T(8,128)S(1)}, f32[136,1152]{1,0:T(8,128)S(1)}, u32[]{:S(2)}, u32[]{:S(2)}) collective-permute-start(f32[136,1152]{1,0:T(8,128)S(1)} %collective-permute-done.7.refs_8_.refs_2_), channel_id=1, source_target_pairs={{0,1},{1,2},{2,3},{3,4},{4,5},{5,6},{6,7},{7,0},{8,9},{9,10},{10,1... | collective-permute-start | bytes 1880072 | tf_op jit(solution)/shard_map/gather/ppermute | solution.py:367
  48.3 8.0 %collective-permute-start.10 = (f32[136,1152]{1,0:T(8,128)S(1)}, f32[136,1152]{1,0:T(8,128)S(1)}, u32[]{:S(2)}, u32[]{:S(2)}) collective-permute-start(f32[136,1152]{1,0:T(8,128)S(1)} %collective-permute-done.6.refs_7_.refs_1_), channel_id=1, source_target_pairs={{0,7},{1,0},{2,1},{3,2},{4,3},{5,4},{6,5},{7,6},{8,15},{9,8},{10,9... | collective-permute-start | bytes 1880072 | tf_op jit(solution)/shard_map/gather/ppermute | solution.py:367
  49.0 7.3 %collective-permute-start.14 = (f32[136,1152]{1,0:T(8,128)S(1)}, f32[136,1152]{1,0:T(8,128)S(1)}, u32[]{:S(2)}, u32[]{:S(2)}) collective-permute-start(f32[136,1152]{1,0:T(8,128)S(1)} %collective-permute-done.12.refs_13_.refs_3_), channel_id=1, source_target_pairs={{0,7},{1,0},{2,1},{3,2},{4,3},{5,4},{6,5},{7,6},{8,15},{9,8},{10,9... | collective-permute-start | bytes 1880072 | tf_op jit(solution)/shard_map/gather/ppermute | solution.py:367
  49.7 6.6 %collective-permute-start.13 = (f32[136,1152]{1,0:T(8,128)S(1)}, f32[136,1152]{1,0:T(8,128)S(1)}, u32[]{:S(2)}, u32[]{:S(2)}) collective-permute-start(f32[136,1152]{1,0:T(8,128)S(1)} %collective-permute-done.9.refs_10_.refs_0_), channel_id=1, source_target_pairs={{0,1},{1,2},{2,3},{3,4},{4,5},{5,6},{6,7},{7,0},{8,9},{9,10},{10,1... | collective-permute-start | bytes 1880072 | tf_op jit(solution)/shard_map/gather/ppermute | solution.py:367
  57.7 1.3 collective-permute-start.15
  59.7 1.3 collective-permute-start.17
  61.8 1.3 collective-permute-start.19
  63.9 1.3 collective-permute-start.21
  65.9 1.3 collective-permute-start.23
  68.0 1.5 collective-permute-start.25
  70.2 1.3 collective-permute-start.27
  72.9 5.2 %collective-permute-start.30 = (f32[16,8,128]{2,1,0:T(8,128)S(1)}, f32[16,8,128]{2,1,0:T(8,128)S(1)}, u32[]{:S(2)}, u32[]{:S(2)}) collective-permute-start(f32[16,8,128]{2,1,0:T(8,128)S(1)} %get-tuple-element.74.before), channel_id=1, source_target_pairs={{96,80},{97,81},{98,82},{99,83},{100,84},{101,85},{102,86},{103,87... | collective-permute-start | bytes 196616 | tf_op jit(solution)/shard_map/ppermute | solution.py:357
  73.6 4.5 %collective-permute-start.29 = (f32[16,8,128]{2,1,0:T(8,128)S(1)}, f32[16,8,128]{2,1,0:T(8,128)S(1)}, u32[]{:S(2)}, u32[]{:S(2)}) collective-permute-start(f32[16,8,128]{2,1,0:T(8,128)S(1)} %get-tuple-element.74.before), channel_id=1, source_target_pairs={{96,88},{97,89},{98,90},{99,91},{100,92},{101,93},{102,94},{103,95... | collective-permute-start | bytes 196616 | tf_op jit(solution)/shard_map/ppermute | solution.py:357
  78.8 1.3 collective-permute-start.32
  80.9 1.3 collective-permute-start.34
  83.0 1.3 collective-permute-start.36
  85.1 1.3 collective-permute-start.38
  87.1 1.3 collective-permute-start.40
  89.4 1.3 collective-permute-start.42
  92.2 13.6 %all-to-all-start = ((f32[8,32,128]{2,1,0:T(8,128)}), f32[8,32,128]{2,1,0:T(8,128)S(1)}, u32[]{:S(2)}, u32[]{:S(2)}) async-start(f32[8,32,128]{2,1,0:T(8,128)} %backward_0.1), calls=%async_computation | async-start | bytes 262144 | tf_op jit(solution)/shard_map/collect/all_to_all | solution.py:405
  105.8 94.8 %collective-permute-start.43 = (f32[2,64,128]{2,1,0:T(8,128)S(1)}, f32[2,64,128]{2,1,0:T(8,128)S(1)}, u32[]{:S(2)}, u32[]{:S(2)}) collective-permute-start(f32[2,64,128]{2,1,0:T(8,128)S(1)} %get-tuple-element.85), channel_id=1, source_target_pairs={{0,24},{1,25},{2,26},{3,27},{4,28},{5,29},{6,30},{7,31},{8,16},{9,... | collective-permute-start | bytes 196616 | tf_op jit(solution)/shard_map/collect/ppermute | solution.py:367
  (13 other events, 9.1 us)

commit v6 on v5

--- a/solution.py
+++ b/solution.py
@@ -24,7 +24,7 @@
 GROUPS = (
     ((0, 0), (0, 1), (-1, 0), (1, 0), (-1, 1), (1, 1)),
     ((-2, 0), (2, 0), (-2, 1), (2, 1)),
-    ((-3, 0), (3, 0), (-3, 1), (3, 1), (-4, 0), (4, 1)),
+    ((-3, 0), (3, 0), (-3, 1), (3, 1), (4, 0), (-4, 1)),
 )
 HIGHEST = lax.Precision.HIGHEST
 CONTRACT_LAST = (((1,), (1,)), ((), ()))
@@ -378,7 +378,7 @@
         for _ in range(2):
             left_a, right_a, left_b, right_b = ring(left_a, 1), ring(right_a, -1), ring(left_b, 1), ring(right_b, -1)
             pieces.append([left_a, right_a, left_b, right_b])
-        pieces[2] += [ring(left_a, 1), ring(right_b, -1)]
+        pieces[2] += [ring(right_a, -1), ring(left_b, 1)]
         weights = [part for group in pieces for part in split_weights(group)]
         pieces = [piece for group in pieces for piece in group]
         residue, table = receive(pieces)

time: 202 us -> 204 us (level)
    all_to_all x1, starting transfers between devices: 4.5 us -> 8.57 us  [body(): lax.all_to_all(both, 'z', 0, 0)]
    ppermute x16, starting transfers between devices: 40.6 us -> 37.1 us  [ring(): return lax.ppermute(value, AXES, pairs)]
where the time goes in v6:
time: 204 us; the launch traced here: 203 us
  waiting for transfers between devices  116 us (57%)
  starting transfers between devices  64.4 us (32%)
  Pallas kernels  20.4 us (10%)
    ppermute x16, waiting for transfers between devices, ring(): return lax.ppermute(value, AXES, pairs)  107 us
    ppermute x16, starting transfers between devices, ring(): return lax.ppermute(value, AXES, pairs)  37.1 us
    ppermute x28, starting transfers between devices, hop(): return lax.ppermute(value, AXES, pairs)  18.8 us
    all_to_all x1, waiting for transfers between devices, body(): lax.all_to_all(both, 'z', 0, 0)  9.08 us
    all_to_all x1, starting transfers between devices, body(): lax.all_to_all(both, 'z', 0, 0)  8.57 us
    pallas_call x8, Pallas kernels, forward_step(): pl.pallas_call(functools.partial(forward_kernel, step, len(arrived)), in_...  6.16 us
    pallas_call x6, Pallas kernels, backward_step(): pl.pallas_call(functools.partial(backward_kernel, level), in_specs=[SMEM]...  4.41 us
  transfers between devices with their start and end apart: 45, of which 4 were waited for; matrix products, arithmetic and copies ran while one was open for 0% of the time, Pallas kernels for 2%

profile of v6, /device:TPU:24, one launch (start us, length us, event | category | flops | bytes accessed | tf_op | source)
XLA Modules:
  0.0 202.5 jit_solution(14005140054887277746)
XLA Ops:
  0.6 2.4 %prepare.1.refs_0_ = f32[136,1152]{1,0:T(8,128)S(1)} custom-call(s32[1,8]{1,0:T(1,128)} %bitcast.26, f32[64,128]{1,0:T(8,128)} %bitcast.25, f32[128,128]{1,0:T(8,128)} %bitcast.24, f32[8,128,128]{2,1,0:T(8,128)} %bitcast.23), custom_call_target="tpu_custom_call" | custom-call | tf_op jit(solution)/shard_map/prepare/pallas_call | solution.py:88
  3.0 3.5 %collective-permute-start.3 = (f32[136,1152]{1,0:T(8,128)S(1)}, f32[136,1152]{1,0:T(8,128)S(1)}, u32[]{:S(2)}, u32[]{:S(2)}) collective-permute-start(f32[136,1152]{1,0:T(8,128)S(1)} %prepare.1.refs_0_), channel_id=1, source_target_pairs={{24,1},{25,2},{26,3},{27,4},{28,5},{29,6},{30,7},{31,0},{16,9},{17... | collective-permute-start | bytes 1880072 | tf_op jit(solution)/shard_map/gather/ppermute | solution.py:367
  6.6 0.7 collective-permute-start.2
  7.3 7.4 %collective-permute-start.4 = (f32[136,1152]{1,0:T(8,128)S(1)}, f32[136,1152]{1,0:T(8,128)S(1)}, u32[]{:S(2)}, u32[]{:S(2)}) collective-permute-start(f32[136,1152]{1,0:T(8,128)S(1)} %prepare.1.refs_0_), channel_id=1, source_target_pairs={{24,7},{25,0},{26,1},{27,2},{28,3},{29,4},{30,5},{31,6},{16,15},{1... | collective-permute-start | bytes 1880072 | tf_op jit(solution)/shard_map/gather/ppermute | solution.py:367
  14.7 0.7 collective-permute-start.1
  15.4 0.7 collective-permute-start.7
  16.2 0.7 collective-permute-start.6
  16.9 8.6 %collective-permute-done.4.refs_5_ = f32[136,1152]{1,0:T(8,128)S(1)} collective-permute-done((f32[136,1152]{1,0:T(8,128)S(1)}, f32[136,1152]{1,0:T(8,128)S(1)}, u32[]{:S(2)}, u32[]{:S(2)}) %collective-permute-start.4) | collective-permute-done | bytes 626720 | tf_op jit(solution)/shard_map/gather/ppermute | solution.py:367
  26.2 0.7 collective-permute-start.5
  26.9 0.7 collective-permute-start.11
  27.6 0.7 collective-permute-start.10
  28.3 16.4 %collective-permute-start = (f32[136,1152]{1,0:T(8,128)S(1)}, f32[136,1152]{1,0:T(8,128)S(1)}, u32[]{:S(2)}, u32[]{:S(2)}) collective-permute-start(f32[136,1152]{1,0:T(8,128)S(1)} %prepare.1.refs_0_), channel_id=1, source_target_pairs={{24,0},{25,1},{26,2},{27,3},{28,4},{29,5},{30,6},{31,7},{16,8},{17... | collective-permute-start | bytes 1880072 | tf_op jit(solution)/shard_map/gather/ppermute | solution.py:367
  44.8 0.7 collective-permute-start.12
  45.5 0.7 collective-permute-start.9
  46.2 0.7 collective-permute-start.14
  46.9 0.7 collective-permute-start.13
  47.6 4.9 %collective-permute-done.refs_1_ = f32[136,1152]{1,0:T(8,128)S(1)} collective-permute-done((f32[136,1152]{1,0:T(8,128)S(1)}, f32[136,1152]{1,0:T(8,128)S(1)}, u32[]{:S(2)}, u32[]{:S(2)}) %collective-permute-start) | collective-permute-done | bytes 626720 | tf_op jit(solution)/shard_map/gather/ppermute | solution.py:367
  65.9 0.8 collective-permute-start.26
  68.8 1.3 forward_7.1
  71.5 2.2 %turn.1 = (bf16[6,1024,128]{2,1,0:T(8,128)(2,1)S(1)}, bf16[6,1024,128]{2,1,0:T(8,128)(2,1)S(1)}, bf16[4,1024,128]{2,1,0:T(8,128)(2,1)S(1)}, bf16[4,1024,128]{2,1...) custom-call(bf16[6,128,1024]{2,1,0:T(8,128)(2,1)S(1)} %get-tuple-element.47.refs_0_.refs_2_, ...), custom_call_target="tpu_custom_call" | custom-call | tf_op jit(solution)/shard_map/turn/pallas_call | solution.py:216
  73.7 1.6 diagonal.1
  75.4 0.7 backward_6.1.before
  77.4 0.7 backward_5.1.before
  79.5 0.7 backward_4.1.before
  81.6 0.7 backward_3.1.before
  83.6 0.7 backward_2.1.before
  85.7 0.9 backward_1.1.before
  88.0 1.4 backward_0.1
  89.4 8.6 %all-to-all-start = ((f32[8,32,128]{2,1,0:T(8,128)}), f32[8,32,128]{2,1,0:T(8,128)S(1)}, u32[]{:S(2)}, u32[]{:S(2)}) async-start(f32[8,32,128]{2,1,0:T(8,128)} %backward_0.1), calls=%async_computation | async-start | bytes 262144 | tf_op jit(solution)/shard_map/collect/all_to_all | solution.py:405
  97.9 9.1 %all-to-all-done.home = f32[8,32,128]{2,1,0:T(8,128)S(1)} async-done(((f32[8,32,128]{2,1,0:T(8,128)}), f32[8,32,128]{2,1,0:T(8,128)S(1)}, u32[]{:S(2)}, u32[]{:S(2)}) %all-to-all-start) | async-done | bytes 131104 | tf_op jit(solution)/shard_map/collect/all_to_all | solution.py:405
  107.0 1.3 collective-permute-start.43
  108.3 93.5 %collective-permute-done.43.moved = f32[2,64,128]{2,1,0:T(8,128)S(1)} collective-permute-done((f32[2,64,128]{2,1,0:T(8,128)S(1)}, f32[2,64,128]{2,1,0:T(8,128)S(1)}, u32[]{:S(2)}, u32[]{:S(2)}) %collective-permute-start.43) | collective-permute-done | bytes 65568 | tf_op jit(solution)/shard_map/collect/ppermute | solution.py:367
  (83 shorter events, 25.8 us)
Async XLA Ops:
  3.0 12.4 %collective-permute-start.3 = (f32[136,1152]{1,0:T(8,128)S(1)}, f32[136,1152]{1,0:T(8,128)S(1)}, u32[]{:S(2)}, u32[]{:S(2)}) collective-permute-start(f32[136,1152]{1,0:T(8,128)S(1)} %prepare.1.refs_0_), channel_id=1, source_target_pairs={{24,1},{25,2},{26,3},{27,4},{28,5},{29,6},{30,7},{31,0},{16,9},{17... | collective-permute-start | bytes 1880072 | tf_op jit(solution)/shard_map/gather/ppermute | solution.py:367
  6.6 9.6 %collective-permute-start.2 = (f32[136,1152]{1,0:T(8,128)S(1)}, f32[136,1152]{1,0:T(8,128)S(1)}, u32[]{:S(2)}, u32[]{:S(2)}) collective-permute-start(f32[136,1152]{1,0:T(8,128)S(1)} %prepare.1.refs_0_), channel_id=1, source_target_pairs={{0,7},{1,0},{2,1},{3,2},{4,3},{5,4},{6,5},{7,6},{8,15},{9,8},{10,9... | collective-permute-start | bytes 1880072 | tf_op jit(solution)/shard_map/gather/ppermute | solution.py:367
  7.3 18.2 %collective-permute-start.4 = (f32[136,1152]{1,0:T(8,128)S(1)}, f32[136,1152]{1,0:T(8,128)S(1)}, u32[]{:S(2)}, u32[]{:S(2)}) collective-permute-start(f32[136,1152]{1,0:T(8,128)S(1)} %prepare.1.refs_0_), channel_id=1, source_target_pairs={{24,7},{25,0},{26,1},{27,2},{28,3},{29,4},{30,5},{31,6},{16,15},{1... | collective-permute-start | bytes 1880072 | tf_op jit(solution)/shard_map/gather/ppermute | solution.py:367
  14.7 11.4 %collective-permute-start.1 = (f32[136,1152]{1,0:T(8,128)S(1)}, f32[136,1152]{1,0:T(8,128)S(1)}, u32[]{:S(2)}, u32[]{:S(2)}) collective-permute-start(f32[136,1152]{1,0:T(8,128)S(1)} %prepare.1.refs_0_), channel_id=1, source_target_pairs={{0,1},{1,2},{2,3},{3,4},{4,5},{5,6},{6,7},{7,0},{8,9},{9,10},{10,1... | collective-permute-start | bytes 1880072 | tf_op jit(solution)/shard_map/gather/ppermute | solution.py:367
  15.4 11.4 %collective-permute-start.7 = (f32[136,1152]{1,0:T(8,128)S(1)}, f32[136,1152]{1,0:T(8,128)S(1)}, u32[]{:S(2)}, u32[]{:S(2)}) collective-permute-start(f32[136,1152]{1,0:T(8,128)S(1)} %collective-permute-done.3.refs_4_), channel_id=1, source_target_pairs={{0,1},{1,2},{2,3},{3,4},{4,5},{5,6},{6,7},{7,0},{8,9},{9,10},{10,1... | collective-permute-start | bytes 1880072 | tf_op jit(solution)/shard_map/gather/ppermute | solution.py:367
  16.2 11.4 %collective-permute-start.6 = (f32[136,1152]{1,0:T(8,128)S(1)}, f32[136,1152]{1,0:T(8,128)S(1)}, u32[]{:S(2)}, u32[]{:S(2)}) collective-permute-start(f32[136,1152]{1,0:T(8,128)S(1)} %collective-permute-done.2.refs_3_), channel_id=1, source_target_pairs={{0,7},{1,0},{2,1},{3,2},{4,3},{5,4},{6,5},{7,6},{8,15},{9,8},{10,9... | collective-permute-start | bytes 1880072 | tf_op jit(solution)/shard_map/gather/ppermute | solution.py:367
  25.5 19.3 %collective-permute-start.8 = (f32[136,1152]{1,0:T(8,128)S(1)}, f32[136,1152]{1,0:T(8,128)S(1)}, u32[]{:S(2)}, u32[]{:S(2)}) collective-permute-start(f32[136,1152]{1,0:T(8,128)S(1)} %collective-permute-done.4.refs_5_), channel_id=1, source_target_pairs={{0,7},{1,0},{2,1},{3,2},{4,3},{5,4},{6,5},{7,6},{8,15},{9,8},{10,9... | collective-permute-start | bytes 1880072 | tf_op jit(solution)/shard_map/gather/ppermute | solution.py:367
  26.2 19.3 %collective-permute-start.5 = (f32[136,1152]{1,0:T(8,128)S(1)}, f32[136,1152]{1,0:T(8,128)S(1)}, u32[]{:S(2)}, u32[]{:S(2)}) collective-permute-start(f32[136,1152]{1,0:T(8,128)S(1)} %collective-permute-done.1.refs_2_), channel_id=1, source_target_pairs={{0,1},{1,2},{2,3},{3,4},{4,5},{5,6},{6,7},{7,0},{8,9},{9,10},{10,1... | collective-permute-start | bytes 1880072 | tf_op jit(solution)/shard_map/gather/ppermute | solution.py:367
  26.9 19.3 %collective-permute-start.11 = (f32[136,1152]{1,0:T(8,128)S(1)}, f32[136,1152]{1,0:T(8,128)S(1)}, u32[]{:S(2)}, u32[]{:S(2)}) collective-permute-start(f32[136,1152]{1,0:T(8,128)S(1)} %collective-permute-done.7.refs_8_.refs_2_), channel_id=1, source_target_pairs={{0,1},{1,2},{2,3},{3,4},{4,5},{5,6},{6,7},{7,0},{8,9},{9,10},{10,1... | collective-permute-start | bytes 1880072 | tf_op jit(solution)/shard_map/gather/ppermute | solution.py:367
  27.6 19.3 %collective-permute-start.10 = (f32[136,1152]{1,0:T(8,128)S(1)}, f32[136,1152]{1,0:T(8,128)S(1)}, u32[]{:S(2)}, u32[]{:S(2)}) collective-permute-start(f32[136,1152]{1,0:T(8,128)S(1)} %collective-permute-done.6.refs_7_.refs_1_), channel_id=1, source_target_pairs={{0,7},{1,0},{2,1},{3,2},{4,3},{5,4},{6,5},{7,6},{8,15},{9,8},{10,9... | collective-permute-start | bytes 1880072 | tf_op jit(solution)/shard_map/gather/ppermute | solution.py:367
  28.3 24.2 %collective-permute-start = (f32[136,1152]{1,0:T(8,128)S(1)}, f32[136,1152]{1,0:T(8,128)S(1)}, u32[]{:S(2)}, u32[]{:S(2)}) collective-permute-start(f32[136,1152]{1,0:T(8,128)S(1)} %prepare.1.refs_0_), channel_id=1, source_target_pairs={{24,0},{25,1},{26,2},{27,3},{28,4},{29,5},{30,6},{31,7},{16,8},{17... | collective-permute-start | bytes 1880072 | tf_op jit(solution)/shard_map/gather/ppermute | solution.py:367
  44.8 8.7 %collective-permute-start.12 = (f32[136,1152]{1,0:T(8,128)S(1)}, f32[136,1152]{1,0:T(8,128)S(1)}, u32[]{:S(2)}, u32[]{:S(2)}) collective-permute-start(f32[136,1152]{1,0:T(8,128)S(1)} %collective-permute-done.8.refs_9_.refs_3_), channel_id=1, source_target_pairs={{0,7},{1,0},{2,1},{3,2},{4,3},{5,4},{6,5},{7,6},{8,15},{9,8},{10,9... | collective-permute-start | bytes 1880072 | tf_op jit(solution)/shard_map/gather/ppermute | solution.py:367
  45.5 8.0 %collective-permute-start.9 = (f32[136,1152]{1,0:T(8,128)S(1)}, f32[136,1152]{1,0:T(8,128)S(1)}, u32[]{:S(2)}, u32[]{:S(2)}) collective-permute-start(f32[136,1152]{1,0:T(8,128)S(1)} %collective-permute-done.5.refs_6_.refs_0_), channel_id=1, source_target_pairs={{0,1},{1,2},{2,3},{3,4},{4,5},{5,6},{6,7},{7,0},{8,9},{9,10},{10,1... | collective-permute-start | bytes 1880072 | tf_op jit(solution)/shard_map/gather/ppermute | solution.py:367
  46.2 7.3 %collective-permute-start.14 = (f32[136,1152]{1,0:T(8,128)S(1)}, f32[136,1152]{1,0:T(8,128)S(1)}, u32[]{:S(2)}, u32[]{:S(2)}) collective-permute-start(f32[136,1152]{1,0:T(8,128)S(1)} %collective-permute-done.11.refs_12_.refs_2_), channel_id=1, source_target_pairs={{0,1},{1,2},{2,3},{3,4},{4,5},{5,6},{6,7},{7,0},{8,9},{9,10},{10,1... | collective-permute-start | bytes 1880072 | tf_op jit(solution)/shard_map/gather/ppermute | solution.py:367
  46.9 6.6 %collective-permute-start.13 = (f32[136,1152]{1,0:T(8,128)S(1)}, f32[136,1152]{1,0:T(8,128)S(1)}, u32[]{:S(2)}, u32[]{:S(2)}) collective-permute-start(f32[136,1152]{1,0:T(8,128)S(1)} %collective-permute-done.10.refs_11_.refs_1_), channel_id=1, source_target_pairs={{0,7},{1,0},{2,1},{3,2},{4,3},{5,4},{6,5},{7,6},{8,15},{9,8},{10,9... | collective-permute-start | bytes 1880072 | tf_op jit(solution)/shard_map/gather/ppermute | solution.py:367
  54.9 1.3 collective-permute-start.15
  56.9 1.3 collective-permute-start.17
  59.0 1.3 collective-permute-start.19
  61.1 1.3 collective-permute-start.21
  63.1 1.3 collective-permute-start.23
  65.2 1.5 collective-permute-start.25
  67.4 1.3 collective-permute-start.27
  70.1 5.2 %collective-permute-start.30 = (f32[16,8,128]{2,1,0:T(8,128)S(1)}, f32[16,8,128]{2,1,0:T(8,128)S(1)}, u32[]{:S(2)}, u32[]{:S(2)}) collective-permute-start(f32[16,8,128]{2,1,0:T(8,128)S(1)} %get-tuple-element.74.before), channel_id=1, source_target_pairs={{96,80},{97,81},{98,82},{99,83},{100,84},{101,85},{102,86},{103,87... | collective-permute-start | bytes 196616 | tf_op jit(solution)/shard_map/ppermute | solution.py:357
  70.8 4.5 %collective-permute-start.29 = (f32[16,8,128]{2,1,0:T(8,128)S(1)}, f32[16,8,128]{2,1,0:T(8,128)S(1)}, u32[]{:S(2)}, u32[]{:S(2)}) collective-permute-start(f32[16,8,128]{2,1,0:T(8,128)S(1)} %get-tuple-element.74.before), channel_id=1, source_target_pairs={{96,88},{97,89},{98,90},{99,91},{100,92},{101,93},{102,94},{103,95... | collective-permute-start | bytes 196616 | tf_op jit(solution)/shard_map/ppermute | solution.py:357
  76.1 1.3 collective-permute-start.32
  78.1 1.3 collective-permute-start.34
  80.2 1.3 collective-permute-start.36
  82.3 1.3 collective-permute-start.38
  84.4 1.3 collective-permute-start.40
  86.6 1.3 collective-permute-start.42
  89.4 17.6 %all-to-all-start = ((f32[8,32,128]{2,1,0:T(8,128)}), f32[8,32,128]{2,1,0:T(8,128)S(1)}, u32[]{:S(2)}, u32[]{:S(2)}) async-start(f32[8,32,128]{2,1,0:T(8,128)} %backward_0.1), calls=%async_computation | async-start | bytes 262144 | tf_op jit(solution)/shard_map/collect/all_to_all | solution.py:405
  107.0 94.8 %collective-permute-start.43 = (f32[2,64,128]{2,1,0:T(8,128)S(1)}, f32[2,64,128]{2,1,0:T(8,128)S(1)}, u32[]{:S(2)}, u32[]{:S(2)}) collective-permute-start(f32[2,64,128]{2,1,0:T(8,128)S(1)} %get-tuple-element.85), channel_id=1, source_target_pairs={{0,24},{1,25},{2,26},{3,27},{4,28},{5,29},{6,30},{7,31},{8,16},{9,... | collective-permute-start | bytes 196616 | tf_op jit(solution)/shard_map/collect/ppermute | solution.py:367
  (13 other events, 9.1 us)

commit v7 on v5

--- a/solution.py
+++ b/solution.py
@@ -107,19 +107,18 @@
     return high, (value - high.astype(F32)).astype(BF16)
 
 
-def split_kernel(count, *refs):
-    high, low = refs[count:]
-    for i, source in enumerate(refs[:count]):
-        high[i], low[i] = split(source[:BLOCK, :WIDE])
+def split_kernel(*refs):
+    for i, source in enumerate(refs[:-1]):
+        refs[-1][i, :BLOCK], refs[-1][i, BLOCK:] = split(source[:BLOCK, :WIDE])
 
 
 def split_weights(pieces):
-    shape = jax.ShapeDtypeStruct((len(pieces), BLOCK, WIDE), BF16)
-    return pl.pallas_call(
-        functools.partial(split_kernel, len(pieces)),
+    shape = jax.ShapeDtypeStruct((len(pieces), 2 * BLOCK, WIDE), BF16)
+    return pl.pallas_call(
+        split_kernel,
         in_specs=[VMEM] * len(pieces),
-        out_specs=[VMEM] * 2,
-        out_shape=[shape] * 2,
+        out_specs=VMEM,
+        out_shape=shape,
         compiler_params=PARAMS,
         cost_estimate=pl.CostEstimate(flops=0, transcendentals=0, bytes_accessed=8 * len(pieces) * BLOCK * WIDE),
         name="split_weights",
@@ -154,9 +153,9 @@
 
 
 def supernodes(weights):
-    for group, (high, low) in zip(GROUPS, zip(weights[::2], weights[1::2])):
+    for group, blocks in zip(GROUPS, weights):
         for i, (away, other) in enumerate(group):
-            yield number(away, other), high.at[i], low.at[i]
+            yield number(away, other), blocks.at[i]
 
 
 def active(level):
@@ -164,7 +163,7 @@
 
 
 def forward_kernel(step, arrivals, table, residue, *refs):
-    arrived, weights, (residue_out, own, other, total) = refs[:arrivals], refs[arrivals:-4], refs[-4:]
+    arrived, weights, (residue_out, own, other, *totals) = refs[:arrivals], refs[arrivals:-5], refs[-5:]
 
     @pl.when(jnp.logical_not(active(step)))
     def _():
@@ -177,20 +176,25 @@
             current = current - piece[...]
         residue_out[...] = current
         if step < LEVELS - 1:
-            total[...] = jnp.zeros_like(total)
-        for sup, high, low in supernodes(weights):
+            for total in totals:
+                total[...] = jnp.zeros_like(total)
+        for count, (sup, blocks) in enumerate(supernodes(weights)):
             left = jnp.concatenate(split(residue_out[sup]), axis=0)
+            left = jnp.concatenate([left, left], axis=1)
             if step == LEVELS - 1:
-                terms = jnp.dot(left, high[:, :BLOCK], preferred_element_type=F32) + jnp.dot(left, low[:, :BLOCK], preferred_element_type=F32)
+                terms = jnp.dot(left, blocks[:, :BLOCK], preferred_element_type=F32)
                 own[sup] = terms[:ROWS] + terms[ROWS:]
                 continue
-            terms = jnp.dot(left, high[...], preferred_element_type=F32) + jnp.dot(left, low[...], preferred_element_type=F32)
+            terms = jnp.dot(left, blocks[...], preferred_element_type=F32)
             summed = terms[:ROWS] + terms[ROWS:]
-            for k in range(NB):
-                total[table[sup, k]] += summed[:, k * BLOCK : (k + 1) * BLOCK]
+            targets = [table[sup, k] for k in range(NB)]
+            total = totals[count % len(totals)]
+            sums = [total[targets[k]] + summed[:, k * BLOCK : (k + 1) * BLOCK] for k in range(NB)]
+            for target, value in zip(targets, sums):
+                total[target] = value
         if step < LEVELS - 1:
-            own[...] = total[:CLASS]
-            other[...] = total[CLASS:]
+            own[...] = totals[0][:CLASS] + totals[1][:CLASS]
+            other[...] = totals[0][CLASS:] + totals[1][CLASS:]
 
 
 def forward_step(step, table, residue, arrived, weights):
@@ -199,17 +203,18 @@
         in_specs=[SMEM] + [VMEM] * (1 + len(arrived) + len(weights)),
         out_specs=[VMEM] * 3,
         out_shape=[PIECE] * 3,
-        scratch_shapes=[pltpu.VMEM((2 * CLASS, ROWS, BLOCK), F32)],
+        scratch_shapes=[pltpu.VMEM((2 * CLASS, ROWS, BLOCK), F32)] * 2,
         compiler_params=PARAMS,
         name=f"forward_{step}",
     )(table, residue, *arrived, *weights)
 
 
 def turn_kernel(*refs):
-    for source, target in zip(refs[:6], refs[6:]):
+    for source, target in zip(refs[:3], refs[3:]):
         for i in range(source.shape[0]):
             for k in range(NB):
-                target[i, k * BLOCK : (k + 1) * BLOCK] = source[i, :, k * BLOCK : (k + 1) * BLOCK].T
+                for part in (slice(BLOCK), slice(BLOCK, 2 * BLOCK)):
+                    target[i, k * BLOCK : (k + 1) * BLOCK, part] = source[i, part, k * BLOCK : (k + 1) * BLOCK].T
 
 
 def turn(weights):
@@ -217,14 +222,14 @@
         turn_kernel,
         in_specs=[VMEM] * len(weights),
         out_specs=[VMEM] * len(weights),
-        out_shape=[jax.ShapeDtypeStruct((part.shape[0], WIDE, BLOCK), BF16) for part in weights],
+        out_shape=[jax.ShapeDtypeStruct((part.shape[0], WIDE, 2 * BLOCK), BF16) for part in weights],
         compiler_params=PARAMS,
         name="turn",
     )(*weights)
 
 
 def backward_kernel(level, table, before, base, own, other, *refs):
-    weights, (answer, picked) = refs[:6], refs[-2:]
+    weights, (answer, picked) = refs[:3], refs[-2:]
 
     @pl.when(jnp.logical_not(active(level)))
     def _():
@@ -234,15 +239,16 @@
     def _():
         for half, source in enumerate((own, other)):
             picked[half * CLASS : (half + 1) * CLASS] = jnp.concatenate(split(source[...]), axis=1)
-        for sup, high, low in supernodes(weights):
+        for sup, blocks in supernodes(weights):
             left = jnp.concatenate([picked[table[sup, k]] for k in range(NB)], axis=1)
-            terms = jnp.dot(left, high[...], preferred_element_type=F32) + jnp.dot(left, low[...], preferred_element_type=F32)
+            terms = jnp.dot(left, blocks[...], preferred_element_type=F32)
+            terms = terms[:, :BLOCK] + terms[:, BLOCK:]
             answer[sup] = base[sup] - (terms[:ROWS] + terms[ROWS:])
 
 
 def last_backward_kernel(table, before, base, own, other, *refs):
-    solved, both, answer, picked = refs[6:]
-    backward_kernel(0, table, before, base, own, other, *refs[:6], answer, picked)
+    solved, both, answer, picked = refs[3:]
+    backward_kernel(0, table, before, base, own, other, *refs[:3], answer, picked)
     for i in range(CLASS):
         start = i // Z * 2 * ROWS
         both[i % Z, start : start + ROWS] = solved[i]
@@ -379,7 +385,7 @@
             left_a, right_a, left_b, right_b = ring(left_a, 1), ring(right_a, -1), ring(left_b, 1), ring(right_b, -1)
             pieces.append([left_a, right_a, left_b, right_b])
         pieces[2] += [ring(left_a, 1), ring(right_b, -1)]
-        weights = [part for group in pieces for part in split_weights(group)]
+        weights = [split_weights(group) for group in pieces]
         pieces = [piece for group in pieces for piece in group]
         residue, table = receive(pieces)
         table = table[:, 0, :NB]

time: 202 us -> 202 us (level)
  no operation moved by 1% of the time
where the time goes in v7:
time: 202 us; the launch traced here: 201 us
  waiting for transfers between devices  115 us (57%)
  starting transfers between devices  63.8 us (32%)
  Pallas kernels  20.2 us (10%)
    ppermute x16, waiting for transfers between devices, ring(): return lax.ppermute(value, AXES, pairs)  106 us
    ppermute x16, starting transfers between devices, ring(): return lax.ppermute(value, AXES, pairs)  40.6 us
    ppermute x28, starting transfers between devices, hop(): return lax.ppermute(value, AXES, pairs)  18.8 us
    all_to_all x1, waiting for transfers between devices, body(): lax.all_to_all(both, 'z', 0, 0)  9.08 us
    pallas_call x8, Pallas kernels, forward_step(): pl.pallas_call(functools.partial(forward_kernel, step, len(arrived)), in_...  6.21 us
    all_to_all x1, starting transfers between devices, body(): lax.all_to_all(both, 'z', 0, 0)  4.5 us
    pallas_call x6, Pallas kernels, backward_step(): pl.pallas_call(functools.partial(backward_kernel, level), in_specs=[SMEM]...  4.18 us
  transfers between devices with their start and end apart: 45, of which 4 were waited for; matrix products, arithmetic and copies ran while one was open for 0% of the time, Pallas kernels for 2%

profile of v7, /device:TPU:24, one launch (start us, length us, event | category | flops | bytes accessed | tf_op | source)
XLA Modules:
  0.0 201.0 jit_solution(9072651216042730109)
XLA Ops:
  0.6 2.4 %prepare.1.refs_0_ = f32[136,1152]{1,0:T(8,128)S(1)} custom-call(s32[1,8]{1,0:T(1,128)} %bitcast.26, f32[64,128]{1,0:T(8,128)} %bitcast.25, f32[128,128]{1,0:T(8,128)} %bitcast.24, f32[8,128,128]{2,1,0:T(8,128)} %bitcast.23), custom_call_target="tpu_custom_call" | custom-call | tf_op jit(solution)/shard_map/prepare/pallas_call | solution.py:88
  3.0 7.5 %collective-permute-start.4 = (f32[136,1152]{1,0:T(8,128)S(1)}, f32[136,1152]{1,0:T(8,128)S(1)}, u32[]{:S(2)}, u32[]{:S(2)}) collective-permute-start(f32[136,1152]{1,0:T(8,128)S(1)} %prepare.1.refs_0_), channel_id=1, source_target_pairs={{24,7},{25,0},{26,1},{27,2},{28,3},{29,4},{30,5},{31,6},{16,15},{1... | collective-permute-start | bytes 1880072 | tf_op jit(solution)/shard_map/gather/ppermute | solution.py:373
  10.5 0.7 collective-permute-start.1
  11.2 1.3 collective-permute-start.3
  12.5 0.7 collective-permute-start.2
  13.3 7.9 %collective-permute-done.4.refs_5_ = f32[136,1152]{1,0:T(8,128)S(1)} collective-permute-done((f32[136,1152]{1,0:T(8,128)S(1)}, f32[136,1152]{1,0:T(8,128)S(1)}, u32[]{:S(2)}, u32[]{:S(2)}) %collective-permute-start.4) | collective-permute-done | bytes 626720 | tf_op jit(solution)/shard_map/gather/ppermute | solution.py:373
  21.9 0.7 collective-permute-start.5
  22.6 0.7 collective-permute-start.7
  23.3 0.7 collective-permute-start.6
  24.0 0.7 collective-permute-start.12
  24.7 0.7 collective-permute-start.9
  25.4 22.1 %collective-permute-start = (f32[136,1152]{1,0:T(8,128)S(1)}, f32[136,1152]{1,0:T(8,128)S(1)}, u32[]{:S(2)}, u32[]{:S(2)}) collective-permute-start(f32[136,1152]{1,0:T(8,128)S(1)} %prepare.1.refs_0_), channel_id=1, source_target_pairs={{24,0},{25,1},{26,2},{27,3},{28,4},{29,5},{30,6},{31,7},{16,8},{17... | collective-permute-start | bytes 1880072 | tf_op jit(solution)/shard_map/gather/ppermute | solution.py:373
  47.5 0.7 collective-permute-start.11
  48.3 0.7 collective-permute-start.10
  49.0 0.7 collective-permute-start.14
  49.7 0.7 collective-permute-start.13
  50.4 4.9 %collective-permute-done.refs_1_ = f32[136,1152]{1,0:T(8,128)S(1)} collective-permute-done((f32[136,1152]{1,0:T(8,128)S(1)}, f32[136,1152]{1,0:T(8,128)S(1)}, u32[]{:S(2)}, u32[]{:S(2)}) %collective-permute-start) | collective-permute-done | bytes 626720 | tf_op jit(solution)/shard_map/gather/ppermute | solution.py:373
  57.0 0.7 forward_0.1
  63.2 0.7 forward_3.1
  65.2 0.7 forward_4.1
  68.7 0.8 collective-permute-start.26
  71.6 1.3 forward_7.1
  74.3 2.2 %turn.1 = (bf16[6,1024,256]{2,1,0:T(8,128)(2,1)S(1)}, bf16[4,1024,256]{2,1,0:T(8,128)(2,1)S(1)}, bf16[6,1024,256]{2,1,0:T(8,128)(2,1)S(1)}) custom-call(bf16[6,256,1024]{2,1,0:T(8,128)(2,1)S(1)} %split_weights.3.refs_0_.refs_2_, bf16[4,256,1024]{2,1,0:T(8,128)(2,1)S(1)} %split_weights.4.refs_1_.refs_3_, bf16[6,256,1024]{2,1,0:T(8,128)(2,1)S(1)} %split_weights.5.refs_2_.refs_4_), custom_call_target="tpu_custom_call" | custom-call | tf_op jit(solution)/shard_map/turn/pallas_call | solution.py:221
  76.5 1.6 diagonal.1
  78.2 0.7 backward_6.1.before
  82.3 0.7 backward_4.1.before
  84.4 0.7 backward_3.1.before
  90.6 1.4 backward_0.1
  92.0 4.5 %all-to-all-start = ((f32[8,32,128]{2,1,0:T(8,128)}), f32[8,32,128]{2,1,0:T(8,128)S(1)}, u32[]{:S(2)}, u32[]{:S(2)}) async-start(f32[8,32,128]{2,1,0:T(8,128)} %backward_0.1), calls=%async_computation | async-start | bytes 262144 | tf_op jit(solution)/shard_map/collect/all_to_all | solution.py:411
  96.5 9.1 %all-to-all-done.home = f32[8,32,128]{2,1,0:T(8,128)S(1)} async-done(((f32[8,32,128]{2,1,0:T(8,128)}), f32[8,32,128]{2,1,0:T(8,128)S(1)}, u32[]{:S(2)}, u32[]{:S(2)}) %all-to-all-start) | async-done | bytes 131104 | tf_op jit(solution)/shard_map/collect/all_to_all | solution.py:411
  105.6 1.3 collective-permute-start.43
  106.9 93.5 %collective-permute-done.43.moved = f32[2,64,128]{2,1,0:T(8,128)S(1)} collective-permute-done((f32[2,64,128]{2,1,0:T(8,128)S(1)}, f32[2,64,128]{2,1,0:T(8,128)S(1)}, u32[]{:S(2)}, u32[]{:S(2)}) %collective-permute-start.43) | collective-permute-done | bytes 65568 | tf_op jit(solution)/shard_map/collect/ppermute | solution.py:373
  (83 shorter events, 25.8 us)
Async XLA Ops:
  3.0 18.1 %collective-permute-start.4 = (f32[136,1152]{1,0:T(8,128)S(1)}, f32[136,1152]{1,0:T(8,128)S(1)}, u32[]{:S(2)}, u32[]{:S(2)}) collective-permute-start(f32[136,1152]{1,0:T(8,128)S(1)} %prepare.1.refs_0_), channel_id=1, source_target_pairs={{24,7},{25,0},{26,1},{27,2},{28,3},{29,4},{30,5},{31,6},{16,15},{1... | collective-permute-start | bytes 1880072 | tf_op jit(solution)/shard_map/gather/ppermute | solution.py:373
  10.5 11.4 %collective-permute-start.1 = (f32[136,1152]{1,0:T(8,128)S(1)}, f32[136,1152]{1,0:T(8,128)S(1)}, u32[]{:S(2)}, u32[]{:S(2)}) collective-permute-start(f32[136,1152]{1,0:T(8,128)S(1)} %prepare.1.refs_0_), channel_id=1, source_target_pairs={{0,1},{1,2},{2,3},{3,4},{4,5},{5,6},{6,7},{7,0},{8,9},{9,10},{10,1... | collective-permute-start | bytes 1880072 | tf_op jit(solution)/shard_map/gather/ppermute | solution.py:373
  11.2 11.4 %collective-permute-start.3 = (f32[136,1152]{1,0:T(8,128)S(1)}, f32[136,1152]{1,0:T(8,128)S(1)}, u32[]{:S(2)}, u32[]{:S(2)}) collective-permute-start(f32[136,1152]{1,0:T(8,128)S(1)} %prepare.1.refs_0_), channel_id=1, source_target_pairs={{24,1},{25,2},{26,3},{27,4},{28,5},{29,6},{30,7},{31,0},{16,9},{17... | collective-permute-start | bytes 1880072 | tf_op jit(solution)/shard_map/gather/ppermute | solution.py:373
  12.5 10.7 %collective-permute-start.2 = (f32[136,1152]{1,0:T(8,128)S(1)}, f32[136,1152]{1,0:T(8,128)S(1)}, u32[]{:S(2)}, u32[]{:S(2)}) collective-permute-start(f32[136,1152]{1,0:T(8,128)S(1)} %prepare.1.refs_0_), channel_id=1, source_target_pairs={{0,7},{1,0},{2,1},{3,2},{4,3},{5,4},{6,5},{7,6},{8,15},{9,8},{10,9... | collective-permute-start | bytes 1880072 | tf_op jit(solution)/shard_map/gather/ppermute | solution.py:373
  21.1 2.9 %collective-permute-start.8 = (f32[136,1152]{1,0:T(8,128)S(1)}, f32[136,1152]{1,0:T(8,128)S(1)}, u32[]{:S(2)}, u32[]{:S(2)}) collective-permute-start(f32[136,1152]{1,0:T(8,128)S(1)} %collective-permute-done.4.refs_5_), channel_id=1, source_target_pairs={{0,7},{1,0},{2,1},{3,2},{4,3},{5,4},{6,5},{7,6},{8,15},{9,8},{10,9... | collective-permute-start | bytes 1880072 | tf_op jit(solution)/shard_map/gather/ppermute | solution.py:373
  21.9 2.9 %collective-permute-start.5 = (f32[136,1152]{1,0:T(8,128)S(1)}, f32[136,1152]{1,0:T(8,128)S(1)}, u32[]{:S(2)}, u32[]{:S(2)}) collective-permute-start(f32[136,1152]{1,0:T(8,128)S(1)} %collective-permute-done.1.refs_2_), channel_id=1, source_target_pairs={{0,1},{1,2},{2,3},{3,4},{4,5},{5,6},{6,7},{7,0},{8,9},{9,10},{10,1... | collective-permute-start | bytes 1880072 | tf_op jit(solution)/shard_map/gather/ppermute | solution.py:373
  22.6 25.0 %collective-permute-start.7 = (f32[136,1152]{1,0:T(8,128)S(1)}, f32[136,1152]{1,0:T(8,128)S(1)}, u32[]{:S(2)}, u32[]{:S(2)}) collective-permute-start(f32[136,1152]{1,0:T(8,128)S(1)} %collective-permute-done.3.refs_4_), channel_id=1, source_target_pairs={{0,1},{1,2},{2,3},{3,4},{4,5},{5,6},{6,7},{7,0},{8,9},{9,10},{10,1... | collective-permute-start | bytes 1880072 | tf_op jit(solution)/shard_map/gather/ppermute | solution.py:373
  23.3 25.0 %collective-permute-start.6 = (f32[136,1152]{1,0:T(8,128)S(1)}, f32[136,1152]{1,0:T(8,128)S(1)}, u32[]{:S(2)}, u32[]{:S(2)}) collective-permute-start(f32[136,1152]{1,0:T(8,128)S(1)} %collective-permute-done.2.refs_3_), channel_id=1, source_target_pairs={{0,7},{1,0},{2,1},{3,2},{4,3},{5,4},{6,5},{7,6},{8,15},{9,8},{10,9... | collective-permute-start | bytes 1880072 | tf_op jit(solution)/shard_map/gather/ppermute | solution.py:373
  24.0 25.0 %collective-permute-start.12 = (f32[136,1152]{1,0:T(8,128)S(1)}, f32[136,1152]{1,0:T(8,128)S(1)}, u32[]{:S(2)}, u32[]{:S(2)}) collective-permute-start(f32[136,1152]{1,0:T(8,128)S(1)} %collective-permute-done.8.refs_9_.refs_3_), channel_id=1, source_target_pairs={{0,7},{1,0},{2,1},{3,2},{4,3},{5,4},{6,5},{7,6},{8,15},{9,8},{10,9... | collective-permute-start | bytes 1880072 | tf_op jit(solution)/shard_map/gather/ppermute | solution.py:373
  24.7 25.0 %collective-permute-start.9 = (f32[136,1152]{1,0:T(8,128)S(1)}, f32[136,1152]{1,0:T(8,128)S(1)}, u32[]{:S(2)}, u32[]{:S(2)}) collective-permute-start(f32[136,1152]{1,0:T(8,128)S(1)} %collective-permute-done.5.refs_6_.refs_0_), channel_id=1, source_target_pairs={{0,1},{1,2},{2,3},{3,4},{4,5},{5,6},{6,7},{7,0},{8,9},{9,10},{10,1... | collective-permute-start | bytes 1880072 | tf_op jit(solution)/shard_map/gather/ppermute | solution.py:373
  25.4 29.8 %collective-permute-start = (f32[136,1152]{1,0:T(8,128)S(1)}, f32[136,1152]{1,0:T(8,128)S(1)}, u32[]{:S(2)}, u32[]{:S(2)}) collective-permute-start(f32[136,1152]{1,0:T(8,128)S(1)} %prepare.1.refs_0_), channel_id=1, source_target_pairs={{24,0},{25,1},{26,2},{27,3},{28,4},{29,5},{30,6},{31,7},{16,8},{17... | collective-permute-start | bytes 1880072 | tf_op jit(solution)/shard_map/gather/ppermute | solution.py:373
  47.5 8.7 %collective-permute-start.11 = (f32[136,1152]{1,0:T(8,128)S(1)}, f32[136,1152]{1,0:T(8,128)S(1)}, u32[]{:S(2)}, u32[]{:S(2)}) collective-permute-start(f32[136,1152]{1,0:T(8,128)S(1)} %collective-permute-done.7.refs_8_.refs_2_), channel_id=1, source_target_pairs={{0,1},{1,2},{2,3},{3,4},{4,5},{5,6},{6,7},{7,0},{8,9},{9,10},{10,1... | collective-permute-start | bytes 1880072 | tf_op jit(solution)/shard_map/gather/ppermute | solution.py:373
  48.3 8.0 %collective-permute-start.10 = (f32[136,1152]{1,0:T(8,128)S(1)}, f32[136,1152]{1,0:T(8,128)S(1)}, u32[]{:S(2)}, u32[]{:S(2)}) collective-permute-start(f32[136,1152]{1,0:T(8,128)S(1)} %collective-permute-done.6.refs_7_.refs_1_), channel_id=1, source_target_pairs={{0,7},{1,0},{2,1},{3,2},{4,3},{5,4},{6,5},{7,6},{8,15},{9,8},{10,9... | collective-permute-start | bytes 1880072 | tf_op jit(solution)/shard_map/gather/ppermute | solution.py:373
  49.0 7.3 %collective-permute-start.14 = (f32[136,1152]{1,0:T(8,128)S(1)}, f32[136,1152]{1,0:T(8,128)S(1)}, u32[]{:S(2)}, u32[]{:S(2)}) collective-permute-start(f32[136,1152]{1,0:T(8,128)S(1)} %collective-permute-done.12.refs_13_.refs_3_), channel_id=1, source_target_pairs={{0,7},{1,0},{2,1},{3,2},{4,3},{5,4},{6,5},{7,6},{8,15},{9,8},{10,9... | collective-permute-start | bytes 1880072 | tf_op jit(solution)/shard_map/gather/ppermute | solution.py:373
  49.7 6.6 %collective-permute-start.13 = (f32[136,1152]{1,0:T(8,128)S(1)}, f32[136,1152]{1,0:T(8,128)S(1)}, u32[]{:S(2)}, u32[]{:S(2)}) collective-permute-start(f32[136,1152]{1,0:T(8,128)S(1)} %collective-permute-done.9.refs_10_.refs_0_), channel_id=1, source_target_pairs={{0,1},{1,2},{2,3},{3,4},{4,5},{5,6},{6,7},{7,0},{8,9},{9,10},{10,1... | collective-permute-start | bytes 1880072 | tf_op jit(solution)/shard_map/gather/ppermute | solution.py:373
  57.7 1.3 collective-permute-start.15
  59.7 1.3 collective-permute-start.17
  61.8 1.3 collective-permute-start.19
  63.9 1.3 collective-permute-start.21
  65.9 1.3 collective-permute-start.23
  68.0 1.5 collective-permute-start.25
  70.3 1.3 collective-permute-start.27
  73.0 5.2 %collective-permute-start.30 = (f32[16,8,128]{2,1,0:T(8,128)S(1)}, f32[16,8,128]{2,1,0:T(8,128)S(1)}, u32[]{:S(2)}, u32[]{:S(2)}) collective-permute-start(f32[16,8,128]{2,1,0:T(8,128)S(1)} %get-tuple-element.59.before), channel_id=1, source_target_pairs={{96,80},{97,81},{98,82},{99,83},{100,84},{101,85},{102,86},{103,87... | collective-permute-start | bytes 196616 | tf_op jit(solution)/shard_map/ppermute | solution.py:363
  73.6 4.5 %collective-permute-start.29 = (f32[16,8,128]{2,1,0:T(8,128)S(1)}, f32[16,8,128]{2,1,0:T(8,128)S(1)}, u32[]{:S(2)}, u32[]{:S(2)}) collective-permute-start(f32[16,8,128]{2,1,0:T(8,128)S(1)} %get-tuple-element.59.before), channel_id=1, source_target_pairs={{96,88},{97,89},{98,90},{99,91},{100,92},{101,93},{102,94},{103,95... | collective-permute-start | bytes 196616 | tf_op jit(solution)/shard_map/ppermute | solution.py:363
  78.9 1.3 collective-permute-start.32
  81.0 1.3 collective-permute-start.34
  83.0 1.3 collective-permute-start.36
  85.1 1.3 collective-permute-start.38
  87.2 1.3 collective-permute-start.40
  89.2 1.3 collective-permute-start.42
  92.0 13.6 %all-to-all-start = ((f32[8,32,128]{2,1,0:T(8,128)}), f32[8,32,128]{2,1,0:T(8,128)S(1)}, u32[]{:S(2)}, u32[]{:S(2)}) async-start(f32[8,32,128]{2,1,0:T(8,128)} %backward_0.1), calls=%async_computation | async-start | bytes 262144 | tf_op jit(solution)/shard_map/collect/all_to_all | solution.py:411
  105.6 94.8 %collective-permute-start.43 = (f32[2,64,128]{2,1,0:T(8,128)S(1)}, f32[2,64,128]{2,1,0:T(8,128)S(1)}, u32[]{:S(2)}, u32[]{:S(2)}) collective-permute-start(f32[2,64,128]{2,1,0:T(8,128)S(1)} %get-tuple-element.67), channel_id=1, source_target_pairs={{0,24},{1,25},{2,26},{3,27},{4,28},{5,29},{6,30},{7,31},{8,16},{9,... | collective-permute-start | bytes 196616 | tf_op jit(solution)/shard_map/collect/ppermute | solution.py:373
  (13 other events, 9.1 us)
